TPU v7x, 32 devices: a whole 2x2x4 slice. The times are simulated.
32 devices in a mesh: dp: 4 (over z), expert: 8 (over y, x, core).
Axes of the slice: x: 2, y: 2, z: 4, core: 2. Of those that a mesh axis runs over, the one named last changes fastest.
Arguments:
- layer_input: bfloat16 [4096, 1024], P(('dp', 'expert')), may hold values from -6 to 6
- segment_ids: int32 [4096], P(('dp', 'expert')), may hold values from 0 to 127, never falling along the last dimension, each value on 1 to 64 neighbouring positions
- expert_routes: int32 [4096, 8], P(('dp', 'expert')), may hold values from 0 to 31, all different within a row; in each aligned block of 128 rows (0 to 127, 128 to 255, ...) at most 40 rows name the same one
- first_gain: float32 [1024], replicated, may hold values from 0.5 to 1.5
- w_query: bfloat16 [1024, 1024], P('dp'), may hold values from -0.1875 to 0.1875
- w_keyvalue: bfloat16 [1024, 1024], P('dp'), may hold values from -0.1875 to 0.1875
- w_output: bfloat16 [1024, 1024], P('dp'), may hold values from -1.5 to 1.5
- second_gain: float32 [1024], replicated, may hold values from 0.5 to 1.5
- w_router: bfloat16 [1024, 32], P('dp'), may hold values from -0.1875 to 0.1875
- w_gate_up: bfloat16 [32, 1024, 1024], P('expert', 'dp'), may hold values from -0.1875 to 0.1875
- w_down: bfloat16 [32, 512, 1024], P('expert', 'dp'), may hold values from -1 to 1
- out_cotangent: bfloat16 [4096, 1024], P(('dp', 'expert')), may hold values from -6 to 6
Outputs:
- layer_output: bfloat16 [4096, 1024], P(('dp', 'expert'))
- input_grad: bfloat16 [4096, 1024], P(('dp', 'expert'))
- first_gain_grad: float32 [1024], replicated
- query_grad: float32 [1024, 1024], P('dp')
- keyvalue_grad: float32 [1024, 1024], P('dp')
- output_grad: float32 [1024, 1024], P('dp')
- second_gain_grad: float32 [1024], replicated
- router_grad: float32 [1024, 32], P('dp')
- gate_up_grad: float32 [32, 1024, 1024], P('expert', 'dp')
- down_grad: float32 [32, 512, 1024], P('expert', 'dp')
Inputs may be any that keep to these rules, and one draw needn't show every extreme that they name: `expert_routes`: each row names 8 different experts. Among the rows of one device no expert is named by more than 40 rows, a bound that some block reaches. `segment_ids`: segment numbers never fall along the tokens; each document holds 1 to 64 tokens, and one holds exactly 64.
All inputs are finite; a program needn't handle non-finite values.
Results may differ from a plain program's by a relative error of at most 0.018.
Values may be sent and summed in bfloat16 or wider, within the bound.
No kernel may reach another device: no remote copies, remote signals or barrier semaphores. Data moves between devices by JAX's collectives and lax.ppermute only.
A program may use at most 128 MiB of HBM per device.

v0:
```python
import jax
import jax.numpy as jnp
import numpy as np
from jax import lax
from jax.experimental import pallas as pl
from jax.experimental.pallas import tpu as pltpu
from jax.sharding import PartitionSpec as P

D = 1024
HEADS = 16
KV_HEADS = 8
HEAD_DIM = 64
F = 512
EXPERTS = 32
TOPK = 8
CAP = 40


epsilon = 1e-06
residual_scale = 0.22
score_scale = 0.015625
rope_base = 10000.0


def rope_tables(length, head_width):
    halfway = head_width // 2
    frequency = jnp.exp(
        -jnp.log(rope_base) * (2.0 * jnp.arange(halfway, dtype=jnp.float32) / head_width)
    )
    angles = jnp.arange(length, dtype=jnp.float32)[:, None] * frequency[None, :]
    cosine = jnp.concatenate([jnp.cos(angles), jnp.cos(angles)], axis=1)
    sine_table = jnp.concatenate([jnp.sin(angles), jnp.sin(angles)], axis=1)
    return (cosine, sine_table)


def rotate(values, cosine, sine_table, direction):
    halfway = values.shape[-1] // 2
    turned = jnp.concatenate([-values[..., halfway:], values[..., :halfway]], axis=-1)
    return values * cosine[:, None, :] + direction * turned * sine_table[:, None, :]


def norm_forward(inputs_f32, gain_vector):
    inverse = lax.rsqrt(jnp.mean(inputs_f32 * inputs_f32, axis=-1, keepdims=True) + epsilon)
    return (inputs_f32 * inverse * gain_vector, inverse)


def norm_backward(inputs_f32, inverse, gain_vector, upstream):
    weighted = upstream * gain_vector
    gain_part = jnp.sum(upstream * inputs_f32 * inverse, axis=0)
    through = inverse * weighted - inputs_f32 * (inverse * inverse * inverse) * jnp.mean(
        weighted * inputs_f32, axis=-1, keepdims=True
    )
    return (gain_part, through)


def activate(pre_act):
    gate_half = pre_act[..., :F]
    up_half = pre_act[..., F:]
    return gate_half * jax.nn.sigmoid(gate_half) * up_half


def activate_backward(pre_act, d_act):
    gate_half = pre_act[..., :F]
    up_half = pre_act[..., F:]
    sigmoid_gate = jax.nn.sigmoid(gate_half)
    d_gate = d_act * up_half * sigmoid_gate * (1.0 + gate_half * (1.0 - sigmoid_gate))
    d_up = d_act * gate_half * sigmoid_gate
    return jnp.concatenate([d_gate, d_up], axis=-1)


def masked_scores(query, keys, visible):
    raw_scores = (
        jnp.einsum("qkgd,pkd->kgqp", query, keys, preferred_element_type=jnp.float32) * score_scale
    )
    return jnp.where(visible[None, None], raw_scores, -1e30)


def attend_forward(normed, full_query, full_keyvalue, visible, cosine, sine_table):
    length = normed.shape[0]
    per_group = HEADS // KV_HEADS
    query_raw = jnp.dot(normed, full_query, preferred_element_type=jnp.float32).reshape(
        length, HEADS, HEAD_DIM
    )
    keyval = jnp.dot(normed, full_keyvalue, preferred_element_type=jnp.float32).reshape(
        length, 2, KV_HEADS, HEAD_DIM
    )
    query = (
        rotate(query_raw, cosine, sine_table, 1.0)
        .astype(jnp.bfloat16)
        .reshape(length, KV_HEADS, per_group, HEAD_DIM)
    )
    keys = rotate(keyval[:, 0], cosine, sine_table, 1.0).astype(jnp.bfloat16)
    values = keyval[:, 1].astype(jnp.bfloat16)
    scores = masked_scores(query, keys, visible)
    highest = jnp.max(scores, axis=-1, keepdims=True)
    log_total = highest + jnp.log(jnp.sum(jnp.exp(scores - highest), axis=-1, keepdims=True))
    probabilities = jnp.exp(scores - log_total).astype(jnp.bfloat16)
    attended = jnp.einsum(
        "kgqp,pkd->qkgd", probabilities, values, preferred_element_type=jnp.float32
    )
    attended = attended.reshape(length, HEADS * HEAD_DIM).astype(jnp.bfloat16)
    return (query, keys, values, attended, log_total)


def attend_backward(query, keys, values, attended, log_total, d_attended, visible):
    length = query.shape[0]
    per_group = HEADS // KV_HEADS
    scores = masked_scores(query, keys, visible)
    probs_f32 = jnp.exp(scores - log_total)
    probs_half = probs_f32.astype(jnp.bfloat16)
    d_att4 = d_attended.reshape(length, KV_HEADS, per_group, HEAD_DIM)
    att_four = attended.reshape(length, KV_HEADS, per_group, HEAD_DIM)
    d_values = jnp.einsum("kgqp,qkgd->pkd", probs_half, d_att4, preferred_element_type=jnp.float32)
    d_probs = jnp.einsum("qkgd,pkd->kgqp", d_att4, values, preferred_element_type=jnp.float32)
    row_delta = jnp.einsum("qkgd,qkgd->kgq", d_att4, att_four, preferred_element_type=jnp.float32)
    d_scores = (probs_f32 * (d_probs - row_delta[..., None]) * score_scale).astype(jnp.bfloat16)
    d_query = jnp.einsum(
        "kgqp,pkd->qkgd", d_scores, keys, preferred_element_type=jnp.float32
    ).reshape(length, HEADS, HEAD_DIM)
    d_keys = jnp.einsum("kgqp,qkgd->pkd", d_scores, query, preferred_element_type=jnp.float32)
    return (d_query, d_keys, d_values)


DP, EX = "dp", "expert"


def butterfly_sum(value, axes):
    for axis in axes:
        size = lax.axis_size(axis)
        step = 1
        while step < size:
            value = value + lax.ppermute(value, axis, [(i, i ^ step) for i in range(size)])
            step *= 2
    return value


def spread_over(axes, array):
    for axis in reversed(axes):
        array = lax.all_gather(array, axis, axis=0, tiled=True)
    return array


def sum_to_owner(axes, array):
    for axis in axes:
        array = lax.psum_scatter(array, axis, scatter_dimension=0, tiled=True)
    return array


def expert_pass(tokens, cotangents, gate, hit, w_up, w_dn):
    blocks = tokens.shape[0] // 128
    ranking = jnp.cumsum(hit.reshape(blocks, 128).astype(jnp.int32), axis=1) - 1
    slot = jnp.where(hit.reshape(blocks, 128), ranking, -1)
    select = slot[:, None, :] == jnp.arange(CAP, dtype=jnp.int32)[None, :, None]
    onehot = select.astype(jnp.bfloat16)
    rows = blocks * CAP
    picked = jnp.einsum(
        "bst,btd->bsd", onehot, tokens.reshape(blocks, 128, D), preferred_element_type=jnp.float32
    ).astype(jnp.bfloat16).reshape(rows, D)
    cot = jnp.einsum(
        "bst,btd->bsd",
        onehot,
        cotangents.reshape(blocks, 128, D),
        preferred_element_type=jnp.float32,
    ).reshape(rows, D)
    gate_slot = jnp.sum(
        jnp.where(select, gate.reshape(blocks, 1, 128), 0.0), axis=2
    ).reshape(rows, 1)
    pre_act = jnp.dot(picked, w_up, preferred_element_type=jnp.float32)
    activated = activate(pre_act).astype(jnp.bfloat16)
    result = (
        jnp.dot(activated, w_dn, preferred_element_type=jnp.float32)
        .astype(jnp.bfloat16)
        .astype(jnp.float32)
    )
    d_gate_slot = residual_scale * jnp.sum(cot * result, axis=1)
    d_gate = jnp.sum(jnp.where(select, d_gate_slot.reshape(blocks, CAP, 1), 0.0), axis=1)
    gated = (gate_slot * result).astype(jnp.bfloat16)
    mixed = jnp.einsum(
        "bst,bsd->btd", onehot, gated.reshape(blocks, CAP, D), preferred_element_type=jnp.float32
    ).reshape(blocks * 128, D)
    d_result = (residual_scale * gate_slot * cot).astype(jnp.bfloat16)
    d_act = jnp.dot(d_result, w_dn.T, preferred_element_type=jnp.float32)
    d_down = jnp.dot(activated.T, d_result, preferred_element_type=jnp.float32)
    d_pre = activate_backward(pre_act, d_act).astype(jnp.bfloat16)
    d_up = jnp.dot(picked.T, d_pre, preferred_element_type=jnp.float32)
    d_rows = jnp.dot(d_pre, w_up.T, preferred_element_type=jnp.float32).astype(jnp.bfloat16)
    back = jnp.einsum(
        "bst,bsd->btd", onehot, d_rows.reshape(blocks, CAP, D), preferred_element_type=jnp.float32
    ).reshape(blocks * 128, D)
    return (mixed, back, d_gate.reshape(blocks * 128), d_up, d_down)


def general_device(
    layer_input,
    segment_ids,
    expert_routes,
    first_gain,
    w_query,
    w_keyvalue,
    w_output,
    second_gain,
    w_router,
    w_gate_up,
    w_down,
    out_cotangent,
):
    length = layer_input.shape[0]
    owners = lax.axis_size(EX)
    groups = lax.axis_size(DP)
    group_at = lax.axis_index(DP)
    owner_at = lax.axis_index(EX)
    per_owner = w_gate_up.shape[0]
    shard = w_query.shape[0]
    part = shard // owners
    every = (DP, EX)

    def own_part(weight):
        return lax.dynamic_slice_in_dim(weight, owner_at * part, part, 0)

    pack = jnp.concatenate([own_part(w_query), own_part(w_keyvalue), own_part(w_output)], axis=0)
    gathered = lax.all_gather(pack, every, axis=0).reshape(groups * owners, 3, part, D)
    full_query = gathered[:, 0].reshape(D, HEADS * HEAD_DIM)
    full_keyvalue = gathered[:, 1].reshape(D, 2 * KV_HEADS * HEAD_DIM)
    full_output = gathered[:, 2].reshape(HEADS * HEAD_DIM, D)
    full_router = lax.all_gather(own_part(w_router), every, axis=0, tiled=True)

    exchange = per_owner % groups == 0
    if exchange:
        local = per_owner // groups
        token_axes = (EX, DP)
        first_expert = owner_at * per_owner + group_at * local
        own_up = lax.all_to_all(w_gate_up, DP, split_axis=0, concat_axis=1, tiled=True)
        own_down = lax.all_to_all(w_down, DP, split_axis=0, concat_axis=1, tiled=True)
    else:
        local = per_owner
        token_axes = (EX,)
        first_expert = owner_at * per_owner
        own_up = lax.all_gather(w_gate_up, DP, axis=1, tiled=True)
        own_down = lax.all_gather(w_down, DP, axis=1, tiled=True)
    all_routes = spread_over(token_axes, expert_routes)
    all_cotangents = spread_over(token_axes, out_cotangent)

    cosine, sine_table = rope_tables(length, HEAD_DIM)
    places = jnp.arange(length)
    visible = (places[:, None] >= places[None, :]) & (segment_ids[:, None] == segment_ids[None, :])
    inputs_f32 = layer_input.astype(jnp.float32)
    normed, inverse = norm_forward(inputs_f32, first_gain)
    normed = normed.astype(jnp.bfloat16)
    query, keys, values, attended, log_total = attend_forward(
        normed, full_query, full_keyvalue, visible, cosine, sine_table
    )
    hidden = inputs_f32 + residual_scale * jnp.dot(
        attended, full_output, preferred_element_type=jnp.float32
    )
    normed2, inverse2 = norm_forward(hidden, second_gain)
    normed2 = normed2.astype(jnp.bfloat16)
    all_normed2 = spread_over(token_axes, normed2)

    def gates_of(rows, routes):
        named = jnp.any(
            routes[:, :, None] == jnp.arange(EXPERTS, dtype=jnp.int32)[None, None, :], axis=1
        )
        logits = jnp.dot(rows, full_router, preferred_element_type=jnp.float32)
        highest = jnp.max(jnp.where(named, logits, -jnp.inf), axis=1, keepdims=True)
        exponent = jnp.where(named, jnp.exp(jnp.where(named, logits - highest, 0.0)), 0.0)
        return exponent / jnp.sum(exponent, axis=1, keepdims=True)

    all_gates = gates_of(all_normed2, all_routes)
    d_out = out_cotangent.astype(jnp.float32)
    mixed, back = 0.0, 0.0
    d_gate_list, up_list, down_list = [], [], []
    for j in range(local):
        hit = jnp.any(all_routes == first_expert + j, axis=1)
        gate = lax.dynamic_index_in_dim(all_gates, first_expert + j, 1, keepdims=False)
        one_mixed, one_back, d_gate, d_up, d_dn = expert_pass(
            all_normed2, all_cotangents, gate, hit, own_up[j], own_down[j]
        )
        mixed, back = mixed + one_mixed, back + one_back
        d_gate_list.append(d_gate)
        up_list.append(d_up.astype(jnp.bfloat16))
        down_list.append(d_dn.astype(jnp.bfloat16))
    back_own = sum_to_owner(token_axes, back.astype(jnp.bfloat16)).astype(jnp.float32)
    sources = EXPERTS // local
    d_gate_out = jnp.stack(d_gate_list).reshape(local, sources, length).transpose(1, 0, 2)
    d_gates = (
        lax.all_to_all(d_gate_out, token_axes, split_axis=0, concat_axis=0, tiled=True)
        .reshape(EXPERTS, length)
        .T
    )
    d_up_all, d_down_all = jnp.stack(up_list), jnp.stack(down_list)
    if exchange:
        gate_up_grad = lax.all_to_all(d_up_all, DP, split_axis=1, concat_axis=0, tiled=True)
        down_grad = lax.all_to_all(d_down_all, DP, split_axis=1, concat_axis=0, tiled=True)
    else:
        gate_up_grad = lax.psum_scatter(d_up_all, DP, scatter_dimension=1, tiled=True)
        down_grad = lax.psum_scatter(d_down_all, DP, scatter_dimension=1, tiled=True)
    mixed_own = sum_to_owner(token_axes, mixed.astype(jnp.bfloat16)).astype(jnp.float32)
    layer_output = (hidden + residual_scale * mixed_own).astype(jnp.bfloat16)

    gates = gates_of(normed2, expert_routes)
    d_logits = (gates * (d_gates - jnp.sum(gates * d_gates, axis=1, keepdims=True))).astype(
        jnp.bfloat16
    )
    d_router = jnp.dot(normed2.T, d_logits, preferred_element_type=jnp.float32)
    d_normed2 = back_own + jnp.dot(d_logits, full_router.T, preferred_element_type=jnp.float32)
    d_second_gain, d_through = norm_backward(hidden, inverse2, second_gain, d_normed2)
    second_gain_grad = butterfly_sum(d_second_gain, (EX, DP))
    d_hidden = d_out + d_through
    d_branch = (residual_scale * d_hidden).astype(jnp.bfloat16)
    d_wout = jnp.dot(attended.T, d_branch, preferred_element_type=jnp.float32)
    d_attended = jnp.dot(d_branch, full_output.T, preferred_element_type=jnp.float32).astype(
        jnp.bfloat16
    )
    d_query, d_keys, d_values = attend_backward(
        query, keys, values, attended, log_total, d_attended, visible
    )
    d_query = (
        rotate(d_query, cosine, sine_table, -1.0)
        .reshape(length, HEADS * HEAD_DIM)
        .astype(jnp.bfloat16)
    )
    d_keys = rotate(d_keys, cosine, sine_table, -1.0)
    d_keyvalue = (
        jnp.stack([d_keys, d_values], axis=1)
        .reshape(length, 2 * KV_HEADS * HEAD_DIM)
        .astype(jnp.bfloat16)
    )
    d_wquery = jnp.dot(normed.T, d_query, preferred_element_type=jnp.float32)
    d_wkeyvalue = jnp.dot(normed.T, d_keyvalue, preferred_element_type=jnp.float32)
    d_normed = jnp.dot(d_query, full_query.T, preferred_element_type=jnp.float32) + jnp.dot(
        d_keyvalue, full_keyvalue.T, preferred_element_type=jnp.float32
    )
    d_first_gain, d_inputs = norm_backward(inputs_f32, inverse, first_gain, d_normed)
    first_gain_grad = butterfly_sum(d_first_gain, (EX, DP))
    input_grad = (d_hidden + d_inputs).astype(jnp.bfloat16)

    def reduced(*grads):
        packed = jnp.stack([g.astype(jnp.bfloat16) for g in grads])
        count, width = len(grads), grads[0].shape[1]
        packed = packed.reshape(count, groups, owners, part, width).transpose(2, 1, 0, 3, 4)
        packed = packed.reshape(owners * groups * count * part, width)
        mine = sum_to_owner((EX, DP), packed).reshape(1, count, part, width)
        whole = lax.all_gather(mine, EX, axis=0, tiled=True)
        whole = whole.transpose(1, 0, 2, 3).reshape(count, owners * part, width)
        return [whole[i].astype(jnp.float32) for i in range(count)]

    output_grad, query_grad, keyvalue_grad = reduced(d_wout, d_wquery, d_wkeyvalue)
    (router_grad,) = reduced(d_router)
    return (
        layer_output,
        input_grad,
        first_gain_grad,
        query_grad,
        keyvalue_grad,
        output_grad,
        second_gain_grad,
        router_grad,
        gate_up_grad.astype(jnp.float32),
        down_grad.astype(jnp.float32),
    )


def expert_kernel(*refs):
    tok_a, tok_b, cot_a, cot_b = refs[0:4], refs[4:8], refs[8:12], refs[12:16]
    up_pieces, down_pieces = refs[16:20], refs[20:24]
    routes_ref, router_ref = refs[24:26]
    mix_a, mix_b, back_a, back_b = refs[26:30], refs[30:34], refs[34:38], refs[38:42]
    d_up_pieces, d_down_pieces = refs[42:46], refs[46:50]
    dgate_ref = refs[50]
    (
        tok_buf,
        cot_buf,
        mix_buf,
        back_buf,
        rows_scr,
        act_scr,
        dres_scr,
        dpre_scr,
        cot_scr,
        gate_scr,
        slot_scr,
        tri_scr,
        up_scr,
        down_scr,
        d_up_scr,
        d_down_scr,
        in_sem,
        out_sem,
        weight_sem,
        grad_sem,
    ) = refs[51:]
    half = D // 2
    owner, group = lax.axis_index(EX), lax.axis_index(DP)
    expert = owner * 4 + group
    chunk_rows = 8 * CAP

    def chunk_copies(kk, slot, sources, sem, outward):
        c, y = kk // 2, kk % 2
        ends = []
        for a, b, buf in sources:
            ends.append((a[kk], buf.at[slot, :, pl.ds(0, half)]))
            for x in range(2):
                ends.append(
                    (
                        b[2 * c + x].at[pl.ds(512 * y, 512), :],
                        buf.at[slot, pl.ds(512 * x, 512), pl.ds(half, half)],
                    )
                )
        if outward:
            ends = [(there, here) for here, there in ends]
        return [
            pltpu.make_async_copy(*pair, sem.at[slot, i]) for i, pair in enumerate(ends)
        ]

    def in_copies(kk, slot):
        sources = ((tok_a, tok_b, tok_buf), (cot_a, cot_b, cot_buf))
        return chunk_copies(kk, slot, sources, in_sem, False)

    def out_copies(kk, slot):
        sources = ((back_a, back_b, back_buf), (mix_a, mix_b, mix_buf))
        return chunk_copies(kk, slot, sources, out_sem, True)

    def weight_pairs():
        found = []
        for s in range(4):
            at = jnp.bitwise_xor(group, s)
            up_from = up_pieces[s].at[group] if s == 0 else up_pieces[s]
            down_from = down_pieces[s].at[group] if s == 0 else down_pieces[s]
            found.append(pltpu.make_async_copy(up_from, up_scr.at[at], weight_sem.at[0, s]))
            found.append(pltpu.make_async_copy(down_from, down_scr.at[at], weight_sem.at[1, s]))
        return found

    for copy in in_copies(0, 0) + weight_pairs():
        copy.start()
    before = lax.broadcasted_iota(jnp.int32, (256, 256), 0)
    after = lax.broadcasted_iota(jnp.int32, (256, 256), 1)
    tri_scr[...] = ((before <= after) & ((before < 128) == (after < 128))).astype(jnp.bfloat16)

    def pair_mask(pair):
        return slot_scr[pair] == lax.broadcasted_iota(jnp.int32, (2 * CAP, 256), 0)

    def chunk_step(k, carry):
        for kk in range(4):

            @pl.when(k == kk)
            def _():
                if kk < 3:
                    for copy in in_copies(kk + 1, (kk + 1) % 2):
                        copy.start()
                for copy in in_copies(kk, kk % 2):
                    copy.wait()
                if kk >= 2:
                    for copy in out_copies(kk - 2, kk % 2):
                        copy.wait()

        at = lax.rem(k, 2)
        base = pl.multiple_of(k * chunk_rows, chunk_rows)
        away = k // 2 + 4 * lax.rem(k, 2)
        for pair in range(4):
            device = jnp.bitwise_xor(owner, away + 2 * (pair // 2)) * 4 + 2 * (pair % 2)
            routes = jnp.concatenate([routes_ref[device], routes_ref[device + 1]], axis=1)
            hit = jnp.max((routes == expert).astype(jnp.float32), axis=0, keepdims=True)
            rank = jnp.dot(
                jnp.broadcast_to(hit, (16, 256)).astype(jnp.bfloat16),
                tri_scr[...],
                preferred_element_type=jnp.float32,
            )[0:1]
            second = lax.broadcasted_iota(jnp.int32, (1, 256), 1) >= 128
            slot = rank.astype(jnp.int32) - 1 + jnp.where(second, CAP, 0)
            slot_scr[pair] = jnp.where(hit > 0.5, slot, -1)
            mask = pair_mask(pair)
            onehot = mask.astype(jnp.bfloat16)
            token_rows = tok_buf[at, pl.ds(256 * pair, 256), :]
            logits = lax.dot_general(
                router_ref[...],
                token_rows,
                (((1,), (1,)), ((), ())),
                preferred_element_type=jnp.float32,
            )
            names = lax.broadcasted_iota(jnp.int32, (EXPERTS, 256), 0)
            named = routes[0:1] == names
            for i in range(1, TOPK):
                named = named | (routes[i : i + 1] == names)
            highest = jnp.max(jnp.where(named, logits, -3e38), axis=0, keepdims=True)
            exponent = jnp.where(named, jnp.exp(jnp.where(named, logits - highest, 0.0)), 0.0)
            own = jnp.sum(jnp.where(names == expert, exponent, 0.0), axis=0, keepdims=True)
            gate = own / jnp.sum(exponent, axis=0, keepdims=True)
            gate_slot = jnp.sum(jnp.where(mask, gate, 0.0), axis=1, keepdims=True)
            gate_scr[pl.ds(2 * CAP * pair, 2 * CAP), :] = gate_slot
            place = pl.ds(base + 2 * CAP * pair, 2 * CAP)
            rows_scr[place, :] = jnp.dot(
                onehot, token_rows, preferred_element_type=jnp.float32
            ).astype(jnp.bfloat16)
            cot = jnp.dot(
                onehot, cot_buf[at, pl.ds(256 * pair, 256), :], preferred_element_type=jnp.float32
            )
            cot_scr[pl.ds(2 * CAP * pair, 2 * CAP), :] = cot.astype(jnp.bfloat16)
            dres_scr[place, :] = (residual_scale * gate_slot * cot).astype(jnp.bfloat16)

        @pl.when(k == 0)
        def _():
            for copy in weight_pairs():
                copy.wait()

        here = pl.ds(base, chunk_rows)
        pre = jnp.dot(rows_scr[here, :], up_scr[...].reshape(D, 2 * F), preferred_element_type=jnp.float32)
        gate_half, up_half = pre[:, :F], pre[:, F:]
        sigmoid_gate = 1.0 / (1.0 + jnp.exp(-gate_half))
        swish = gate_half * sigmoid_gate
        activated = (swish * up_half).astype(jnp.bfloat16)
        act_scr[here, :] = activated
        d_act = lax.dot_general(
            dres_scr[here, :],
            down_scr[...].reshape(F, D),
            (((1,), (1,)), ((), ())),
            preferred_element_type=jnp.float32,
        )
        dpre_scr[here, 0:F] = (
            d_act * up_half * sigmoid_gate * (1.0 + gate_half * (1.0 - sigmoid_gate))
        ).astype(jnp.bfloat16)
        dpre_scr[here, F : 2 * F] = (d_act * swish).astype(jnp.bfloat16)
        result = (
            jnp.dot(activated, down_scr[...].reshape(F, D), preferred_element_type=jnp.float32)
            .astype(jnp.bfloat16)
            .astype(jnp.float32)
        )
        d_gate_slot = residual_scale * jnp.sum(
            cot_scr[...].astype(jnp.float32) * result, axis=1, keepdims=True
        )
        gated = (gate_scr[...] * result).astype(jnp.bfloat16)
        d_rows = lax.dot_general(
            dpre_scr[here, :],
            up_scr[...].reshape(D, 2 * F),
            (((1,), (1,)), ((), ())),
            preferred_element_type=jnp.float32,
        ).astype(jnp.bfloat16)
        for pair in range(4):
            device = jnp.bitwise_xor(owner, away + 2 * (pair // 2)) * 4 + 2 * (pair % 2)
            mask = pair_mask(pair)
            onehot = mask.astype(jnp.bfloat16)
            mine = slice(2 * CAP * pair, 2 * CAP * (pair + 1))
            d_gate = jnp.sum(jnp.where(mask, d_gate_slot[mine], 0.0), axis=0, keepdims=True)
            dgate_ref[device] = d_gate[:, :128]
            dgate_ref[device + 1] = d_gate[:, 128:]
            rows = pl.ds(256 * pair, 256)
            mix_buf[at, rows, :] = lax.dot_general(
                onehot,
                gated[mine],
                (((0,), (0,)), ((), ())),
                preferred_element_type=jnp.float32,
            ).astype(jnp.bfloat16)
            back_buf[at, rows, :] = lax.dot_general(
                onehot,
                d_rows[mine],
                (((0,), (0,)), ((), ())),
                preferred_element_type=jnp.float32,
            ).astype(jnp.bfloat16)
        for kk in range(4):

            @pl.when(k == kk)
            def _():
                for copy in out_copies(kk, kk % 2):
                    copy.start()

        return carry

    lax.fori_loop(0, 4, chunk_step, 0)

    def up_step(t, carry):
        at = jnp.bitwise_xor(group, t)
        d_up_scr[t] = lax.dot_general(
            rows_scr[:, pl.ds(pl.multiple_of(at * 256, 256), 256)],
            dpre_scr[...],
            (((0,), (0,)), ((), ())),
            preferred_element_type=jnp.float32,
        ).astype(jnp.bfloat16)
        d_down_scr[t] = lax.dot_general(
            act_scr[:, pl.ds(pl.multiple_of(at * 128, 128), 128)],
            dres_scr[...],
            (((0,), (0,)), ((), ())),
            preferred_element_type=jnp.float32,
        ).astype(jnp.bfloat16)
        for s in range(4):

            @pl.when(t == s)
            def _():
                for copy in grad_copies(s):
                    copy.start()

        return carry

    def grad_copies(s):
        return (
            pltpu.make_async_copy(d_up_scr.at[s], d_up_pieces[s], grad_sem.at[0, s]),
            pltpu.make_async_copy(d_down_scr.at[s], d_down_pieces[s], grad_sem.at[1, s]),
        )

    lax.fori_loop(0, 4, up_step, 0)
    for kk in (2, 3):
        for copy in out_copies(kk, kk % 2):
            copy.wait()
    for s in range(4):
        for copy in grad_copies(s):
            copy.wait()


def expert_call(tok_a, tok_b, cot_a, cot_b, up_pieces, down_pieces, routes, router):
    half = D // 2
    token_count = 1024
    hbm = pl.BlockSpec(memory_space=pltpu.HBM)
    vmem = pl.BlockSpec(memory_space=pltpu.VMEM)
    slots = 32 * CAP
    b16 = jnp.bfloat16
    piece = jax.ShapeDtypeStruct((token_count, half), b16)
    outs = pl.pallas_call(
        expert_kernel,
        in_specs=[hbm] * 24 + [vmem] * 2,
        out_specs=[hbm] * 24 + [vmem],
        out_shape=[piece] * 16
        + [jax.ShapeDtypeStruct((256, 2 * F), b16)] * 4
        + [jax.ShapeDtypeStruct((128, D), b16)] * 4
        + [jax.ShapeDtypeStruct((32, 1, 128), jnp.float32)],
        scratch_shapes=[pltpu.VMEM((2, token_count, D), b16)] * 4
        + [
            pltpu.VMEM((slots, D), b16),
            pltpu.VMEM((slots, F), b16),
            pltpu.VMEM((slots, D), b16),
            pltpu.VMEM((slots, 2 * F), b16),
            pltpu.VMEM((8 * CAP, D), b16),
            pltpu.VMEM((8 * CAP, 1), jnp.float32),
            pltpu.VMEM((4, 1, 256), jnp.int32),
            pltpu.VMEM((256, 256), b16),
            pltpu.VMEM((4, 256, 2 * F), b16),
            pltpu.VMEM((4, 128, D), b16),
            pltpu.VMEM((4, 256, 2 * F), b16),
            pltpu.VMEM((4, 128, D), b16),
            pltpu.SemaphoreType.DMA((2, 6)),
            pltpu.SemaphoreType.DMA((2, 6)),
            pltpu.SemaphoreType.DMA((2, 4)),
            pltpu.SemaphoreType.DMA((2, 4)),
        ],
        compiler_params=pltpu.CompilerParams(vmem_limit_bytes=48 * 1024 * 1024),
    )(*tok_a, *tok_b, *cot_a, *cot_b, *up_pieces, *down_pieces, routes, router)
    groups = [outs[4 * i : 4 * i + 4] for i in range(6)]
    return (*groups, outs[24])


def rope_constants(length):
    frequency = rope_base ** (-2.0 * np.arange(HEAD_DIM // 2) / HEAD_DIM)
    angles = np.arange(length)[:, None] * frequency[None, :]
    cosine = np.tile(np.cos(angles), (1, 4)).astype(np.float32)
    sine = np.sin(angles)
    signed = np.concatenate([-sine, sine, -sine, sine], axis=1).astype(np.float32)
    return cosine, signed


def turn(slab, cosine, signed):
    low = (lax.broadcasted_iota(jnp.int32, slab.shape, 1) & 32) == 0
    swapped = jnp.where(low, pltpu.roll(slab, 96, 1), pltpu.roll(slab, 32, 1))
    return slab * cosine + swapped * signed


def halves_stacked(slab, low):
    zero = jnp.zeros_like(slab)
    return jnp.concatenate([jnp.where(low, slab, zero), jnp.where(low, zero, slab)], axis=0)


def doubled(slab, low, second):
    other = pltpu.roll(slab, 64, 1)
    return jnp.where(low, other, slab) if second else jnp.where(low, slab, other)


def weight_copies(pieces_a, pieces_b, whole, sems, owner, kind, outward):
    half = D // 2
    copies = []
    for rel in range(8):
        c, x, y = rel & 1, (rel >> 1) & 1, (rel >> 2) & 1
        at = jnp.bitwise_xor(owner, rel)
        rows = pl.ds(32 * kind, 32)
        ends = (
            (pieces_a[2 * c + y].at[x, :, rows, :], whole.at[kind, :, at, :, pl.ds(0, half)]),
            (pieces_b[2 * c + x].at[y, :, rows, :], whole.at[kind, :, at, :, pl.ds(half, half)]),
        )
        for i, (piece, place) in enumerate(ends):
            pair = (place, piece) if outward else (piece, place)
            copies.append(pltpu.make_async_copy(*pair, sems.at[kind, rel, i]))
    return copies


def packed_views(pack_ref):
    starts = (0, D, 2 * D, 2 * D + D // 2, 3 * D, 4 * D)
    return [pack_ref.at[:, pl.ds(a, b - a)] for a, b in zip(starts[:-1], starts[1:])]


def attention_forward_kernel(*refs):
    pieces_a, pieces_b = refs[0:4], refs[4:8]
    x_ref, seg_row, seg_col, gain_ref, rope_ref = refs[8:13]
    finals = refs[13:17]
    pack_ref, hidden_ref, small_ref, normed2_ref, whole, sems, out_sems = refs[17:]
    outs = [
        pltpu.make_async_copy(here, there, out_sems.at[i])
        for i, (here, there) in enumerate(zip(refs[17:21], finals))
    ]
    normed_ref, q_ref, k_ref, v_ref, att_ref = packed_views(pack_ref)
    owner = lax.axis_index(EX)
    half = D // 2
    for kind in range(3):
        for copy in weight_copies(pieces_a, pieces_b, whole, sems, owner, kind, False):
            copy.start()
    inputs = x_ref[...].astype(jnp.float32)
    inverse = lax.rsqrt(jnp.mean(inputs * inputs, axis=1, keepdims=True) + epsilon)
    normed = (inputs * inverse * gain_ref[0:1, :]).astype(jnp.bfloat16)
    normed_ref[...] = normed
    small_ref[:128, 8:9] = inverse
    small_ref[:128, 10:11] = seg_col[...].astype(jnp.float32)
    cosine, signed = rope_ref[0], rope_ref[1]
    for kind in range(2):
        for copy in weight_copies(pieces_a, pieces_b, whole, sems, owner, kind, False):
            copy.wait()
    query = jnp.dot(normed, whole[0].reshape(D, D), preferred_element_type=jnp.float32)
    keyval = jnp.dot(normed, whole[1].reshape(D, D), preferred_element_type=jnp.float32)
    for s in range(8):
        cols = slice(128 * s, 128 * s + 128)
        q_ref[:, cols] = turn(query[:, cols], cosine, signed).astype(jnp.bfloat16)
    for s in range(4):
        cols = slice(128 * s, 128 * s + 128)
        k_ref[:, cols] = turn(keyval[:, cols], cosine, signed).astype(jnp.bfloat16)
    v_ref[...] = keyval[:, half:].astype(jnp.bfloat16)
    rows_at = lax.broadcasted_iota(jnp.int32, (128, 128), 0)
    cols_at = lax.broadcasted_iota(jnp.int32, (128, 128), 1)
    visible = (rows_at >= cols_at) & (seg_col[...] == seg_row[...])
    visible2 = jnp.concatenate([visible, visible], axis=0)
    low = cols_at < 64
    for head in range(KV_HEADS):
        slab = slice(128 * (head // 2), 128 * (head // 2) + 128)
        q2 = halves_stacked(q_ref[:, 128 * head : 128 * head + 128], low)
        k2 = doubled(k_ref[:, slab], low, head % 2)
        v2 = doubled(v_ref[:, slab], low, head % 2)
        scores = lax.dot_general(
            q2, k2, (((1,), (1,)), ((), ())), preferred_element_type=jnp.float32
        )
        scores = jnp.where(visible2, scores * score_scale, -1e30)
        highest = jnp.max(scores, axis=1, keepdims=True)
        log_total = highest + jnp.log(jnp.sum(jnp.exp(scores - highest), axis=1, keepdims=True))
        probabilities = jnp.exp(scores - log_total).astype(jnp.bfloat16)
        small_ref[:, head : head + 1] = log_total
        mixed = jnp.dot(probabilities, v2, preferred_element_type=jnp.float32)
        att_ref[:, 128 * head : 128 * head + 128] = jnp.where(
            low, mixed[:128], mixed[128:]
        ).astype(jnp.bfloat16)
    for copy in weight_copies(pieces_a, pieces_b, whole, sems, owner, 2, False):
        copy.wait()
    outs[0].start()
    hidden = inputs + residual_scale * jnp.dot(
        att_ref[...], whole[2].reshape(D, D), preferred_element_type=jnp.float32
    )
    inverse2 = lax.rsqrt(jnp.mean(hidden * hidden, axis=1, keepdims=True) + epsilon)
    normed2 = (hidden * inverse2 * gain_ref[1:2, :]).astype(jnp.bfloat16)
    hidden_ref[...] = hidden
    small_ref[:128, 9:10] = inverse2
    outs[1].start()
    outs[2].start()
    for z in range(4):
        normed2_ref[z, 0] = normed2[:, :half]
        normed2_ref[z, 1] = normed2[:, half:]
    outs[3].start()
    for out in outs:
        out.wait()


def attention_forward(pieces_a, pieces_b, x, seg, gains, rope):
    hbm = pl.BlockSpec(memory_space=pltpu.HBM)
    vmem = pl.BlockSpec(memory_space=pltpu.VMEM)
    f32, b16 = jnp.float32, jnp.bfloat16
    shapes = [
        ((128, 4 * D), b16),
        ((128, D), f32),
        ((256, 16), f32),
        ((4, 2, 128, D // 2), b16),
    ]
    return pl.pallas_call(
        attention_forward_kernel,
        in_specs=[hbm] * 8 + [vmem] * 5,
        out_specs=[hbm] * 4,
        out_shape=[pltpu.HBM(s, t) for s, t in shapes],
        scratch_shapes=[pltpu.VMEM(s, t) for s, t in shapes]
        + [
            pltpu.VMEM((3, 4, 8, 32, D), b16),
            pltpu.SemaphoreType.DMA((3, 8, 2)),
            pltpu.SemaphoreType.DMA((4,)),
        ],
        compiler_params=pltpu.CompilerParams(vmem_limit_bytes=40 * 1024 * 1024),
    )(*pieces_a, *pieces_b, x, seg[None, :], seg[:, None], gains, rope)


def attention_backward_kernel(*refs):
    pieces_a, pieces_b = refs[0:4], refs[4:8]
    arrays = refs[8:20]
    grads_a, grads_b = refs[20:24], refs[24:28]
    finals = refs[28:31]
    buffers = refs[31:43]
    (
        x_ref,
        seg_row,
        gain_ref,
        rope_ref,
        pack_ref,
        hidden_ref,
        small_ref,
        dout_ref,
        back_ref,
        dgate_ref,
        routes_ref,
        router_ref,
    ) = buffers
    input_grad_ref, gains_ref, router_grad_ref = refs[43:46]
    whole, grad, datt_scr, dq_scr, dkv_scr, sems, out_sems, load_sems, last_sems = refs[46:]
    loads = [
        pltpu.make_async_copy(there, here, load_sems.at[i])
        for i, (there, here) in enumerate(zip(arrays, buffers))
    ]
    lasts = [
        pltpu.make_async_copy(here, there, last_sems.at[i])
        for i, (here, there) in enumerate(zip(refs[43:46], finals))
    ]
    for load in loads:
        load.start()
    normed_ref, q_ref, k_ref, v_ref, att_ref = packed_views(pack_ref)
    owner = lax.axis_index(EX)
    half = D // 2
    for kind in (2, 0, 1):
        for copy in weight_copies(pieces_a, pieces_b, whole, sems, owner, kind, False):
            copy.start()
    for load in loads:
        load.wait()
    hidden, inverse2 = hidden_ref[...], small_ref[:128, 9:10]
    normed2 = (hidden * inverse2 * gain_ref[1:2, :]).astype(jnp.bfloat16)
    names = lax.broadcasted_iota(jnp.int32, (EXPERTS, 128), 0)
    routes = routes_ref[...]
    named = routes[0:1] == names
    for i in range(1, TOPK):
        named = named | (routes[i : i + 1] == names)
    logits = lax.dot_general(
        router_ref[...], normed2, (((1,), (1,)), ((), ())), preferred_element_type=jnp.float32
    )
    highest = jnp.max(jnp.where(named, logits, -3e38), axis=0, keepdims=True)
    exponent = jnp.where(named, jnp.exp(jnp.where(named, logits - highest, 0.0)), 0.0)
    gates = exponent / jnp.sum(exponent, axis=0, keepdims=True)
    d_gates = dgate_ref[...]
    d_logits = (gates * (d_gates - jnp.sum(gates * d_gates, axis=0, keepdims=True))).astype(
        jnp.bfloat16
    )
    router_grad_ref[...] = jnp.dot(d_logits, normed2, preferred_element_type=jnp.float32)
    back = [
        sum(back_ref[z, i].astype(jnp.float32) for z in range(4)) for i in range(2)
    ]
    d_normed2 = jnp.concatenate(back, axis=1) + lax.dot_general(
        d_logits, router_ref[...], (((0,), (0,)), ((), ())), preferred_element_type=jnp.float32
    )
    gains_ref[1:2, :] = jnp.sum(d_normed2 * hidden * inverse2, axis=0, keepdims=True)
    weighted = d_normed2 * gain_ref[1:2, :]
    d_hidden = (
        dout_ref[...].astype(jnp.float32)
        + inverse2 * weighted
        - hidden
        * (inverse2 * inverse2 * inverse2)
        * jnp.mean(weighted * hidden, axis=1, keepdims=True)
    )
    d_branch = (residual_scale * d_hidden).astype(jnp.bfloat16)
    tn = (((0,), (0,)), ((), ()))
    nt = (((1,), (1,)), ((), ()))
    for z in range(4):
        grad[2, z] = (
            lax.dot_general(
                att_ref[:, 256 * z : 256 * z + 256], d_branch, tn, preferred_element_type=jnp.float32
            )
            .astype(jnp.bfloat16)
            .reshape(8, 32, D)
        )
    for copy in weight_copies(grads_a, grads_b, grad, out_sems, owner, 2, True):
        copy.start()
    for copy in weight_copies(pieces_a, pieces_b, whole, sems, owner, 2, False):
        copy.wait()
    datt_scr[...] = lax.dot_general(
        d_branch, whole[2].reshape(D, D), nt, preferred_element_type=jnp.float32
    ).astype(jnp.bfloat16)
    cosine, signed = rope_ref[0], -rope_ref[1]
    rows_at = lax.broadcasted_iota(jnp.int32, (128, 128), 0)
    cols_at = lax.broadcasted_iota(jnp.int32, (128, 128), 1)
    visible = (rows_at >= cols_at) & (
        small_ref[:128, 10:11] == seg_row[...].astype(jnp.float32)
    )
    visible2 = jnp.concatenate([visible, visible], axis=0)
    low = cols_at < 64
    keep_k = keep_v = None
    for head in range(KV_HEADS):
        cols = slice(128 * head, 128 * head + 128)
        slab = slice(128 * (head // 2), 128 * (head // 2) + 128)
        q2 = halves_stacked(q_ref[:, cols], low)
        k2 = doubled(k_ref[:, slab], low, head % 2)
        v2 = doubled(v_ref[:, slab], low, head % 2)
        d_att = datt_scr[:, cols]
        da2 = halves_stacked(d_att, low)
        scores = lax.dot_general(q2, k2, nt, preferred_element_type=jnp.float32)
        scores = jnp.where(visible2, scores * score_scale, -1e30)
        probs = jnp.exp(scores - small_ref[:, head : head + 1])
        d_value = lax.dot_general(
            probs.astype(jnp.bfloat16), da2, tn, preferred_element_type=jnp.float32
        )
        d_probs = lax.dot_general(da2, v2, nt, preferred_element_type=jnp.float32)
        product = d_att.astype(jnp.float32) * att_ref[:, cols].astype(jnp.float32)
        delta = jnp.sum(halves_stacked(product, low), axis=1, keepdims=True)
        d_scores = (probs * (d_probs - delta) * score_scale).astype(jnp.bfloat16)
        d_q2 = jnp.dot(d_scores, k2, preferred_element_type=jnp.float32)
        d_query = jnp.where(low, d_q2[:128], d_q2[128:])
        dq_scr[:, cols] = turn(d_query, cosine, signed).astype(jnp.bfloat16)
        d_key = lax.dot_general(d_scores, q2, tn, preferred_element_type=jnp.float32)
        d_key = d_key + pltpu.roll(d_key, 64, 1)
        d_value = d_value + pltpu.roll(d_value, 64, 1)
        if head % 2 == 0:
            keep_k, keep_v = d_key, d_value
        else:
            dkv_scr[:, slab] = turn(jnp.where(low, keep_k, d_key), cosine, signed).astype(
                jnp.bfloat16
            )
            dkv_scr[:, half + slab.start : half + slab.stop] = jnp.where(
                low, keep_v, d_value
            ).astype(jnp.bfloat16)
    for kind, source in ((0, dq_scr), (1, dkv_scr)):
        for z in range(4):
            grad[kind, z] = (
                lax.dot_general(
                    normed_ref[:, 256 * z : 256 * z + 256],
                    source[...],
                    tn,
                    preferred_element_type=jnp.float32,
                )
                .astype(jnp.bfloat16)
                .reshape(8, 32, D)
            )
        for copy in weight_copies(grads_a, grads_b, grad, out_sems, owner, kind, True):
            copy.start()
    for kind in range(2):
        for copy in weight_copies(pieces_a, pieces_b, whole, sems, owner, kind, False):
            copy.wait()
    d_normed = lax.dot_general(
        dq_scr[...], whole[0].reshape(D, D), nt, preferred_element_type=jnp.float32
    ) + lax.dot_general(
        dkv_scr[...], whole[1].reshape(D, D), nt, preferred_element_type=jnp.float32
    )
    inputs, inverse = x_ref[...].astype(jnp.float32), small_ref[:128, 8:9]
    gains_ref[0:1, :] = jnp.sum(d_normed * inputs * inverse, axis=0, keepdims=True)
    weighted = d_normed * gain_ref[0:1, :]
    input_grad_ref[...] = (
        d_hidden
        + inverse * weighted
        - inputs
        * (inverse * inverse * inverse)
        * jnp.mean(weighted * inputs, axis=1, keepdims=True)
    ).astype(jnp.bfloat16)
    for last in lasts:
        last.start()
    for kind in range(3):
        for copy in weight_copies(grads_a, grads_b, grad, out_sems, owner, kind, True):
            copy.wait()
    for last in lasts:
        last.wait()


def attention_backward(pieces_a, pieces_b, *rest):
    hbm = pl.BlockSpec(memory_space=pltpu.HBM)
    f32, b16 = jnp.float32, jnp.bfloat16
    piece = jax.ShapeDtypeStruct((2, 4, 96, D // 2), b16)
    shapes = [((128, D), b16), ((2, D), f32), ((EXPERTS, D), f32)]
    outs = pl.pallas_call(
        attention_backward_kernel,
        in_specs=[hbm] * (8 + len(rest)),
        out_specs=[hbm] * 11,
        out_shape=[piece] * 8 + [jax.ShapeDtypeStruct(*pair) for pair in shapes],
        scratch_shapes=[pltpu.VMEM(array.shape, array.dtype) for array in rest]
        + [pltpu.VMEM(*pair) for pair in shapes]
        + [
            pltpu.VMEM((3, 4, 8, 32, D), b16),
            pltpu.VMEM((3, 4, 8, 32, D), b16),
            pltpu.VMEM((128, D), b16),
            pltpu.VMEM((128, D), b16),
            pltpu.VMEM((128, D), b16),
            pltpu.SemaphoreType.DMA((3, 8, 2)),
            pltpu.SemaphoreType.DMA((3, 8, 2)),
            pltpu.SemaphoreType.DMA((len(rest),)),
            pltpu.SemaphoreType.DMA((3,)),
        ],
        compiler_params=pltpu.CompilerParams(vmem_limit_bytes=48 * 1024 * 1024),
    )(*pieces_a, *pieces_b, *rest)
    return outs[0:4], outs[4:8], outs[8], outs[9], outs[10]


def slice_kernel(*refs):
    weights, outs, buffers, sems = refs[0:2], refs[2:8], refs[8:14], refs[14]
    group = lax.axis_index(DP)
    loads, stores = [], []
    for i, weight in enumerate(weights):
        for s in range(1, 4):
            j = 3 * i + s - 1
            source = weight.at[jnp.bitwise_xor(group, s)]
            loads.append(pltpu.make_async_copy(source, buffers[j], sems.at[0, j]))
            stores.append(pltpu.make_async_copy(buffers[j], outs[j], sems.at[1, j]))
    for load in loads:
        load.start()
    for load, store in zip(loads, stores):
        load.wait()
        store.start()
    for store in stores:
        store.wait()


def sliced(up, down):
    hbm = pl.BlockSpec(memory_space=pltpu.HBM)
    outs = pl.pallas_call(
        slice_kernel,
        in_specs=[hbm] * 2,
        out_specs=[hbm] * 6,
        out_shape=[jax.ShapeDtypeStruct(up.shape[1:], up.dtype)] * 3
        + [jax.ShapeDtypeStruct(down.shape[1:], down.dtype)] * 3,
        scratch_shapes=[pltpu.VMEM(up.shape[1:], up.dtype)] * 3
        + [pltpu.VMEM(down.shape[1:], down.dtype)] * 3
        + [pltpu.SemaphoreType.DMA((2, 6))],
    )(up, down)
    return outs[:3], outs[3:]


def finish_experts_kernel(*refs):
    up, down, up_out, down_out = refs[0:4], refs[4:8], refs[8], refs[9]
    for s in range(4):
        at = jnp.bitwise_xor(lax.axis_index(DP), s)
        up_out[at] = up[s][...].astype(jnp.float32)
        down_out[at] = down[s][...].astype(jnp.float32)


def finish_experts(up, down):
    vmem = pl.BlockSpec(memory_space=pltpu.VMEM)
    return pl.pallas_call(
        finish_experts_kernel,
        in_specs=[vmem] * 8,
        out_specs=[vmem] * 2,
        out_shape=[
            jax.ShapeDtypeStruct((4, 256, 2 * F), jnp.float32),
            jax.ShapeDtypeStruct((4, 128, D), jnp.float32),
        ],
    )(*up, *down)


def finish_weights_kernel(*refs):
    pieces_a, pieces_b, outs, router_out = refs[0:4], refs[4:8], refs[8:11], refs[11]
    half = D // 2
    owner = lax.axis_index(EX)
    for rel in range(8):
        c, x, y = rel & 1, (rel >> 1) & 1, (rel >> 2) & 1
        at = jnp.bitwise_xor(owner, rel)
        rows = pl.ds(pl.multiple_of(at * 32, 32), 32)
        for i, piece in enumerate((pieces_a[2 * c + y].at[x], pieces_b[2 * c + x].at[y])):
            cols = pl.ds(half * i, half)
            for kind in range(3):
                outs[kind][rows, cols] = piece[32 * kind : 32 * kind + 32, :].astype(jnp.float32)
            router_out[at, :, cols] = piece[96:97, :].astype(jnp.float32)


def finish_weights(pieces_a, pieces_b):
    vmem = pl.BlockSpec(memory_space=pltpu.VMEM)
    return pl.pallas_call(
        finish_weights_kernel,
        in_specs=[vmem] * 8,
        out_specs=[vmem] * 4,
        out_shape=[jax.ShapeDtypeStruct((256, D), jnp.float32)] * 3
        + [jax.ShapeDtypeStruct((8, 1, D), jnp.float32)],
    )(*pieces_a, *pieces_b)


CORE, ACROSS, ALONG = 1, 2, 4


def swap(array, bit):
    return lax.ppermute(array, EX, [(i, i ^ bit) for i in range(8)])


def trade(array, step):
    return lax.ppermute(array, DP, [(i, i ^ step) for i in range(4)])


def everyone(array, axes):
    return lax.all_to_all(array, axes, split_axis=0, concat_axis=0, tiled=True)


def to_group(array, axes, count):
    return everyone(jnp.broadcast_to(array[None], (count,) + array.shape), axes)


def gather_halves(halves):
    column = everyone(halves, DP)
    return gather_plane(column[:, 0], column[:, 1])


def gather_plane(a0, b0):
    a = jnp.stack([a0, swap(a0, ACROSS)])
    b = jnp.stack([b0, swap(b0, ALONG)])
    a_far, b_far = swap(a, ALONG), swap(b, ACROSS)
    pieces_a = [a, a_far, swap(a, CORE), swap(a_far, CORE)]
    pieces_b = [b, b_far, swap(b, CORE), swap(b_far, CORE)]
    return pieces_a, pieces_b


def add(one, two):
    return (one.astype(jnp.float32) + two.astype(jnp.float32)).astype(jnp.bfloat16)


def scatter_halves(pieces_a, pieces_b):
    a_far = add(pieces_a[1], swap(pieces_a[3], CORE))
    b_far = add(pieces_b[1], swap(pieces_b[3], CORE))
    a_near = add(pieces_a[0], swap(pieces_a[2], CORE))
    b_near = add(pieces_b[0], swap(pieces_b[2], CORE))
    a = add(a_near, swap(a_far, ALONG))
    b = add(b_near, swap(b_far, ACROSS))
    a_own = add(a[0], swap(a[1], ACROSS))
    b_own = add(b[0], swap(b[1], ALONG))
    return everyone(jnp.stack([a_own, b_own], axis=1), DP)


def block_inner(
    layer_input,
    segment_ids,
    expert_routes,
    first_gain,
    w_query,
    w_keyvalue,
    w_output,
    second_gain,
    w_router,
    w_gate_up,
    w_down,
    out_cotangent,
):
    half = D // 2
    owner_at = lax.axis_index(EX)

    def own_part(weight):
        return lax.dynamic_slice_in_dim(weight, owner_at * 32, 32, 0)

    def split(rows):
        return jnp.stack([rows[:, :half], rows[:, half:]])

    pack = jnp.concatenate([own_part(w_query), own_part(w_keyvalue), own_part(w_output)], axis=0)
    weights_a, weights_b = gather_halves(jnp.broadcast_to(split(pack)[None], (4, 2, 96, half)))
    routes = expert_routes.T
    small = jnp.stack(
        [routes.astype(jnp.bfloat16).reshape(D), own_part(w_router).T.reshape(32 * EXPERTS)]
    )
    small = to_group(small, (EX, DP), 32)
    all_routes = small[:, 0].astype(jnp.int32).reshape(32, TOPK, 128)
    router = small[:, 1].reshape(8, 4, EXPERTS, 32).transpose(2, 1, 0, 3).reshape(EXPERTS, D)

    def exchange(pieces):
        return [pieces[0]] + [trade(pieces[s], s) for s in range(1, 4)]

    up_sent, down_sent = sliced(w_gate_up, w_down)
    up_pieces, down_pieces = exchange([w_gate_up, *up_sent]), exchange([w_down, *down_sent])
    cot_a, cot_b = gather_halves(jnp.broadcast_to(split(out_cotangent)[None], (4, 2, 128, half)))

    rope = jnp.asarray(np.stack(rope_constants(128)))
    gains = jnp.stack([first_gain, second_gain])
    saved = attention_forward(
        weights_a, weights_b, layer_input, segment_ids, gains, rope
    )
    packed, hidden, scalars, normed2 = saved
    tok_a, tok_b = gather_halves(normed2)

    def flat(pieces):
        return [p.reshape(1024, half) for p in pieces]

    mix_a, mix_b, back_a, back_b, d_up, d_down, d_gate = expert_call(
        flat(tok_a),
        flat(tok_b),
        flat(cot_a),
        flat(cot_b),
        up_pieces,
        down_pieces,
        all_routes,
        router,
    )

    def deep(pieces):
        return [p.reshape(2, 4, 128, half) for p in pieces]

    back = scatter_halves(deep(back_a), deep(back_b))
    d_gates = everyone(d_gate, (EX, DP)).reshape(EXPERTS, 128)
    grads_a, grads_b, input_grad, d_gains, d_router = attention_backward(
        weights_a,
        weights_b,
        layer_input,
        segment_ids[None, :],
        gains,
        rope,
        packed,
        hidden,
        scalars,
        out_cotangent,
        back,
        d_gates,
        routes,
        router,
    )
    d_up, d_down = exchange(d_up), exchange(d_down)
    gate_up_grad, down_grad = finish_experts(d_up, d_down)
    mixed = jnp.sum(scatter_halves(deep(mix_a), deep(mix_b)).astype(jnp.float32), axis=0)
    mixed = jnp.concatenate([mixed[0], mixed[1]], axis=1)
    layer_output = (hidden + residual_scale * mixed).astype(jnp.bfloat16)

    small = jnp.concatenate(
        [
            jnp.broadcast_to(d_gains.reshape(1, 2 * D), (32, 2 * D)),
            d_router.reshape(EXPERTS, 32, 32).transpose(1, 2, 0).reshape(32, D),
        ],
        axis=1,
    )
    small = jnp.sum(everyone(small, (DP, EX)), axis=0)
    first_gain_grad, second_gain_grad = small[:D], small[D : 2 * D]

    summed = jnp.sum(scatter_halves(grads_a, grads_b).astype(jnp.float32), axis=0)
    summed = jnp.concatenate([summed, small[2 * D :].reshape(2, 1, half)], axis=1)
    summed = summed.astype(jnp.bfloat16)
    whole_a, whole_b = gather_plane(summed[0], summed[1])
    query_grad, keyvalue_grad, output_grad, router_grad = finish_weights(whole_a, whole_b)
    router_grad = router_grad.reshape(256, EXPERTS)
    return (
        layer_output,
        input_grad,
        first_gain_grad,
        query_grad,
        keyvalue_grad,
        output_grad,
        second_gain_grad,
        router_grad,
        gate_up_grad,
        down_grad,
    )


def block_device(*args):
    return block_inner(*args)


def solution(mesh):
    sizes = (mesh.shape[DP], mesh.shape[EX])
    return jax.shard_map(
        block_device if sizes == (4, 8) else general_device,
        mesh=mesh,
        in_specs=(
            P((DP, EX), None),
            P((DP, EX)),
            P((DP, EX), None),
            P(),
            P(DP, None),
            P(DP, None),
            P(DP, None),
            P(),
            P(DP, None),
            P(EX, DP, None),
            P(EX, DP, None),
            P((DP, EX), None),
        ),
        out_specs=(
            P((DP, EX), None),
            P((DP, EX), None),
            P(),
            P(DP, None),
            P(DP, None),
            P(DP, None),
            P(),
            P(DP, None),
            P(EX, DP, None),
            P(EX, DP, None),
        ),
        check_vma=False,
    )
```

profile of v0, /device:TPU:0, one launch (start us, length us, event | category | flops | bytes accessed | tf_op | source)
XLA Modules:
  0.0 516.6 jit_solution(6611902737953694585)
XLA Ops:
  2.7 26.4 %all_to_all.49 = bf16[4,2,96,512]{3,2,1,0:T(8,128)(2,1)S(1)} all-to-all(bf16[4,2,96,512]{3,2,1,0:T(8,128)(2,1)S(1)} %broadcast_in_dim.14), channel_id=1, replica_groups=mesh['dp'=4,'expert'=8] {'dp'}, dimensions={0} | all-to-all | bytes 1572864 | tf_op jit(solution)/shard_map/all_to_all | solution.py:1091
  29.3 1.6 collective-permute-start.4
  30.9 1.5 collective-permute-start
  32.4 6.7 %collective-permute-done.4 = bf16[4,96,512]{2,1,0:T(8,128)(2,1)S(1)} collective-permute-done((bf16[4,96,512]{2,1,0:T(8,128)(2,1)S(1)}, bf16[4,96,512]{2,1,0:T(8,128)(2,1)S(1)}, u32[]{:S(2)}, u32[]{:S(2)}) %collective-permute-start.4) | collective-permute-done | bytes 393248 | tf_op jit(solution)/shard_map/ppermute | solution.py:1083
  39.2 1.6 collective-permute-start.5
  41.1 1.4 collective-permute-start.1
  43.6 4.2 all-to-all-start.2
  48.4 8.8 %collective-permute-done.5.refs_5_ = bf16[2,4,96,512]{3,2,1,0:T(8,128)(2,1)S(1)} collective-permute-done((bf16[2,4,96,512]{3,2,1,0:T(8,128)(2,1)S(1)}, bf16[2,4,96,512]{3,2,1,0:T(8,128)(2,1)S(1)}, u32[]{:S(2)}, u32[]{:S(2)}) %collective-permute-start.5) | collective-permute-done | bytes 786464 | tf_op jit(solution)/shard_map/ppermute | solution.py:1083
  62.6 6.1 %shard_map.204 = (bf16[128,4096]{1,0:T(8,128)(2,1)}, f32[128,1024]{1,0:T(8,128)}, f32[256,16]{1,0:T(8,128)}, bf16[4,2,128,512]{3,2,1,0:T(8,128)(2,1)}) custom-call(bf16[2,4,96,512]{3,2,1,0:T(8,128)(2,1)S(1)} %pad_maximum_fusion.6.refs_0_, bf16[2,4,96,512]{3,2,1,0:T(8,128)(2,1)S(1)} %collective-permute-done.1.refs_1_, ...), custom_call_target="tpu_custom_call" | custom-call | tf_op jit(solution)/shard_map/pallas_call | solution.py:781
  68.7 2.7 all-to-all-done.2
  71.4 3.5 all-to-all-start.1
  74.9 2.4 slice_bitcast_fusion.9
  77.9 2.6 shard_map.205
  80.4 2.0 collective-permute-start.27
  82.5 2.4 collective-permute-start.28
  86.0 4.6 collective-permute-done.20
  90.6 2.1 pad_maximum_fusion.3
  92.7 10.2 %all-to-all-done.1 = bf16[4,2,128,512]{3,2,1,0:T(8,128)(2,1)S(1)} async-done(((bf16[4,2,128,512]{3,2,1,0:T(8,128)(2,1)}), bf16[4,2,128,512]{3,2,1,0:T(8,128)(2,1)S(1)}, u32[]{:S(2)}, u32[]{:S(2)}) %all-to-all-start.1) | async-done | bytes 1048608 | tf_op jit(solution)/shard_map/all_to_all | solution.py:1091
  103.8 1.5 collective-permute-start.21
  105.3 12.7 %collective-permute-done.28.refs_22_ = bf16[128,1024]{1,0:T(8,128)(2,1)S(1)} collective-permute-done((bf16[128,1024]{1,0:T(8,128)(2,1)}, bf16[128,1024]{1,0:T(8,128)(2,1)S(1)}, u32[]{:S(2)}, u32[]{:S(2)}) %collective-permute-start.28) | collective-permute-done | bytes 262176 | tf_op jit(solution)/shard_map/ppermute | solution.py:1087
  118.5 4.7 collective-permute-start.24
  123.4 6.6 %collective-permute-done.12 = bf16[4,128,512]{2,1,0:T(8,128)(2,1)S(1)} collective-permute-done((bf16[4,128,512]{2,1,0:T(8,128)(2,1)S(1)}, bf16[4,128,512]{2,1,0:T(8,128)(2,1)S(1)}, u32[]{:S(2)}, u32[]{:S(2)}) %collective-permute-start.12) | collective-permute-done | bytes 524320 | tf_op jit(solution)/shard_map/ppermute | solution.py:1083
  134.0 11.9 %collective-permute-done.24.refs_17_ = bf16[256,1024]{1,0:T(8,128)(2,1)S(1)} collective-permute-done((bf16[256,1024]{1,0:T(8,128)(2,1)S(1)}, bf16[256,1024]{1,0:T(8,128)(2,1)S(1)}, u32[]{:S(2)}, u32[]{:S(2)}) %collective-permute-start.24) | collective-permute-done | bytes 524320 | tf_op jit(solution)/shard_map/ppermute | solution.py:1087
  146.4 15.1 %collective-permute-done.25.refs_18_ = bf16[256,1024]{1,0:T(8,128)(2,1)S(1)} collective-permute-done((bf16[256,1024]{1,0:T(8,128)(2,1)S(1)}, bf16[256,1024]{1,0:T(8,128)(2,1)S(1)}, u32[]{:S(2)}, u32[]{:S(2)}) %collective-permute-start.25) | collective-permute-done | bytes 524320 | tf_op jit(solution)/shard_map/ppermute | solution.py:1087
  163.2 8.8 %collective-permute-done.17 = bf16[2,4,128,512]{3,2,1,0:T(8,128)(2,1)} collective-permute-done((bf16[2,4,128,512]{3,2,1,0:T(8,128)(2,1)S(1)}, bf16[2,4,128,512]{3,2,1,0:T(8,128)(2,1)}, u32[]{:S(2)}, u32[]{:S(2)}) %collective-permute-start.17) | collective-permute-done | bytes 1048608 | tf_op jit(solution)/shard_map/ppermute | solution.py:1083
  173.0 14.5 %collective-permute-done.13 = bf16[2,4,128,512]{3,2,1,0:T(8,128)(2,1)} collective-permute-done((bf16[2,4,128,512]{3,2,1,0:T(8,128)(2,1)}, bf16[2,4,128,512]{3,2,1,0:T(8,128)(2,1)}, u32[]{:S(2)}, u32[]{:S(2)}) %collective-permute-start.13) | collective-permute-done | bytes 1048608 | tf_op jit(solution)/shard_map/ppermute | solution.py:1083
  187.5 5.9 %collective-permute-done.9 = bf16[2,4,128,512]{3,2,1,0:T(8,128)(2,1)} collective-permute-done((bf16[2,4,128,512]{3,2,1,0:T(8,128)(2,1)}, bf16[2,4,128,512]{3,2,1,0:T(8,128)(2,1)}, u32[]{:S(2)}, u32[]{:S(2)}) %collective-permute-start.9) | collective-permute-done | bytes 1048608 | tf_op jit(solution)/shard_map/ppermute | solution.py:1083
  193.7 13.6 %all_to_all.50 = bf16[32,2,1024]{2,1,0:T(2,128)(2,1)S(1)} all-to-all(bf16[32,2,1024]{2,1,0:T(2,128)(2,1)S(1)} %broadcast_in_dim.36), channel_id=1, replica_groups=mesh['dp'=4,'expert'=8] {'expert','dp'}, dimensions={0} | all-to-all | bytes 262144 | tf_op jit(solution)/shard_map/all_to_all | solution.py:1091
  210.1 30.1 %shard_map.206 = (bf16[1024,512]{1,0:T(8,128)(2,1)}, bf16[1024,512]{1,0:T(8,128)(2,1)}, bf16[1024,512]{1,0:T(8,128)(2,1)}, bf16[1024,512]{1,0:T(8,128)(2,1)}, bf...) custom-call(bf16[1024,512]{1,0:T(8,128)(2,1)} %bitcast.15.refs_0_, ...), custom_call_target="tpu_custom_call" | custom-call | tf_op jit(solution)/shard_map/pallas_call | solution.py:615
  240.9 2.3 collective-permute-done.39
  243.2 1.5 fusion.2
  246.8 23.2 %collective-permute-done.40 = bf16[2,4,128,512]{3,2,1,0:T(8,128)(2,1)S(1)} collective-permute-done((bf16[2,4,128,512]{3,2,1,0:T(8,128)(2,1)S(1)}, bf16[2,4,128,512]{3,2,1,0:T(8,128)(2,1)S(1)}, u32[]{:S(2)}, u32[]{:S(2)}) %collective-permute-start.40) | collective-permute-done | bytes 1048608 | tf_op jit(solution)/shard_map/ppermute | solution.py:1083
  274.1 2.9 all-to-all-start.6
  277.6 7.2 %collective-permute-done.41 = bf16[4,128,512]{2,1,0:T(8,128)(2,1)} collective-permute-done((bf16[4,128,512]{2,1,0:T(8,128)(2,1)}, bf16[4,128,512]{2,1,0:T(8,128)(2,1)}, u32[]{:S(2)}, u32[]{:S(2)}) %collective-permute-start.41) | collective-permute-done | bytes 524320 | tf_op jit(solution)/shard_map/ppermute | solution.py:1083
  289.1 3.7 all-to-all-start.5
  292.9 1.9 fusion.6
  296.1 2.5 fusion.4
  299.4 18.9 %collective-permute-done.32 = bf16[2,4,128,512]{3,2,1,0:T(8,128)(2,1)S(1)} collective-permute-done((bf16[2,4,128,512]{3,2,1,0:T(8,128)(2,1)S(1)}, bf16[2,4,128,512]{3,2,1,0:T(8,128)(2,1)S(1)}, u32[]{:S(2)}, u32[]{:S(2)}) %collective-permute-start.32) | collective-permute-done | bytes 1048608 | tf_op jit(solution)/shard_map/ppermute | solution.py:1083
  318.3 2.7 add_convert_fusion.3
  322.0 12.4 %shard_map.207 = (bf16[2,4,96,512]{3,2,1,0:T(8,128)(2,1)S(1)}, bf16[2,4,96,512]{3,2,1,0:T(8,128)(2,1)S(1)}, bf16[2,4,96,512]{3,2,1,0:T(8,128)(2,1)}, bf16[2,4,96...) custom-call(bf16[2,4,96,512]{3,2,1,0:T(8,128)(2,1)} %copy-done.3, ...), custom_call_target="tpu_custom_call" | custom-call | tf_op jit(solution)/shard_map/pallas_call | solution.py:975
  335.4 2.1 add_convert_fusion.2
  341.1 7.8 %collective-permute-done.33 = bf16[4,128,512]{2,1,0:T(8,128)(2,1)S(1)} collective-permute-done((bf16[4,128,512]{2,1,0:T(8,128)(2,1)S(1)}, bf16[4,128,512]{2,1,0:T(8,128)(2,1)S(1)}, u32[]{:S(2)}, u32[]{:S(2)}) %collective-permute-start.33) | collective-permute-done | bytes 524320 | tf_op jit(solution)/shard_map/ppermute | solution.py:1083
  351.1 1.6 collective-permute-done.37
  353.9 4.5 all-to-all-start.4
  358.9 10.1 %collective-permute-done.48 = bf16[2,4,96,512]{3,2,1,0:T(8,128)(2,1)} collective-permute-done((bf16[2,4,96,512]{3,2,1,0:T(8,128)(2,1)}, bf16[2,4,96,512]{3,2,1,0:T(8,128)(2,1)}, u32[]{:S(2)}, u32[]{:S(2)}) %collective-permute-start.48) | collective-permute-done | bytes 786464 | tf_op jit(solution)/shard_map/ppermute | solution.py:1083
  369.0 1.7 add_convert_fusion.7
  372.0 1.7 add_convert_fusion.4
  374.4 1.7 collective-permute-start.53
  377.2 6.1 %all-to-all-done.4 = bf16[4,2,128,512]{3,2,1,0:T(8,128)(2,1)} async-done(((bf16[4,2,128,512]{3,2,1,0:T(8,128)(2,1)}), bf16[4,2,128,512]{3,2,1,0:T(8,128)(2,1)}, u32[]{:S(2)}, u32[]{:S(2)}) %all-to-all-start.4) | async-done | bytes 1048608 | tf_op jit(solution)/shard_map/all_to_all | solution.py:1091
  383.2 3.5 all-to-all-start.7
  390.1 10.0 %all-to-all-done.7 = f32[32,1,3072]{2,1,0:T(1,128)S(1)} async-done(((f32[32,1,3072]{2,1,0:T(1,128)}), f32[32,1,3072]{2,1,0:T(1,128)S(1)}, u32[]{:S(2)}, u32[]{:S(2)}) %all-to-all-start.7) | async-done | bytes 393248 | tf_op jit(solution)/shard_map/all_to_all | solution.py:1091
  400.0 4.2 all-to-all-start.8
  404.2 2.0 collective-permute-start.65
  406.3 2.8 collective-permute-start.63
  409.1 1.5 collective-permute-start.64
  410.6 1.5 collective-permute-start.66
  412.1 25.4 %collective-permute-done.65.refs_5_ = bf16[128,1024]{1,0:T(8,128)(2,1)S(1)} collective-permute-done((bf16[128,1024]{1,0:T(8,128)(2,1)S(1)}, bf16[128,1024]{1,0:T(8,128)(2,1)S(1)}, u32[]{:S(2)}, u32[]{:S(2)}) %collective-permute-start.65) | collective-permute-done | bytes 262176 | tf_op jit(solution)/shard_map/ppermute | solution.py:1087
  437.4 2.2 collective-permute-start.67
  439.6 47.3 %collective-permute-done.66.refs_6_ = bf16[128,1024]{1,0:T(8,128)(2,1)S(1)} collective-permute-done((bf16[128,1024]{1,0:T(8,128)(2,1)S(1)}, bf16[128,1024]{1,0:T(8,128)(2,1)S(1)}, u32[]{:S(2)}, u32[]{:S(2)}) %collective-permute-start.66) | collective-permute-done | bytes 262176 | tf_op jit(solution)/shard_map/ppermute | solution.py:1087
  488.6 4.9 shard_map.209
  493.5 1.4 convert_reduce_fusion
  498.8 2.5 collective-permute-done.54
  505.8 2.6 collective-permute-done.59.refs_5_
  511.6 3.4 shard_map.208
  (302 shorter events, 66.9 us)
Async XLA Ops:
  29.3 9.8 %collective-permute-start.4 = (bf16[4,96,512]{2,1,0:T(8,128)(2,1)S(1)}, bf16[4,96,512]{2,1,0:T(8,128)(2,1)S(1)}, u32[]{:S(2)}, u32[]{:S(2)}) collective-permute-start(bf16[4,96,512]{2,1,0:T(8,128)(2,1)S(1)} %get-tuple-element.155), channel_id=1, source_target_pairs={{0,4},{1,5},{2,6},{3,7},{4,0},{5,1},{6,2},{7,3},{8,12},{9,13},{10,... | collective-permute-start | bytes 1179656 | tf_op jit(solution)/shard_map/ppermute | solution.py:1083
  30.9 10.1 %collective-permute-start = (bf16[4,96,512]{2,1,0:T(8,128)(2,1)S(1)}, bf16[4,96,512]{2,1,0:T(8,128)(2,1)S(1)}, u32[]{:S(2)}, u32[]{:S(2)}) collective-permute-start(bf16[4,96,512]{2,1,0:T(8,128)(2,1)S(1)} %get-tuple-element.154), channel_id=1, source_target_pairs={{0,2},{1,3},{2,0},{3,1},{4,6},{5,7},{6,4},{7,5},{8,10},{9,11},{10,... | collective-permute-start | bytes 1179656 | tf_op jit(solution)/shard_map/ppermute | solution.py:1083
  39.2 18.0 %collective-permute-start.5 = (bf16[2,4,96,512]{3,2,1,0:T(8,128)(2,1)S(1)}, bf16[2,4,96,512]{3,2,1,0:T(8,128)(2,1)S(1)}, u32[]{:S(2)}, u32[]{:S(2)}) collective-permute-start(bf16[2,4,96,512]{3,2,1,0:T(8,128)(2,1)S(1)} %pad_maximum_fusion.7.refs_4_), channel_id=1, source_target_pairs={{0,2},{1,3},{2,0},{3,1},{4,6},{5,7},{6,4},{7,5},{8,10},{9,11},{10,... | collective-permute-start | bytes 2359304 | tf_op jit(solution)/shard_map/ppermute | solution.py:1083
  41.1 16.9 %collective-permute-start.1 = (bf16[2,4,96,512]{3,2,1,0:T(8,128)(2,1)S(1)}, bf16[2,4,96,512]{3,2,1,0:T(8,128)(2,1)S(1)}, u32[]{:S(2)}, u32[]{:S(2)}) collective-permute-start(bf16[2,4,96,512]{3,2,1,0:T(8,128)(2,1)S(1)} %pad_maximum_fusion.6.refs_0_), channel_id=1, source_target_pairs={{0,4},{1,5},{2,6},{3,7},{4,0},{5,1},{6,2},{7,3},{8,12},{9,13},{10,... | collective-permute-start | bytes 2359304 | tf_op jit(solution)/shard_map/ppermute | solution.py:1083
  43.6 27.8 %all-to-all-start.2 = ((bf16[4,2,128,512]{3,2,1,0:T(8,128)(2,1)}), bf16[4,2,128,512]{3,2,1,0:T(8,128)(2,1)}, u32[]{:S(2)}, u32[]{:S(2)}) async-start(bf16[4,2,128,512]{3,2,1,0:T(8,128)(2,1)} %broadcast_in_dim.17), calls=%async_computation.2 | async-start | bytes 2097152 | tf_op jit(solution)/shard_map/all_to_all | solution.py:1091
  47.8 11.8 %collective-permute-start.6 = (bf16[2,4,96,512]{3,2,1,0:T(8,128)(2,1)S(1)}, bf16[2,4,96,512]{3,2,1,0:T(8,128)(2,1)}, u32[]{:S(2)}, u32[]{:S(2)}) collective-permute-start(bf16[2,4,96,512]{3,2,1,0:T(8,128)(2,1)S(1)} %pad_maximum_fusion.7.refs_4_), channel_id=1, source_target_pairs={{0,1},{1,0},{2,3},{3,2},{4,5},{5,4},{6,7},{7,6},{8,9},{9,8},{10,11... | collective-permute-start | bytes 2359304 | tf_op jit(solution)/shard_map/ppermute | solution.py:1083
  47.9 11.7 %collective-permute-start.2 = (bf16[2,4,96,512]{3,2,1,0:T(8,128)(2,1)S(1)}, bf16[2,4,96,512]{3,2,1,0:T(8,128)(2,1)}, u32[]{:S(2)}, u32[]{:S(2)}) collective-permute-start(bf16[2,4,96,512]{3,2,1,0:T(8,128)(2,1)S(1)} %pad_maximum_fusion.6.refs_0_), channel_id=1, source_target_pairs={{0,1},{1,0},{2,3},{3,2},{4,5},{5,4},{6,7},{7,6},{8,9},{9,8},{10,11... | collective-permute-start | bytes 2359304 | tf_op jit(solution)/shard_map/ppermute | solution.py:1083
  71.4 31.6 %all-to-all-start.1 = ((bf16[4,2,128,512]{3,2,1,0:T(8,128)(2,1)}), bf16[4,2,128,512]{3,2,1,0:T(8,128)(2,1)S(1)}, u32[]{:S(2)}, u32[]{:S(2)}) async-start(bf16[4,2,128,512]{3,2,1,0:T(8,128)(2,1)} %get-tuple-element.63), calls=%async_computation.1 | async-start | bytes 2097152 | tf_op jit(solution)/shard_map/all_to_all | solution.py:1091
  77.4 13.3 %collective-permute-start.20 = (bf16[4,128,512]{2,1,0:T(8,128)(2,1)}, bf16[4,128,512]{2,1,0:T(8,128)(2,1)}, u32[]{:S(2)}, u32[]{:S(2)}) collective-permute-start(bf16[4,128,512]{2,1,0:T(8,128)(2,1)} %get-tuple-element.146), channel_id=1, source_target_pairs={{0,4},{1,5},{2,6},{3,7},{4,0},{5,1},{6,2},{7,3},{8,12},{9,13},{10,... | collective-permute-start | bytes 1572872 | tf_op jit(solution)/shard_map/ppermute | solution.py:1083
  80.4 23.4 %collective-permute-start.27 = (bf16[128,1024]{1,0:T(8,128)(2,1)}, bf16[128,1024]{1,0:T(8,128)(2,1)S(1)}, u32[]{:S(2)}, u32[]{:S(2)}) collective-permute-start(bf16[128,1024]{1,0:T(8,128)(2,1)} %get-tuple-element.67), channel_id=1, source_target_pairs={{0,8},{8,0},{16,24},{24,16},{1,9},{9,1},{17,25},{25,17},{2,10},{10... | collective-permute-start | bytes 786440 | tf_op jit(solution)/shard_map/ppermute | solution.py:1087
  82.5 35.5 %collective-permute-start.28 = (bf16[128,1024]{1,0:T(8,128)(2,1)}, bf16[128,1024]{1,0:T(8,128)(2,1)S(1)}, u32[]{:S(2)}, u32[]{:S(2)}) collective-permute-start(bf16[128,1024]{1,0:T(8,128)(2,1)} %get-tuple-element.68), channel_id=1, source_target_pairs={{0,16},{8,24},{16,0},{24,8},{1,17},{9,25},{17,1},{25,9},{2,18},{10... | collective-permute-start | bytes 786440 | tf_op jit(solution)/shard_map/ppermute | solution.py:1087
  84.8 33.7 %collective-permute-start.29 = (bf16[128,1024]{1,0:T(8,128)(2,1)}, bf16[128,1024]{1,0:T(8,128)(2,1)S(1)}, u32[]{:S(2)}, u32[]{:S(2)}) collective-permute-start(bf16[128,1024]{1,0:T(8,128)(2,1)} %get-tuple-element.69), channel_id=1, source_target_pairs={{0,24},{8,16},{16,8},{24,0},{1,25},{9,17},{17,9},{25,1},{2,26},{10... | collective-permute-start | bytes 786440 | tf_op jit(solution)/shard_map/ppermute | solution.py:1087
  84.9 33.6 %collective-permute-start.16 = (bf16[4,128,512]{2,1,0:T(8,128)(2,1)}, bf16[4,128,512]{2,1,0:T(8,128)(2,1)}, u32[]{:S(2)}, u32[]{:S(2)}) collective-permute-start(bf16[4,128,512]{2,1,0:T(8,128)(2,1)} %get-tuple-element.145), channel_id=1, source_target_pairs={{0,2},{1,3},{2,0},{3,1},{4,6},{5,7},{6,4},{7,5},{8,10},{9,11},{10,... | collective-permute-start | bytes 1572872 | tf_op jit(solution)/shard_map/ppermute | solution.py:1083
  103.2 20.1 %collective-permute-start.8 = (bf16[4,128,512]{2,1,0:T(8,128)(2,1)S(1)}, bf16[4,128,512]{2,1,0:T(8,128)(2,1)S(1)}, u32[]{:S(2)}, u32[]{:S(2)}) collective-permute-start(bf16[4,128,512]{2,1,0:T(8,128)(2,1)S(1)} %get-tuple-element.149), channel_id=1, source_target_pairs={{0,2},{1,3},{2,0},{3,1},{4,6},{5,7},{6,4},{7,5},{8,10},{9,11},{10,... | collective-permute-start | bytes 1572872 | tf_op jit(solution)/shard_map/ppermute | solution.py:1083
  103.8 57.7 %collective-permute-start.21 = (bf16[2,4,128,512]{3,2,1,0:T(8,128)(2,1)}, bf16[2,4,128,512]{3,2,1,0:T(8,128)(2,1)S(1)}, u32[]{:S(2)}, u32[]{:S(2)}) collective-permute-start(bf16[2,4,128,512]{3,2,1,0:T(8,128)(2,1)} %pad_maximum_fusion.3), channel_id=1, source_target_pairs={{0,2},{1,3},{2,0},{3,1},{4,6},{5,7},{6,4},{7,5},{8,10},{9,11},{10,... | collective-permute-start | bytes 3145736 | tf_op jit(solution)/shard_map/ppermute | solution.py:1083
  118.0 11.9 %collective-permute-start.12 = (bf16[4,128,512]{2,1,0:T(8,128)(2,1)S(1)}, bf16[4,128,512]{2,1,0:T(8,128)(2,1)S(1)}, u32[]{:S(2)}, u32[]{:S(2)}) collective-permute-start(bf16[4,128,512]{2,1,0:T(8,128)(2,1)S(1)} %get-tuple-element.150), channel_id=1, source_target_pairs={{0,4},{1,5},{2,6},{3,7},{4,0},{5,1},{6,2},{7,3},{8,12},{9,13},{10,... | collective-permute-start | bytes 1572872 | tf_op jit(solution)/shard_map/ppermute | solution.py:1083
  118.5 44.0 %collective-permute-start.22 = (bf16[2,4,128,512]{3,2,1,0:T(8,128)(2,1)}, bf16[2,4,128,512]{3,2,1,0:T(8,128)(2,1)S(1)}, u32[]{:S(2)}, u32[]{:S(2)}) collective-permute-start(bf16[2,4,128,512]{3,2,1,0:T(8,128)(2,1)} %pad_maximum_fusion.3), channel_id=1, source_target_pairs={{0,1},{1,0},{2,3},{3,2},{4,5},{5,4},{6,7},{7,6},{8,9},{9,8},{10,11... | collective-permute-start | bytes 3145736 | tf_op jit(solution)/shard_map/ppermute | solution.py:1083
  118.5 27.4 %collective-permute-start.24 = (bf16[256,1024]{1,0:T(8,128)(2,1)S(1)}, bf16[256,1024]{1,0:T(8,128)(2,1)S(1)}, u32[]{:S(2)}, u32[]{:S(2)}) collective-permute-start(bf16[256,1024]{1,0:T(8,128)(2,1)S(1)} %copy-done.64), channel_id=1, source_target_pairs={{0,8},{8,0},{16,24},{24,16},{1,9},{9,1},{17,25},{25,17},{2,10},{10... | collective-permute-start | bytes 1572872 | tf_op jit(solution)/shard_map/ppermute | solution.py:1087
  123.3 38.2 %collective-permute-start.25 = (bf16[256,1024]{1,0:T(8,128)(2,1)S(1)}, bf16[256,1024]{1,0:T(8,128)(2,1)S(1)}, u32[]{:S(2)}, u32[]{:S(2)}) collective-permute-start(bf16[256,1024]{1,0:T(8,128)(2,1)S(1)} %copy-done.63), channel_id=1, source_target_pairs={{0,16},{8,24},{16,0},{24,8},{1,17},{9,25},{17,1},{25,9},{2,18},{10... | collective-permute-start | bytes 1572872 | tf_op jit(solution)/shard_map/ppermute | solution.py:1087
  130.0 32.1 %collective-permute-start.26 = (bf16[256,1024]{1,0:T(8,128)(2,1)S(1)}, bf16[256,1024]{1,0:T(8,128)(2,1)S(1)}, u32[]{:S(2)}, u32[]{:S(2)}) collective-permute-start(bf16[256,1024]{1,0:T(8,128)(2,1)S(1)} %copy-done.62), channel_id=1, source_target_pairs={{0,24},{8,16},{16,8},{24,0},{1,25},{9,17},{17,9},{25,1},{2,26},{10... | collective-permute-start | bytes 1572872 | tf_op jit(solution)/shard_map/ppermute | solution.py:1087
  145.9 26.1 %collective-permute-start.17 = (bf16[2,4,128,512]{3,2,1,0:T(8,128)(2,1)S(1)}, bf16[2,4,128,512]{3,2,1,0:T(8,128)(2,1)}, u32[]{:S(2)}, u32[]{:S(2)}) collective-permute-start(bf16[2,4,128,512]{3,2,1,0:T(8,128)(2,1)S(1)} %pad_maximum_fusion.2), channel_id=1, source_target_pairs={{0,4},{1,5},{2,6},{3,7},{4,0},{5,1},{6,2},{7,3},{8,12},{9,13},{10,... | collective-permute-start | bytes 3145736 | tf_op jit(solution)/shard_map/ppermute | solution.py:1083
  161.5 10.5 %collective-permute-start.18 = (bf16[2,4,128,512]{3,2,1,0:T(8,128)(2,1)S(1)}, bf16[2,4,128,512]{3,2,1,0:T(8,128)(2,1)S(1)}, u32[]{:S(2)}, u32[]{:S(2)}) collective-permute-start(bf16[2,4,128,512]{3,2,1,0:T(8,128)(2,1)S(1)} %pad_maximum_fusion.2), channel_id=1, source_target_pairs={{0,1},{1,0},{2,3},{3,2},{4,5},{5,4},{6,7},{7,6},{8,9},{9,8},{10,11... | collective-permute-start | bytes 3145736 | tf_op jit(solution)/shard_map/ppermute | solution.py:1083
  161.5 11.1 %collective-permute-start.23 = (bf16[2,4,128,512]{3,2,1,0:T(8,128)(2,1)S(1)}, bf16[2,4,128,512]{3,2,1,0:T(8,128)(2,1)S(1)}, u32[]{:S(2)}, u32[]{:S(2)}) collective-permute-start(bf16[2,4,128,512]{3,2,1,0:T(8,128)(2,1)S(1)} %collective-permute-done.21), channel_id=1, source_target_pairs={{0,1},{1,0},{2,3},{3,2},{4,5},{5,4},{6,7},{7,6},{8,9},{9,8},{10,11... | collective-permute-start | bytes 3145736 | tf_op jit(solution)/shard_map/ppermute | solution.py:1083
  162.0 25.5 %collective-permute-start.13 = (bf16[2,4,128,512]{3,2,1,0:T(8,128)(2,1)}, bf16[2,4,128,512]{3,2,1,0:T(8,128)(2,1)}, u32[]{:S(2)}, u32[]{:S(2)}) collective-permute-start(bf16[2,4,128,512]{3,2,1,0:T(8,128)(2,1)} %pad_maximum_fusion.1), channel_id=1, source_target_pairs={{0,2},{1,3},{2,0},{3,1},{4,6},{5,7},{6,4},{7,5},{8,10},{9,11},{10,... | collective-permute-start | bytes 3145736 | tf_op jit(solution)/shard_map/ppermute | solution.py:1083
  162.6 30.8 %collective-permute-start.9 = (bf16[2,4,128,512]{3,2,1,0:T(8,128)(2,1)}, bf16[2,4,128,512]{3,2,1,0:T(8,128)(2,1)}, u32[]{:S(2)}, u32[]{:S(2)}) collective-permute-start(bf16[2,4,128,512]{3,2,1,0:T(8,128)(2,1)} %pad_maximum_fusion), channel_id=1, source_target_pairs={{0,4},{1,5},{2,6},{3,7},{4,0},{5,1},{6,2},{7,3},{8,12},{9,13},{10,... | collective-permute-start | bytes 3145736 | tf_op jit(solution)/shard_map/ppermute | solution.py:1083
  172.0 38.0 %collective-permute-start.19 = (bf16[2,4,128,512]{3,2,1,0:T(8,128)(2,1)}, bf16[2,4,128,512]{3,2,1,0:T(8,128)(2,1)}, u32[]{:S(2)}, u32[]{:S(2)}) collective-permute-start(bf16[2,4,128,512]{3,2,1,0:T(8,128)(2,1)} %collective-permute-done.17), channel_id=1, source_target_pairs={{0,1},{1,0},{2,3},{3,2},{4,5},{5,4},{6,7},{7,6},{8,9},{9,8},{10,11... | collective-permute-start | bytes 3145736 | tf_op jit(solution)/shard_map/ppermute | solution.py:1083
  172.1 38.0 %collective-permute-start.14 = (bf16[2,4,128,512]{3,2,1,0:T(8,128)(2,1)}, bf16[2,4,128,512]{3,2,1,0:T(8,128)(2,1)}, u32[]{:S(2)}, u32[]{:S(2)}) collective-permute-start(bf16[2,4,128,512]{3,2,1,0:T(8,128)(2,1)} %pad_maximum_fusion.1), channel_id=1, source_target_pairs={{0,1},{1,0},{2,3},{3,2},{4,5},{5,4},{6,7},{7,6},{8,9},{9,8},{10,11... | collective-permute-start | bytes 3145736 | tf_op jit(solution)/shard_map/ppermute | solution.py:1083
  172.6 37.4 %collective-permute-start.10 = (bf16[2,4,128,512]{3,2,1,0:T(8,128)(2,1)}, bf16[2,4,128,512]{3,2,1,0:T(8,128)(2,1)}, u32[]{:S(2)}, u32[]{:S(2)}) collective-permute-start(bf16[2,4,128,512]{3,2,1,0:T(8,128)(2,1)} %pad_maximum_fusion), channel_id=1, source_target_pairs={{0,1},{1,0},{2,3},{3,2},{4,5},{5,4},{6,7},{7,6},{8,9},{9,8},{10,11... | collective-permute-start | bytes 3145736 | tf_op jit(solution)/shard_map/ppermute | solution.py:1083
  187.5 22.6 %collective-permute-start.15 = (bf16[2,4,128,512]{3,2,1,0:T(8,128)(2,1)}, bf16[2,4,128,512]{3,2,1,0:T(8,128)(2,1)}, u32[]{:S(2)}, u32[]{:S(2)}) collective-permute-start(bf16[2,4,128,512]{3,2,1,0:T(8,128)(2,1)} %collective-permute-done.13), channel_id=1, source_target_pairs={{0,1},{1,0},{2,3},{3,2},{4,5},{5,4},{6,7},{7,6},{8,9},{9,8},{10,11... | collective-permute-start | bytes 3145736 | tf_op jit(solution)/shard_map/ppermute | solution.py:1083
  193.4 16.7 %collective-permute-start.11 = (bf16[2,4,128,512]{3,2,1,0:T(8,128)(2,1)}, bf16[2,4,128,512]{3,2,1,0:T(8,128)(2,1)}, u32[]{:S(2)}, u32[]{:S(2)}) collective-permute-start(bf16[2,4,128,512]{3,2,1,0:T(8,128)(2,1)} %collective-permute-done.9), channel_id=1, source_target_pairs={{0,1},{1,0},{2,3},{3,2},{4,5},{5,4},{6,7},{7,6},{8,9},{9,8},{10,11... | collective-permute-start | bytes 3145736 | tf_op jit(solution)/shard_map/ppermute | solution.py:1083
  240.9 5.9 %collective-permute-start.38 = (bf16[2,4,128,512]{3,2,1,0:T(8,128)(2,1)}, bf16[2,4,128,512]{3,2,1,0:T(8,128)(2,1)S(1)}, u32[]{:S(2)}, u32[]{:S(2)}) collective-permute-start(bf16[2,4,128,512]{3,2,1,0:T(8,128)(2,1)} %bitcast.209), channel_id=1, source_target_pairs={{0,1},{1,0},{2,3},{3,2},{4,5},{5,4},{6,7},{7,6},{8,9},{9,8},{10,11... | collective-permute-start | bytes 3145736 | tf_op jit(solution)/shard_map/ppermute | solution.py:1083
  244.7 25.3 %collective-permute-start.40 = (bf16[2,4,128,512]{3,2,1,0:T(8,128)(2,1)S(1)}, bf16[2,4,128,512]{3,2,1,0:T(8,128)(2,1)S(1)}, u32[]{:S(2)}, u32[]{:S(2)}) collective-permute-start(bf16[2,4,128,512]{3,2,1,0:T(8,128)(2,1)S(1)} %fusion.2), channel_id=1, source_target_pairs={{0,4},{1,5},{2,6},{3,7},{4,0},{5,1},{6,2},{7,3},{8,12},{9,13},{10,... | collective-permute-start | bytes 3145736 | tf_op jit(solution)/shard_map/ppermute | solution.py:1083
  245.6 26.4 %collective-permute-start.42 = (bf16[2,4,128,512]{3,2,1,0:T(8,128)(2,1)S(1)}, bf16[2,4,128,512]{3,2,1,0:T(8,128)(2,1)S(1)}, u32[]{:S(2)}, u32[]{:S(2)}) collective-permute-start(bf16[2,4,128,512]{3,2,1,0:T(8,128)(2,1)S(1)} %bitcast.208), channel_id=1, source_target_pairs={{0,1},{1,0},{2,3},{3,2},{4,5},{5,4},{6,7},{7,6},{8,9},{9,8},{10,11... | collective-permute-start | bytes 3145736 | tf_op jit(solution)/shard_map/ppermute | solution.py:1083
  246.0 26.1 %collective-permute-start.44 = (bf16[2,4,128,512]{3,2,1,0:T(8,128)(2,1)S(1)}, bf16[2,4,128,512]{3,2,1,0:T(8,128)(2,1)S(1)}, u32[]{:S(2)}, u32[]{:S(2)}) collective-permute-start(bf16[2,4,128,512]{3,2,1,0:T(8,128)(2,1)S(1)} %fusion), channel_id=1, source_target_pairs={{0,2},{1,3},{2,0},{3,1},{4,6},{5,7},{6,4},{7,5},{8,10},{9,11},{10,... | collective-permute-start | bytes 3145736 | tf_op jit(solution)/shard_map/ppermute | solution.py:1083
  246.6 46.3 %collective-permute-start.31 = (bf16[2,4,128,512]{3,2,1,0:T(8,128)(2,1)}, bf16[2,4,128,512]{3,2,1,0:T(8,128)(2,1)}, u32[]{:S(2)}, u32[]{:S(2)}) collective-permute-start(bf16[2,4,128,512]{3,2,1,0:T(8,128)(2,1)} %bitcast.49), channel_id=1, source_target_pairs={{0,1},{1,0},{2,3},{3,2},{4,5},{5,4},{6,7},{7,6},{8,9},{9,8},{10,11... | collective-permute-start | bytes 3145736 | tf_op jit(solution)/shard_map/ppermute | solution.py:1083
  271.3 13.6 %collective-permute-start.41 = (bf16[4,128,512]{2,1,0:T(8,128)(2,1)}, bf16[4,128,512]{2,1,0:T(8,128)(2,1)}, u32[]{:S(2)}, u32[]{:S(2)}) collective-permute-start(bf16[4,128,512]{2,1,0:T(8,128)(2,1)} %slice_bitcast_fusion.2), channel_id=1, source_target_pairs={{0,2},{1,3},{2,0},{3,1},{4,6},{5,7},{6,4},{7,5},{8,10},{9,11},{10,... | collective-permute-start | bytes 1572872 | tf_op jit(solution)/shard_map/ppermute | solution.py:1083
  273.3 13.5 %collective-permute-start.45 = (bf16[4,128,512]{2,1,0:T(8,128)(2,1)}, bf16[4,128,512]{2,1,0:T(8,128)(2,1)}, u32[]{:S(2)}, u32[]{:S(2)}) collective-permute-start(bf16[4,128,512]{2,1,0:T(8,128)(2,1)} %slice_bitcast_fusion), channel_id=1, source_target_pairs={{0,4},{1,5},{2,6},{3,7},{4,0},{5,1},{6,2},{7,3},{8,12},{9,13},{10,... | collective-permute-start | bytes 1572872 | tf_op jit(solution)/shard_map/ppermute | solution.py:1083
  274.1 15.0 %all-to-all-start.6 = ((f32[32,1,128]{2,1,0:T(1,128)}), f32[32,1,128]{2,1,0:T(1,128)S(1)}, u32[]{:S(2)}, u32[]{:S(2)}) async-start(f32[32,1,128]{2,1,0:T(1,128)} %get-tuple-element.88), calls=%async_computation.6 | async-start | bytes 32768 | tf_op jit(solution)/shard_map/all_to_all | solution.py:1091
  277.0 22.3 %collective-permute-start.30 = (bf16[2,4,128,512]{3,2,1,0:T(8,128)(2,1)}, bf16[2,4,128,512]{3,2,1,0:T(8,128)(2,1)}, u32[]{:S(2)}, u32[]{:S(2)}) collective-permute-start(bf16[2,4,128,512]{3,2,1,0:T(8,128)(2,1)} %bitcast.206), channel_id=1, source_target_pairs={{0,1},{1,0},{2,3},{3,2},{4,5},{5,4},{6,7},{7,6},{8,9},{9,8},{10,11... | collective-permute-start | bytes 3145736 | tf_op jit(solution)/shard_map/ppermute | solution.py:1083
  277.4 18.7 %collective-permute-start.35 = (bf16[2,4,128,512]{3,2,1,0:T(8,128)(2,1)}, bf16[2,4,128,512]{3,2,1,0:T(8,128)(2,1)}, u32[]{:S(2)}, u32[]{:S(2)}) collective-permute-start(bf16[2,4,128,512]{3,2,1,0:T(8,128)(2,1)} %bitcast.207), channel_id=1, source_target_pairs={{0,1},{1,0},{2,3},{3,2},{4,5},{5,4},{6,7},{7,6},{8,9},{9,8},{10,11... | collective-permute-start | bytes 3145736 | tf_op jit(solution)/shard_map/ppermute | solution.py:1083
  289.1 31.9 %all-to-all-start.5 = ((bf16[4,2,128,512]{3,2,1,0:T(8,128)(2,1)}), bf16[4,2,128,512]{3,2,1,0:T(8,128)(2,1)S(1)}, u32[]{:S(2)}, u32[]{:S(2)}) async-start(bf16[4,2,128,512]{3,2,1,0:T(8,128)(2,1)} %pad_maximum_fusion.5), calls=%async_computation.5 | async-start | bytes 2097152 | tf_op jit(solution)/shard_map/all_to_all | solution.py:1091
  294.8 23.5 %collective-permute-start.32 = (bf16[2,4,128,512]{3,2,1,0:T(8,128)(2,1)S(1)}, bf16[2,4,128,512]{3,2,1,0:T(8,128)(2,1)S(1)}, u32[]{:S(2)}, u32[]{:S(2)}) collective-permute-start(bf16[2,4,128,512]{3,2,1,0:T(8,128)(2,1)S(1)} %fusion.6), channel_id=1, source_target_pairs={{0,4},{1,5},{2,6},{3,7},{4,0},{5,1},{6,2},{7,3},{8,12},{9,13},{10,... | collective-permute-start | bytes 3145736 | tf_op jit(solution)/shard_map/ppermute | solution.py:1083
  296.1 39.3 %collective-permute-start.34 = (bf16[2,4,128,512]{3,2,1,0:T(8,128)(2,1)}, bf16[2,4,128,512]{3,2,1,0:T(8,128)(2,1)}, u32[]{:S(2)}, u32[]{:S(2)}) collective-permute-start(bf16[2,4,128,512]{3,2,1,0:T(8,128)(2,1)} %bitcast.54), channel_id=1, source_target_pairs={{0,1},{1,0},{2,3},{3,2},{4,5},{5,4},{6,7},{7,6},{8,9},{9,8},{10,11... | collective-permute-start | bytes 3145736 | tf_op jit(solution)/shard_map/ppermute | solution.py:1083
  298.6 36.8 %collective-permute-start.36 = (bf16[2,4,128,512]{3,2,1,0:T(8,128)(2,1)}, bf16[2,4,128,512]{3,2,1,0:T(8,128)(2,1)}, u32[]{:S(2)}, u32[]{:S(2)}) collective-permute-start(bf16[2,4,128,512]{3,2,1,0:T(8,128)(2,1)} %fusion.4), channel_id=1, source_target_pairs={{0,2},{1,3},{2,0},{3,1},{4,6},{5,7},{6,4},{7,5},{8,10},{9,11},{10,... | collective-permute-start | bytes 3145736 | tf_op jit(solution)/shard_map/ppermute | solution.py:1083
  334.5 14.4 %collective-permute-start.33 = (bf16[4,128,512]{2,1,0:T(8,128)(2,1)S(1)}, bf16[4,128,512]{2,1,0:T(8,128)(2,1)S(1)}, u32[]{:S(2)}, u32[]{:S(2)}) collective-permute-start(bf16[4,128,512]{2,1,0:T(8,128)(2,1)S(1)} %slice_bitcast_fusion.6), channel_id=1, source_target_pairs={{0,2},{1,3},{2,0},{3,1},{4,6},{5,7},{6,4},{7,5},{8,10},{9,11},{10,... | collective-permute-start | bytes 1572872 | tf_op jit(solution)/shard_map/ppermute | solution.py:1083
  337.5 11.6 %collective-permute-start.51 = (bf16[2,4,96,512]{3,2,1,0:T(8,128)(2,1)S(1)}, bf16[2,4,96,512]{3,2,1,0:T(8,128)(2,1)S(1)}, u32[]{:S(2)}, u32[]{:S(2)}) collective-permute-start(bf16[2,4,96,512]{3,2,1,0:T(8,128)(2,1)S(1)} %copy-done.61), channel_id=1, source_target_pairs={{0,1},{1,0},{2,3},{3,2},{4,5},{5,4},{6,7},{7,6},{8,9},{9,8},{10,11... | collective-permute-start | bytes 2359304 | tf_op jit(solution)/shard_map/ppermute | solution.py:1083
  337.8 14.9 %collective-permute-start.37 = (bf16[4,128,512]{2,1,0:T(8,128)(2,1)S(1)}, bf16[4,128,512]{2,1,0:T(8,128)(2,1)S(1)}, u32[]{:S(2)}, u32[]{:S(2)}) collective-permute-start(bf16[4,128,512]{2,1,0:T(8,128)(2,1)S(1)} %slice_bitcast_fusion.4), channel_id=1, source_target_pairs={{0,4},{1,5},{2,6},{3,7},{4,0},{5,1},{6,2},{7,3},{8,12},{9,13},{10,... | collective-permute-start | bytes 1572872 | tf_op jit(solution)/shard_map/ppermute | solution.py:1083
  339.0 19.9 %collective-permute-start.46 = (bf16[2,4,96,512]{3,2,1,0:T(8,128)(2,1)}, bf16[2,4,96,512]{3,2,1,0:T(8,128)(2,1)}, u32[]{:S(2)}, u32[]{:S(2)}) collective-permute-start(bf16[2,4,96,512]{3,2,1,0:T(8,128)(2,1)} %get-tuple-element.93), channel_id=1, source_target_pairs={{0,1},{1,0},{2,3},{3,2},{4,5},{5,4},{6,7},{7,6},{8,9},{9,8},{10,11... | collective-permute-start | bytes 2359304 | tf_op jit(solution)/shard_map/ppermute | solution.py:1083
  340.1 28.8 %collective-permute-start.48 = (bf16[2,4,96,512]{3,2,1,0:T(8,128)(2,1)}, bf16[2,4,96,512]{3,2,1,0:T(8,128)(2,1)}, u32[]{:S(2)}, u32[]{:S(2)}) collective-permute-start(bf16[2,4,96,512]{3,2,1,0:T(8,128)(2,1)} %add_convert_fusion.8), channel_id=1, source_target_pairs={{0,4},{1,5},{2,6},{3,7},{4,0},{5,1},{6,2},{7,3},{8,12},{9,13},{10,... | collective-permute-start | bytes 2359304 | tf_op jit(solution)/shard_map/ppermute | solution.py:1083
  349.0 22.9 %collective-permute-start.50 = (bf16[2,4,96,512]{3,2,1,0:T(8,128)(2,1)}, bf16[2,4,96,512]{3,2,1,0:T(8,128)(2,1)}, u32[]{:S(2)}, u32[]{:S(2)}) collective-permute-start(bf16[2,4,96,512]{3,2,1,0:T(8,128)(2,1)} %get-tuple-element.97), channel_id=1, source_target_pairs={{0,1},{1,0},{2,3},{3,2},{4,5},{5,4},{6,7},{7,6},{8,9},{9,8},{10,11... | collective-permute-start | bytes 2359304 | tf_op jit(solution)/shard_map/ppermute | solution.py:1083
  350.2 21.7 %collective-permute-start.52 = (bf16[2,4,96,512]{3,2,1,0:T(8,128)(2,1)}, bf16[2,4,96,512]{3,2,1,0:T(8,128)(2,1)}, u32[]{:S(2)}, u32[]{:S(2)}) collective-permute-start(bf16[2,4,96,512]{3,2,1,0:T(8,128)(2,1)} %add_convert_fusion.5), channel_id=1, source_target_pairs={{0,2},{1,3},{2,0},{3,1},{4,6},{5,7},{6,4},{7,5},{8,10},{9,11},{10,... | collective-permute-start | bytes 2359304 | tf_op jit(solution)/shard_map/ppermute | solution.py:1083
  353.9 29.3 %all-to-all-start.4 = ((bf16[4,2,128,512]{3,2,1,0:T(8,128)(2,1)}), bf16[4,2,128,512]{3,2,1,0:T(8,128)(2,1)}, u32[]{:S(2)}, u32[]{:S(2)}) async-start(bf16[4,2,128,512]{3,2,1,0:T(8,128)(2,1)} %pad_maximum_fusion.4), calls=%async_computation.4 | async-start | bytes 2097152 | tf_op jit(solution)/shard_map/all_to_all | solution.py:1091
  370.7 16.0 %collective-permute-start.49 = (bf16[4,96,512]{2,1,0:T(8,128)(2,1)S(1)}, bf16[4,96,512]{2,1,0:T(8,128)(2,1)}, u32[]{:S(2)}, u32[]{:S(2)}) collective-permute-start(bf16[4,96,512]{2,1,0:T(8,128)(2,1)S(1)} %slice_bitcast_fusion.18), channel_id=1, source_target_pairs={{0,2},{1,3},{2,0},{3,1},{4,6},{5,7},{6,4},{7,5},{8,10},{9,11},{10,... | collective-permute-start | bytes 1179656 | tf_op jit(solution)/shard_map/ppermute | solution.py:1083
  374.4 13.5 %collective-permute-start.53 = (bf16[4,96,512]{2,1,0:T(8,128)(2,1)}, bf16[4,96,512]{2,1,0:T(8,128)(2,1)}, u32[]{:S(2)}, u32[]{:S(2)}) collective-permute-start(bf16[4,96,512]{2,1,0:T(8,128)(2,1)} %slice_bitcast_fusion.16), channel_id=1, source_target_pairs={{0,4},{1,5},{2,6},{3,7},{4,0},{5,1},{6,2},{7,3},{8,12},{9,13},{10,... | collective-permute-start | bytes 1179656 | tf_op jit(solution)/shard_map/ppermute | solution.py:1083
  383.2 16.8 %all-to-all-start.7 = ((f32[32,1,3072]{2,1,0:T(1,128)}), f32[32,1,3072]{2,1,0:T(1,128)S(1)}, u32[]{:S(2)}, u32[]{:S(2)}) async-start(f32[32,1,3072]{2,1,0:T(1,128)} %all_to_all.37), calls=%async_computation.7 | async-start | bytes 786432 | tf_op jit(solution)/shard_map/all_to_all | solution.py:1091
  400.0 95.2 %all-to-all-start.8 = ((bf16[4,2,96,512]{3,2,1,0:T(8,128)(2,1)}), bf16[4,2,96,512]{3,2,1,0:T(8,128)(2,1)}, u32[]{:S(2)}, u32[]{:S(2)}) async-start(bf16[4,2,96,512]{3,2,1,0:T(8,128)(2,1)} %copy.37), calls=%async_computation.8 | async-start | bytes 1572864 | tf_op jit(solution)/shard_map/all_to_all | solution.py:1091
  404.2 33.2 %collective-permute-start.65 = (bf16[128,1024]{1,0:T(8,128)(2,1)S(1)}, bf16[128,1024]{1,0:T(8,128)(2,1)S(1)}, u32[]{:S(2)}, u32[]{:S(2)}) collective-permute-start(bf16[128,1024]{1,0:T(8,128)(2,1)S(1)} %copy-done.26), channel_id=1, source_target_pairs={{0,8},{8,0},{16,24},{24,16},{1,9},{9,1},{17,25},{25,17},{2,10},{10... | collective-permute-start | bytes 786440 | tf_op jit(solution)/shard_map/ppermute | solution.py:1087
  406.2 80.8 %collective-permute-start.62 = (bf16[256,1024]{1,0:T(8,128)(2,1)S(1)}, bf16[256,1024]{1,0:T(8,128)(2,1)S(1)}, u32[]{:S(2)}, u32[]{:S(2)}) collective-permute-start(bf16[256,1024]{1,0:T(8,128)(2,1)S(1)} %copy-done.22), channel_id=1, source_target_pairs={{0,8},{8,0},{16,24},{24,16},{1,9},{9,1},{17,25},{25,17},{2,10},{10... | collective-permute-start | bytes 1572872 | tf_op jit(solution)/shard_map/ppermute | solution.py:1087
  406.3 80.7 %collective-permute-start.63 = (bf16[256,1024]{1,0:T(8,128)(2,1)S(1)}, bf16[256,1024]{1,0:T(8,128)(2,1)S(1)}, u32[]{:S(2)}, u32[]{:S(2)}) collective-permute-start(bf16[256,1024]{1,0:T(8,128)(2,1)S(1)} %copy-done.20), channel_id=1, source_target_pairs={{0,16},{8,24},{16,0},{24,8},{1,17},{9,25},{17,1},{25,9},{2,18},{10... | collective-permute-start | bytes 1572872 | tf_op jit(solution)/shard_map/ppermute | solution.py:1087
  409.1 77.9 %collective-permute-start.64 = (bf16[256,1024]{1,0:T(8,128)(2,1)S(1)}, bf16[256,1024]{1,0:T(8,128)(2,1)S(1)}, u32[]{:S(2)}, u32[]{:S(2)}) collective-permute-start(bf16[256,1024]{1,0:T(8,128)(2,1)S(1)} %copy-done.18), channel_id=1, source_target_pairs={{0,24},{8,16},{16,8},{24,0},{1,25},{9,17},{17,9},{25,1},{2,26},{10... | collective-permute-start | bytes 1572872 | tf_op jit(solution)/shard_map/ppermute | solution.py:1087
  410.6 76.4 %collective-permute-start.66 = (bf16[128,1024]{1,0:T(8,128)(2,1)S(1)}, bf16[128,1024]{1,0:T(8,128)(2,1)S(1)}, u32[]{:S(2)}, u32[]{:S(2)}) collective-permute-start(bf16[128,1024]{1,0:T(8,128)(2,1)S(1)} %copy-done.24), channel_id=1, source_target_pairs={{0,16},{8,24},{16,0},{24,8},{1,17},{9,25},{17,1},{25,9},{2,18},{10... | collective-permute-start | bytes 786440 | tf_op jit(solution)/shard_map/ppermute | solution.py:1087
  437.4 49.5 %collective-permute-start.67 = (bf16[128,1024]{1,0:T(8,128)(2,1)S(1)}, bf16[128,1024]{1,0:T(8,128)(2,1)S(1)}, u32[]{:S(2)}, u32[]{:S(2)}) collective-permute-start(bf16[128,1024]{1,0:T(8,128)(2,1)S(1)} %get-tuple-element.111), channel_id=1, source_target_pairs={{0,24},{8,16},{16,8},{24,0},{1,25},{9,17},{17,9},{25,1},{2,26},{10... | collective-permute-start | bytes 786440 | tf_op jit(solution)/shard_map/ppermute | solution.py:1087
  502.4 5.9 %collective-permute-start.59 = (bf16[2,97,512]{2,1,0:T(8,128)(2,1)S(1)}, bf16[2,97,512]{2,1,0:T(8,128)(2,1)S(1)}, u32[]{:S(2)}, u32[]{:S(2)}) collective-permute-start(bf16[2,97,512]{2,1,0:T(8,128)(2,1)S(1)} %pad_maximum_fusion.12.refs_4_), channel_id=1, source_target_pairs={{0,2},{1,3},{2,0},{3,1},{4,6},{5,7},{6,4},{7,5},{8,10},{9,11},{10,... | collective-permute-start | bytes 595976 | tf_op jit(solution)/shard_map/ppermute | solution.py:1083
  503.5 5.8 %collective-permute-start.55 = (bf16[2,97,512]{2,1,0:T(8,128)(2,1)S(1)}, bf16[2,97,512]{2,1,0:T(8,128)(2,1)S(1)}, u32[]{:S(2)}, u32[]{:S(2)}) collective-permute-start(bf16[2,97,512]{2,1,0:T(8,128)(2,1)S(1)} %pad_maximum_fusion.11.refs_0_), channel_id=1, source_target_pairs={{0,4},{1,5},{2,6},{3,7},{4,0},{5,1},{6,2},{7,3},{8,12},{9,13},{10,... | collective-permute-start | bytes 595976 | tf_op jit(solution)/shard_map/ppermute | solution.py:1083
  (76 other events, 837.0 us)
where the time goes:
time: 521 us; the launch traced here: 517 us
  waiting for transfers between devices  279 us (54%)
  starting transfers between devices  78.9 us (15%)
  Pallas kernels  59.4 us (11%)
  blocking collectives  40 us (8%)
  other arithmetic  36 us (7%)
  local copies, waits for them, and re-layouts  21.2 us (4%)
    ppermute x56, waiting for transfers between devices, swap(): return lax.ppermute(array, EX, [(i, i ^ bit) for i in range(8)])  138 us
    ppermute x12, waiting for transfers between devices, trade(): return lax.ppermute(array, DP, [(i, i ^ step) for i in range(4)])  112 us
    all_to_all x2, blocking collectives, everyone(): return lax.all_to_all(array, axes, split_axis=0, concat_axis=0, tiled=True)  40 us
    ppermute x56, starting transfers between devices, swap(): return lax.ppermute(array, EX, [(i, i ^ bit) for i in range(8)])  32.2 us
    pallas_call x1, Pallas kernels, expert_call(): pl.pallas_call(expert_kernel, in_specs=[hbm] * 24 + [vmem] * 2, out_specs...  30.1 us
    all_to_all x7, waiting for transfers between devices, everyone(): return lax.all_to_all(array, axes, split_axis=0, concat_axis=0, tiled=True)  28.9 us
    all_to_all x7, starting transfers between devices, everyone(): return lax.all_to_all(array, axes, split_axis=0, concat_axis=0, tiled=True)  26.7 us
    ppermute x12, starting transfers between devices, trade(): return lax.ppermute(array, DP, [(i, i ^ step) for i in range(4)])  19.9 us
  transfers between devices with their start and end apart: 75, of which 32 were waited for; matrix products, arithmetic and copies ran while one was open for 9% of the time, Pallas kernels for 5%

commit v1 on v0

--- a/solution.py
+++ b/solution.py
@@ -362,11 +362,10 @@
 
 def expert_kernel(*refs):
     tok_a, tok_b, cot_a, cot_b = refs[0:4], refs[4:8], refs[8:12], refs[12:16]
-    up_pieces, down_pieces = refs[16:20], refs[20:24]
-    routes_ref, router_ref = refs[24:26]
-    mix_a, mix_b, back_a, back_b = refs[26:30], refs[30:34], refs[34:38], refs[38:42]
-    d_up_pieces, d_down_pieces = refs[42:46], refs[46:50]
-    dgate_ref = refs[50]
+    own_up, own_down, pieces = refs[16], refs[17], refs[18:21]
+    routes_ref, router_ref = refs[21:23]
+    mix_a, mix_b, back_a, back_b = refs[23:27], refs[27:31], refs[31:35], refs[35:39]
+    grad_pieces, dgate_ref = refs[39:43], refs[43]
     (
         tok_buf,
         cot_buf,
@@ -388,7 +387,7 @@
         out_sem,
         weight_sem,
         grad_sem,
-    ) = refs[51:]
+    ) = refs[44:]
     half = D // 2
     owner, group = lax.axis_index(EX), lax.axis_index(DP)
     expert = owner * 4 + group
@@ -424,8 +423,10 @@
         found = []
         for s in range(4):
             at = jnp.bitwise_xor(group, s)
-            up_from = up_pieces[s].at[group] if s == 0 else up_pieces[s]
-            down_from = down_pieces[s].at[group] if s == 0 else down_pieces[s]
+            up_from, down_from = own_up.at[group], own_down.at[group]
+            if s > 0:
+                up_from = pieces[s - 1].at[pl.ds(0, 256), :]
+                down_from = pieces[s - 1].at[pl.ds(256, 128), :]
             found.append(pltpu.make_async_copy(up_from, up_scr.at[at], weight_sem.at[0, s]))
             found.append(pltpu.make_async_copy(down_from, down_scr.at[at], weight_sem.at[1, s]))
         return found
@@ -591,8 +592,12 @@
 
     def grad_copies(s):
         return (
-            pltpu.make_async_copy(d_up_scr.at[s], d_up_pieces[s], grad_sem.at[0, s]),
-            pltpu.make_async_copy(d_down_scr.at[s], d_down_pieces[s], grad_sem.at[1, s]),
+            pltpu.make_async_copy(
+                d_up_scr.at[s], grad_pieces[s].at[pl.ds(0, 256), :], grad_sem.at[0, s]
+            ),
+            pltpu.make_async_copy(
+                d_down_scr.at[s], grad_pieces[s].at[pl.ds(256, 128), :], grad_sem.at[1, s]
+            ),
         )
 
     lax.fori_loop(0, 4, up_step, 0)
@@ -604,7 +609,7 @@
             copy.wait()
 
 
-def expert_call(tok_a, tok_b, cot_a, cot_b, up_pieces, down_pieces, routes, router):
+def expert_call(tok_a, tok_b, cot_a, cot_b, weights, routes, router):
     half = D // 2
     token_count = 1024
     hbm = pl.BlockSpec(memory_space=pltpu.HBM)
@@ -612,13 +617,14 @@
     slots = 32 * CAP
     b16 = jnp.bfloat16
     piece = jax.ShapeDtypeStruct((token_count, half), b16)
+    far = pltpu.HBM((token_count, half), b16)
     outs = pl.pallas_call(
         expert_kernel,
-        in_specs=[hbm] * 24 + [vmem] * 2,
-        out_specs=[hbm] * 24 + [vmem],
-        out_shape=[piece] * 16
-        + [jax.ShapeDtypeStruct((256, 2 * F), b16)] * 4
-        + [jax.ShapeDtypeStruct((128, D), b16)] * 4
+        in_specs=[hbm] * 21 + [vmem] * 2,
+        out_specs=[hbm] * 20 + [vmem],
+        out_shape=([piece] * 2 + [far] * 2) * 4
+        + [jax.ShapeDtypeStruct((384, D), b16)]
+        + [pltpu.HBM((384, D), b16)] * 3
         + [jax.ShapeDtypeStruct((32, 1, 128), jnp.float32)],
         scratch_shapes=[pltpu.VMEM((2, token_count, D), b16)] * 4
         + [
@@ -640,9 +646,9 @@
             pltpu.SemaphoreType.DMA((2, 4)),
         ],
         compiler_params=pltpu.CompilerParams(vmem_limit_bytes=48 * 1024 * 1024),
-    )(*tok_a, *tok_b, *cot_a, *cot_b, *up_pieces, *down_pieces, routes, router)
-    groups = [outs[4 * i : 4 * i + 4] for i in range(6)]
-    return (*groups, outs[24])
+    )(*tok_a, *tok_b, *cot_a, *cot_b, *weights, routes, router)
+    groups = [outs[4 * i : 4 * i + 4] for i in range(5)]
+    return (*groups, outs[20])
 
 
 def rope_constants(length):
@@ -687,6 +693,12 @@
     return copies
 
 
+def seen(seg_row, rows_at, cols_at):
+    row = seg_row.astype(jnp.float32)
+    column = jnp.sum(jnp.where(rows_at == cols_at, row, 0.0), axis=1, keepdims=True)
+    return (rows_at >= cols_at) & (column == row)
+
+
 def packed_views(pack_ref):
     starts = (0, D, 2 * D, 2 * D + D // 2, 3 * D, 4 * D)
     return [pack_ref.at[:, pl.ds(a, b - a)] for a, b in zip(starts[:-1], starts[1:])]
@@ -694,12 +706,18 @@
 
 def attention_forward_kernel(*refs):
     pieces_a, pieces_b = refs[0:4], refs[4:8]
-    x_ref, seg_row, seg_col, gain_ref, rope_ref = refs[8:13]
-    finals = refs[13:17]
-    pack_ref, hidden_ref, small_ref, normed2_ref, whole, sems, out_sems = refs[17:]
+    arrays, finals, buffers = refs[8:13], refs[13:17], refs[17:22]
+    x_ref, seg_row, gain1_ref, gain2_ref, rope_ref = buffers
+    pack_ref, hidden_ref, small_ref, normed2_ref, whole, sems, out_sems, load_sems = refs[22:]
+    loads = [
+        pltpu.make_async_copy(there, here, load_sems.at[i])
+        for i, (there, here) in enumerate(zip(arrays, buffers))
+    ]
+    for load in loads:
+        load.start()
     outs = [
         pltpu.make_async_copy(here, there, out_sems.at[i])
-        for i, (here, there) in enumerate(zip(refs[17:21], finals))
+        for i, (here, there) in enumerate(zip(refs[22:26], finals))
     ]
     normed_ref, q_ref, k_ref, v_ref, att_ref = packed_views(pack_ref)
     owner = lax.axis_index(EX)
@@ -707,12 +725,13 @@
     for kind in range(3):
         for copy in weight_copies(pieces_a, pieces_b, whole, sems, owner, kind, False):
             copy.start()
+    for load in loads:
+        load.wait()
     inputs = x_ref[...].astype(jnp.float32)
     inverse = lax.rsqrt(jnp.mean(inputs * inputs, axis=1, keepdims=True) + epsilon)
-    normed = (inputs * inverse * gain_ref[0:1, :]).astype(jnp.bfloat16)
+    normed = (inputs * inverse * gain1_ref[...]).astype(jnp.bfloat16)
     normed_ref[...] = normed
     small_ref[:128, 8:9] = inverse
-    small_ref[:128, 10:11] = seg_col[...].astype(jnp.float32)
     cosine, signed = rope_ref[0], rope_ref[1]
     for kind in range(2):
         for copy in weight_copies(pieces_a, pieces_b, whole, sems, owner, kind, False):
@@ -728,7 +747,7 @@
     v_ref[...] = keyval[:, half:].astype(jnp.bfloat16)
     rows_at = lax.broadcasted_iota(jnp.int32, (128, 128), 0)
     cols_at = lax.broadcasted_iota(jnp.int32, (128, 128), 1)
-    visible = (rows_at >= cols_at) & (seg_col[...] == seg_row[...])
+    visible = seen(seg_row[...], rows_at, cols_at)
     visible2 = jnp.concatenate([visible, visible], axis=0)
     low = cols_at < 64
     for head in range(KV_HEADS):
@@ -755,7 +774,7 @@
         att_ref[...], whole[2].reshape(D, D), preferred_element_type=jnp.float32
     )
     inverse2 = lax.rsqrt(jnp.mean(hidden * hidden, axis=1, keepdims=True) + epsilon)
-    normed2 = (hidden * inverse2 * gain_ref[1:2, :]).astype(jnp.bfloat16)
+    normed2 = (hidden * inverse2 * gain2_ref[...]).astype(jnp.bfloat16)
     hidden_ref[...] = hidden
     small_ref[:128, 9:10] = inverse2
     outs[1].start()
@@ -768,9 +787,8 @@
         out.wait()
 
 
-def attention_forward(pieces_a, pieces_b, x, seg, gains, rope):
+def attention_forward(pieces_a, pieces_b, *rest):
     hbm = pl.BlockSpec(memory_space=pltpu.HBM)
-    vmem = pl.BlockSpec(memory_space=pltpu.VMEM)
     f32, b16 = jnp.float32, jnp.bfloat16
     shapes = [
         ((128, 4 * D), b16),
@@ -780,29 +798,32 @@
     ]
     return pl.pallas_call(
         attention_forward_kernel,
-        in_specs=[hbm] * 8 + [vmem] * 5,
+        in_specs=[hbm] * (8 + len(rest)),
         out_specs=[hbm] * 4,
         out_shape=[pltpu.HBM(s, t) for s, t in shapes],
-        scratch_shapes=[pltpu.VMEM(s, t) for s, t in shapes]
+        scratch_shapes=[pltpu.VMEM(array.shape, array.dtype) for array in rest]
+        + [pltpu.VMEM(s, t) for s, t in shapes]
         + [
             pltpu.VMEM((3, 4, 8, 32, D), b16),
             pltpu.SemaphoreType.DMA((3, 8, 2)),
             pltpu.SemaphoreType.DMA((4,)),
+            pltpu.SemaphoreType.DMA((len(rest),)),
         ],
         compiler_params=pltpu.CompilerParams(vmem_limit_bytes=40 * 1024 * 1024),
-    )(*pieces_a, *pieces_b, x, seg[None, :], seg[:, None], gains, rope)
+    )(*pieces_a, *pieces_b, *rest)
 
 
 def attention_backward_kernel(*refs):
     pieces_a, pieces_b = refs[0:4], refs[4:8]
-    arrays = refs[8:20]
-    grads_a, grads_b = refs[20:24], refs[24:28]
-    finals = refs[28:31]
-    buffers = refs[31:43]
+    arrays = refs[8:21]
+    grads_a, grads_b = refs[21:25], refs[25:29]
+    finals = refs[29:32]
+    buffers = refs[32:45]
     (
         x_ref,
         seg_row,
-        gain_ref,
+        gain1_ref,
+        gain2_ref,
         rope_ref,
         pack_ref,
         hidden_ref,
@@ -813,15 +834,15 @@
         routes_ref,
         router_ref,
     ) = buffers
-    input_grad_ref, gains_ref, router_grad_ref = refs[43:46]
-    whole, grad, datt_scr, dq_scr, dkv_scr, sems, out_sems, load_sems, last_sems = refs[46:]
+    input_grad_ref, gains_ref, router_grad_ref = refs[45:48]
+    whole, grad, datt_scr, dq_scr, dkv_scr, sems, out_sems, load_sems, last_sems = refs[48:]
     loads = [
         pltpu.make_async_copy(there, here, load_sems.at[i])
         for i, (there, here) in enumerate(zip(arrays, buffers))
     ]
     lasts = [
         pltpu.make_async_copy(here, there, last_sems.at[i])
-        for i, (here, there) in enumerate(zip(refs[43:46], finals))
+        for i, (here, there) in enumerate(zip(refs[45:48], finals))
     ]
     for load in loads:
         load.start()
@@ -834,7 +855,7 @@
     for load in loads:
         load.wait()
     hidden, inverse2 = hidden_ref[...], small_ref[:128, 9:10]
-    normed2 = (hidden * inverse2 * gain_ref[1:2, :]).astype(jnp.bfloat16)
+    normed2 = (hidden * inverse2 * gain2_ref[...]).astype(jnp.bfloat16)
     names = lax.broadcasted_iota(jnp.int32, (EXPERTS, 128), 0)
     routes = routes_ref[...]
     named = routes[0:1] == names
@@ -858,7 +879,7 @@
         d_logits, router_ref[...], (((0,), (0,)), ((), ())), preferred_element_type=jnp.float32
     )
     gains_ref[1:2, :] = jnp.sum(d_normed2 * hidden * inverse2, axis=0, keepdims=True)
-    weighted = d_normed2 * gain_ref[1:2, :]
+    weighted = d_normed2 * gain2_ref[...]
     d_hidden = (
         dout_ref[...].astype(jnp.float32)
         + inverse2 * weighted
@@ -887,9 +908,7 @@
     cosine, signed = rope_ref[0], -rope_ref[1]
     rows_at = lax.broadcasted_iota(jnp.int32, (128, 128), 0)
     cols_at = lax.broadcasted_iota(jnp.int32, (128, 128), 1)
-    visible = (rows_at >= cols_at) & (
-        small_ref[:128, 10:11] == seg_row[...].astype(jnp.float32)
-    )
+    visible = seen(seg_row[...], rows_at, cols_at)
     visible2 = jnp.concatenate([visible, visible], axis=0)
     low = cols_at < 64
     keep_k = keep_v = None
@@ -950,7 +969,7 @@
     )
     inputs, inverse = x_ref[...].astype(jnp.float32), small_ref[:128, 8:9]
     gains_ref[0:1, :] = jnp.sum(d_normed * inputs * inverse, axis=0, keepdims=True)
-    weighted = d_normed * gain_ref[0:1, :]
+    weighted = d_normed * gain1_ref[...]
     input_grad_ref[...] = (
         d_hidden
         + inverse * weighted
@@ -971,12 +990,13 @@
     hbm = pl.BlockSpec(memory_space=pltpu.HBM)
     f32, b16 = jnp.float32, jnp.bfloat16
     piece = jax.ShapeDtypeStruct((2, 4, 96, D // 2), b16)
+    far = pltpu.HBM((2, 4, 96, D // 2), b16)
     shapes = [((128, D), b16), ((2, D), f32), ((EXPERTS, D), f32)]
     outs = pl.pallas_call(
         attention_backward_kernel,
         in_specs=[hbm] * (8 + len(rest)),
         out_specs=[hbm] * 11,
-        out_shape=[piece] * 8 + [jax.ShapeDtypeStruct(*pair) for pair in shapes],
+        out_shape=([piece] * 2 + [far] * 2) * 2 + [pltpu.HBM(*pair) for pair in shapes],
         scratch_shapes=[pltpu.VMEM(array.shape, array.dtype) for array in rest]
         + [pltpu.VMEM(*pair) for pair in shapes]
         + [
@@ -996,58 +1016,56 @@
 
 
 def slice_kernel(*refs):
-    weights, outs, buffers, sems = refs[0:2], refs[2:8], refs[8:14], refs[14]
+    weights, outs, buffers, sems = refs[0:2], refs[2:5], refs[5:8], refs[8]
     group = lax.axis_index(DP)
     loads, stores = [], []
-    for i, weight in enumerate(weights):
-        for s in range(1, 4):
-            j = 3 * i + s - 1
-            source = weight.at[jnp.bitwise_xor(group, s)]
-            loads.append(pltpu.make_async_copy(source, buffers[j], sems.at[0, j]))
-            stores.append(pltpu.make_async_copy(buffers[j], outs[j], sems.at[1, j]))
+    for s in range(3):
+        at = jnp.bitwise_xor(group, s + 1)
+        for i, rows in enumerate((pl.ds(0, 256), pl.ds(256, 128))):
+            loads.append(
+                pltpu.make_async_copy(weights[i].at[at], buffers[s].at[rows, :], sems.at[i, s])
+            )
+        stores.append(pltpu.make_async_copy(buffers[s], outs[s], sems.at[2, s]))
     for load in loads:
         load.start()
-    for load, store in zip(loads, stores):
-        load.wait()
-        store.start()
+    for s in range(3):
+        loads[2 * s].wait()
+        loads[2 * s + 1].wait()
+        stores[s].start()
     for store in stores:
         store.wait()
 
 
 def sliced(up, down):
     hbm = pl.BlockSpec(memory_space=pltpu.HBM)
-    outs = pl.pallas_call(
+    return pl.pallas_call(
         slice_kernel,
         in_specs=[hbm] * 2,
-        out_specs=[hbm] * 6,
-        out_shape=[jax.ShapeDtypeStruct(up.shape[1:], up.dtype)] * 3
-        + [jax.ShapeDtypeStruct(down.shape[1:], down.dtype)] * 3,
-        scratch_shapes=[pltpu.VMEM(up.shape[1:], up.dtype)] * 3
-        + [pltpu.VMEM(down.shape[1:], down.dtype)] * 3
-        + [pltpu.SemaphoreType.DMA((2, 6))],
+        out_specs=[hbm] * 3,
+        out_shape=[pltpu.HBM((384, D), up.dtype)] * 3,
+        scratch_shapes=[pltpu.VMEM((384, D), up.dtype)] * 3 + [pltpu.SemaphoreType.DMA((3, 3))],
     )(up, down)
-    return outs[:3], outs[3:]
 
 
 def finish_experts_kernel(*refs):
-    up, down, up_out, down_out = refs[0:4], refs[4:8], refs[8], refs[9]
+    pieces, up_out, down_out = refs[0:4], refs[4], refs[5]
     for s in range(4):
         at = jnp.bitwise_xor(lax.axis_index(DP), s)
-        up_out[at] = up[s][...].astype(jnp.float32)
-        down_out[at] = down[s][...].astype(jnp.float32)
-
-
-def finish_experts(up, down):
+        up_out[at] = pieces[s][0:256, :].astype(jnp.float32)
+        down_out[at] = pieces[s][256:384, :].astype(jnp.float32)
+
+
+def finish_experts(pieces):
     vmem = pl.BlockSpec(memory_space=pltpu.VMEM)
     return pl.pallas_call(
         finish_experts_kernel,
-        in_specs=[vmem] * 8,
+        in_specs=[vmem] * 4,
         out_specs=[vmem] * 2,
         out_shape=[
             jax.ShapeDtypeStruct((4, 256, 2 * F), jnp.float32),
             jax.ShapeDtypeStruct((4, 128, D), jnp.float32),
         ],
-    )(*up, *down)
+    )(*pieces)
 
 
 def finish_weights_kernel(*refs):
@@ -1095,9 +1113,23 @@
     return everyone(jnp.broadcast_to(array[None], (count,) + array.shape), axes)
 
 
-def gather_halves(halves):
-    column = everyone(halves, DP)
+def gather_halves(copies):
+    column = everyone(copies, DP)
     return gather_plane(column[:, 0], column[:, 1])
+
+
+def gather_traded(halves):
+    traded = [halves] + [trade(halves, s) for s in range(1, 4)]
+    here = lax.axis_index(DP)
+
+    def at(place, column):
+        picked = traded[3 ^ place][column]
+        for z in range(2, -1, -1):
+            picked = jnp.where(here == z, traded[z ^ place][column], picked)
+        return picked
+
+    a0, b0 = (jnp.stack([at(place, column) for place in range(4)]) for column in range(2))
+    return gather_plane(a0, b0)
 
 
 def gather_plane(a0, b0):
@@ -1120,9 +1152,9 @@
     b_near = add(pieces_b[0], swap(pieces_b[2], CORE))
     a = add(a_near, swap(a_far, ALONG))
     b = add(b_near, swap(b_far, ACROSS))
-    a_own = add(a[0], swap(a[1], ACROSS))
-    b_own = add(b[0], swap(b[1], ALONG))
-    return everyone(jnp.stack([a_own, b_own], axis=1), DP)
+    a_end, b_end = swap(a[1], ACROSS), swap(b[1], ALONG)
+    a_own, b_own = add(a[0], a_end), add(b[0], b_end)
+    return a_own, b_own
 
 
 def block_inner(
@@ -1156,33 +1188,32 @@
     )
     small = to_group(small, (EX, DP), 32)
     all_routes = small[:, 0].astype(jnp.int32).reshape(32, TOPK, 128)
-    router = small[:, 1].reshape(8, 4, EXPERTS, 32).transpose(2, 1, 0, 3).reshape(EXPERTS, D)
-
-    def exchange(pieces):
-        return [pieces[0]] + [trade(pieces[s], s) for s in range(1, 4)]
-
-    up_sent, down_sent = sliced(w_gate_up, w_down)
-    up_pieces, down_pieces = exchange([w_gate_up, *up_sent]), exchange([w_down, *down_sent])
-    cot_a, cot_b = gather_halves(jnp.broadcast_to(split(out_cotangent)[None], (4, 2, 128, half)))
-
+    router = small[:, 1].reshape(8, 4, EXPERTS, 32).transpose(2, 1, 0, 3)
+    router = router.reshape(EXPERTS, D)
+
+    sent = sliced(w_gate_up, w_down)
+    weights = [w_gate_up, w_down] + [trade(sent[s - 1], s) for s in range(1, 4)]
+    cot_a, cot_b = gather_traded(split(out_cotangent))
+
+    def in_hbm(pieces):
+        return [pltpu.with_memory_space_constraint(p, pltpu.HBM) for p in pieces]
+
+    weights_a, weights_b = in_hbm(weights_a), in_hbm(weights_b)
     rope = jnp.asarray(np.stack(rope_constants(128)))
-    gains = jnp.stack([first_gain, second_gain])
-    saved = attention_forward(
-        weights_a, weights_b, layer_input, segment_ids, gains, rope
-    )
+    shared = (segment_ids[None, :], first_gain[None, :], second_gain[None, :], rope)
+    saved = attention_forward(weights_a, weights_b, layer_input, *shared)
     packed, hidden, scalars, normed2 = saved
     tok_a, tok_b = gather_halves(normed2)
 
     def flat(pieces):
         return [p.reshape(1024, half) for p in pieces]
 
-    mix_a, mix_b, back_a, back_b, d_up, d_down, d_gate = expert_call(
+    mix_a, mix_b, back_a, back_b, d_experts, d_gate = expert_call(
         flat(tok_a),
         flat(tok_b),
         flat(cot_a),
         flat(cot_b),
-        up_pieces,
-        down_pieces,
+        weights,
         all_routes,
         router,
     )
@@ -1190,15 +1221,13 @@
     def deep(pieces):
         return [p.reshape(2, 4, 128, half) for p in pieces]
 
-    back = scatter_halves(deep(back_a), deep(back_b))
+    back = everyone(jnp.stack(scatter_halves(deep(back_a), deep(back_b)), axis=1), DP)
     d_gates = everyone(d_gate, (EX, DP)).reshape(EXPERTS, 128)
     grads_a, grads_b, input_grad, d_gains, d_router = attention_backward(
         weights_a,
         weights_b,
         layer_input,
-        segment_ids[None, :],
-        gains,
-        rope,
+        *shared,
         packed,
         hidden,
         scalars,
@@ -1208,9 +1237,19 @@
         routes,
         router,
     )
-    d_up, d_down = exchange(d_up), exchange(d_down)
-    gate_up_grad, down_grad = finish_experts(d_up, d_down)
-    mixed = jnp.sum(scatter_halves(deep(mix_a), deep(mix_b)).astype(jnp.float32), axis=0)
+    arrived = [d_experts[0]] + [trade(d_experts[s], s) for s in range(1, 4)]
+    gate_up_grad, down_grad = finish_experts(arrived)
+    mix_near = scatter_halves(deep(mix_a), deep(mix_b))
+    group_at = lax.axis_index(DP)
+
+    def part_for(step):
+        at = jnp.bitwise_xor(group_at, step)
+        pair = [lax.dynamic_index_in_dim(own, at, 0, keepdims=False) for own in mix_near]
+        return jnp.stack(pair)
+
+    mixed = part_for(0).astype(jnp.float32)
+    for step in range(1, 4):
+        mixed = mixed + trade(part_for(step), step).astype(jnp.float32)
     mixed = jnp.concatenate([mixed[0], mixed[1]], axis=1)
     layer_output = (hidden + residual_scale * mixed).astype(jnp.bfloat16)
 
@@ -1224,7 +1263,9 @@
     small = jnp.sum(everyone(small, (DP, EX)), axis=0)
     first_gain_grad, second_gain_grad = small[:D], small[D : 2 * D]
 
-    summed = jnp.sum(scatter_halves(grads_a, grads_b).astype(jnp.float32), axis=0)
+    summed = jnp.stack(scatter_halves(grads_a, grads_b), axis=1)
+    summed = everyone(summed, DP)
+    summed = jnp.sum(summed.astype(jnp.float32), axis=0)
     summed = jnp.concatenate([summed, small[2 * D :].reshape(2, 1, half)], axis=1)
     summed = summed.astype(jnp.bfloat16)
     whole_a, whole_b = gather_plane(summed[0], summed[1])

time: 521 us -> 538 us (1.033)
  waiting for transfers between devices: 279 us -> 287 us
    ppermute x12, waiting for transfers between devices: 112 us -> 137 us  [trade(): return lax.ppermute(array, DP, [(i, i ^ step) for i in range(4)])]
    all_to_all x7 -> x5, waiting for transfers between devices: 28.9 us -> 4.56 us  [everyone(): return lax.all_to_all(array, axes, split_axis=0, concat_axis=0, tiled=True)]
    all_to_all x7 -> x5, starting transfers between devices: 26.7 us -> 20.1 us  [everyone(): return lax.all_to_all(array, axes, split_axis=0, concat_axis=0, tiled=True)]
    ppermute x56, waiting for transfers between devices: 138 us -> 144 us  [swap(): return lax.ppermute(array, EX, [(i, i ^ bit) for i in range(8)])]
    ppermute x12, starting transfers between devices: 19.9 us -> 25.7 us  [trade(): return lax.ppermute(array, DP, [(i, i ^ step) for i in range(4)])]
    convert_element_type x12 -> x14, other arithmetic: 17.5 us -> 23.2 us  [add(): (one.astype(jnp.float32) + two.astype(jnp.float32)).astype(jnp.bfloat16)]
  transfers between devices with their start and end apart: 75 -> 73, of which waited for: 32 -> 33; matrix products, arithmetic and copies ran while one was open for 9% -> 9% of each run, Pallas kernels for 5% -> 4%
where the time goes in v1:
time: 538 us; the launch traced here: 534 us
  waiting for transfers between devices  287 us (53%)
  starting transfers between devices  81.5 us (15%)
  Pallas kernels  60.7 us (11%)
  blocking collectives  44.7 us (8%)
  other arithmetic  38.9 us (7%)
  local copies, waits for them, and re-layouts  19.8 us (4%)
    ppermute x56, waiting for transfers between devices, swap(): return lax.ppermute(array, EX, [(i, i ^ bit) for i in range(8)])  144 us
    ppermute x12, waiting for transfers between devices, trade(): return lax.ppermute(array, DP, [(i, i ^ step) for i in range(4)])  137 us
    all_to_all x2, blocking collectives, everyone(): return lax.all_to_all(array, axes, split_axis=0, concat_axis=0, tiled=True)  44.7 us
    ppermute x56, starting transfers between devices, swap(): return lax.ppermute(array, EX, [(i, i ^ bit) for i in range(8)])  35.6 us
    pallas_call x1, Pallas kernels, expert_call(): pl.pallas_call(expert_kernel, in_specs=[hbm] * 21 + [vmem] * 2, out_specs...  31 us
    ppermute x12, starting transfers between devices, trade(): return lax.ppermute(array, DP, [(i, i ^ step) for i in range(4)])  25.7 us
    convert_element_type x14, other arithmetic, add(): (one.astype(jnp.float32) + two.astype(jnp.float32)).astype(jnp.bfloat16)  23.2 us
    all_to_all x5, starting transfers between devices, everyone(): return lax.all_to_all(array, axes, split_axis=0, concat_axis=0, tiled=True)  20.1 us
  transfers between devices with their start and end apart: 73, of which 33 were waited for; matrix products, arithmetic and copies ran while one was open for 9% of the time, Pallas kernels for 4%

profile of v1, /device:TPU:0, one launch (start us, length us, event | category | flops | bytes accessed | tf_op | source)
XLA Modules:
  0.0 533.8 jit_solution(16579398140130121289)
XLA Ops:
  2.7 26.3 %all_to_all.39 = bf16[4,2,96,512]{3,2,1,0:T(8,128)(2,1)S(1)} all-to-all(bf16[4,2,96,512]{3,2,1,0:T(8,128)(2,1)S(1)} %broadcast_in_dim.28), channel_id=1, replica_groups=mesh['dp'=4,'expert'=8] {'dp'}, dimensions={0} | all-to-all | bytes 1572864 | tf_op jit(solution)/shard_map/all_to_all | solution.py:1109
  29.2 1.6 collective-permute-start.4
  32.3 6.8 %collective-permute-done.4 = bf16[4,96,512]{2,1,0:T(8,128)(2,1)S(1)} collective-permute-done((bf16[4,96,512]{2,1,0:T(8,128)(2,1)S(1)}, bf16[4,96,512]{2,1,0:T(8,128)(2,1)S(1)}, u32[]{:S(2)}, u32[]{:S(2)}) %collective-permute-start.4) | collective-permute-done | bytes 393248 | tf_op jit(solution)/shard_map/ppermute | solution.py:1101
  39.1 1.6 collective-permute-start.5
  42.9 14.3 %collective-permute-done.5.refs_5_ = bf16[2,4,96,512]{3,2,1,0:T(8,128)(2,1)S(1)} collective-permute-done((bf16[2,4,96,512]{3,2,1,0:T(8,128)(2,1)S(1)}, bf16[2,4,96,512]{3,2,1,0:T(8,128)(2,1)S(1)}, u32[]{:S(2)}, u32[]{:S(2)}) %collective-permute-start.5) | collective-permute-done | bytes 786464 | tf_op jit(solution)/shard_map/ppermute | solution.py:1101
  61.5 6.9 %shard_map.204 = (bf16[128,4096]{1,0:T(8,128)(2,1)}, f32[128,1024]{1,0:T(8,128)}, f32[256,16]{1,0:T(8,128)}, bf16[4,2,128,512]{3,2,1,0:T(8,128)(2,1)}) custom-call(bf16[2,4,96,512]{3,2,1,0:T(8,128)(2,1)} %copy-done.26, bf16[2,4,96,512]{3,2,1,0:T(8,128)(2,1)} %copy-done.32, bf16[2,4,96,512]{3,2,1,0:T(8,128)(2,1)} %copy-done.34, ...), custom_call_target="tpu_custom_call" | custom-call | tf_op jit(solution)/shard_map/pallas_call | solution.py:799
  68.4 3.8 all-to-all-start.1
  72.3 2.1 collective-permute-start.16
  74.4 2.4 collective-permute-start.17
  76.9 19.2 %collective-permute-done.16 = bf16[2,128,512]{2,1,0:T(8,128)(2,1)S(1)} collective-permute-done((bf16[2,128,512]{2,1,0:T(8,128)(2,1)S(1)}, bf16[2,128,512]{2,1,0:T(8,128)(2,1)S(1)}, u32[]{:S(2)}, u32[]{:S(2)}) %collective-permute-start.16) | collective-permute-done | bytes 262176 | tf_op jit(solution)/shard_map/ppermute | solution.py:1105
  96.1 20.2 %collective-permute-done.17 = bf16[2,128,512]{2,1,0:T(8,128)(2,1)S(1)} collective-permute-done((bf16[2,128,512]{2,1,0:T(8,128)(2,1)S(1)}, bf16[2,128,512]{2,1,0:T(8,128)(2,1)S(1)}, u32[]{:S(2)}, u32[]{:S(2)}) %collective-permute-start.17) | collective-permute-done | bytes 262176 | tf_op jit(solution)/shard_map/ppermute | solution.py:1105
  122.2 9.3 %collective-permute-done.23 = bf16[4,128,512]{2,1,0:T(8,128)(2,1)} collective-permute-done((bf16[4,128,512]{2,1,0:T(8,128)(2,1)S(1)}, bf16[4,128,512]{2,1,0:T(8,128)(2,1)}, u32[]{:S(2)}, u32[]{:S(2)}) %collective-permute-start.23) | collective-permute-done | bytes 524320 | tf_op jit(solution)/shard_map/ppermute | solution.py:1101
  131.4 2.1 pad_maximum_fusion.3
  134.9 2.1 pad_maximum_fusion.2
  138.3 2.6 shard_map.205
  140.9 5.2 collective-permute-start.27
  147.0 1.6 collective-permute-start.28
  148.6 2.4 collective-permute-start.29
  150.9 2.3 pad_maximum_fusion.1
  153.2 2.1 pad_maximum_fusion
  155.3 18.2 %collective-permute-done.27.refs_18_ = bf16[384,1024]{1,0:T(8,128)(2,1)S(1)} collective-permute-done((bf16[384,1024]{1,0:T(8,128)(2,1)}, bf16[384,1024]{1,0:T(8,128)(2,1)S(1)}, u32[]{:S(2)}, u32[]{:S(2)}) %collective-permute-start.27) | collective-permute-done | bytes 786464 | tf_op jit(solution)/shard_map/ppermute | solution.py:1105
  173.5 28.7 %collective-permute-done.28.refs_19_ = bf16[384,1024]{1,0:T(8,128)(2,1)S(1)} collective-permute-done((bf16[384,1024]{1,0:T(8,128)(2,1)}, bf16[384,1024]{1,0:T(8,128)(2,1)S(1)}, u32[]{:S(2)}, u32[]{:S(2)}) %collective-permute-start.28) | collective-permute-done | bytes 786464 | tf_op jit(solution)/shard_map/ppermute | solution.py:1105
  206.8 21.3 %collective-permute-done.13 = bf16[2,4,128,512]{3,2,1,0:T(8,128)(2,1)} collective-permute-done((bf16[2,4,128,512]{3,2,1,0:T(8,128)(2,1)}, bf16[2,4,128,512]{3,2,1,0:T(8,128)(2,1)}, u32[]{:S(2)}, u32[]{:S(2)}) %collective-permute-start.13) | collective-permute-done | bytes 1048608 | tf_op jit(solution)/shard_map/ppermute | solution.py:1101
  229.0 18.5 %all_to_all.40 = bf16[32,2,1024]{2,1,0:T(2,128)(2,1)S(1)} all-to-all(bf16[32,2,1024]{2,1,0:T(2,128)(2,1)S(1)} %broadcast_in_dim.32), channel_id=1, replica_groups=mesh['dp'=4,'expert'=8] {'expert','dp'}, dimensions={0} | all-to-all | bytes 262144 | tf_op jit(solution)/shard_map/all_to_all | solution.py:1109
  250.8 31.0 %shard_map.206 = (bf16[1024,512]{1,0:T(8,128)(2,1)S(1)}, bf16[1024,512]{1,0:T(8,128)(2,1)S(1)}, bf16[1024,512]{1,0:T(8,128)(2,1)}, bf16[1024,512]{1,0:T(8,128)(2...) custom-call(bf16[1024,512]{1,0:T(8,128)(2,1)} %bitcast.14.refs_0_, ...), custom_call_target="tpu_custom_call" | custom-call | tf_op jit(solution)/shard_map/pallas_call | solution.py:621
  282.5 2.3 collective-permute-done.42
  288.3 23.3 %collective-permute-done.43 = bf16[2,4,128,512]{3,2,1,0:T(8,128)(2,1)S(1)} collective-permute-done((bf16[2,4,128,512]{3,2,1,0:T(8,128)(2,1)S(1)}, bf16[2,4,128,512]{3,2,1,0:T(8,128)(2,1)S(1)}, u32[]{:S(2)}, u32[]{:S(2)}) %collective-permute-start.43) | collective-permute-done | bytes 1048608 | tf_op jit(solution)/shard_map/ppermute | solution.py:1101
  315.1 1.9 slice_bitcast_fusion
  317.6 3.1 all-to-all-start.4
  321.1 5.3 collective-permute-done.44
  327.6 2.8 collective-permute-done.48
  332.8 4.5 all-to-all-start.3
  337.3 2.6 fusion.6
  341.1 2.5 fusion.4
  344.3 1.7 collective-permute-start.65
  346.1 17.4 %collective-permute-done.32 = bf16[2,4,128,512]{3,2,1,0:T(8,128)(2,1)} collective-permute-done((bf16[2,4,128,512]{3,2,1,0:T(8,128)(2,1)}, bf16[2,4,128,512]{3,2,1,0:T(8,128)(2,1)}, u32[]{:S(2)}, u32[]{:S(2)}) %collective-permute-start.32) | collective-permute-done | bytes 1048608 | tf_op jit(solution)/shard_map/ppermute | solution.py:1101
  363.5 3.1 add_convert_fusion.3
  368.4 12.0 %shard_map.207 = (bf16[2,4,96,512]{3,2,1,0:T(8,128)(2,1)S(1)}, bf16[2,4,96,512]{3,2,1,0:T(8,128)(2,1)S(1)}, bf16[2,4,96,512]{3,2,1,0:T(8,128)(2,1)}, bf16[2,4,96...) custom-call(bf16[2,4,96,512]{3,2,1,0:T(8,128)(2,1)} %copy-done.26, ...), custom_call_target="tpu_custom_call" | custom-call | tf_op jit(solution)/shard_map/pallas_call | solution.py:995
  381.0 2.2 add_convert_fusion.2
  386.3 2.2 add_convert_fusion.8
  388.5 1.7 collective-permute-start.51
  390.3 2.3 add_convert_fusion.5
  393.8 5.2 all-to-all-start.5
  399.0 2.5 collective-permute-start.66
  401.5 9.8 %collective-permute-done.51 = bf16[2,4,96,512]{3,2,1,0:T(8,128)(2,1)} collective-permute-done((bf16[2,4,96,512]{3,2,1,0:T(8,128)(2,1)}, bf16[2,4,96,512]{3,2,1,0:T(8,128)(2,1)}, u32[]{:S(2)}, u32[]{:S(2)}) %collective-permute-start.51) | collective-permute-done | bytes 786464 | tf_op jit(solution)/shard_map/ppermute | solution.py:1101
  411.3 3.2 collective-permute-start.67
  414.5 1.7 add_convert_fusion.7
  418.4 1.7 add_convert_fusion.4
  420.1 11.0 %collective-permute-done.33 = bf16[4,128,512]{2,1,0:T(8,128)(2,1)S(1)} collective-permute-done((bf16[4,128,512]{2,1,0:T(8,128)(2,1)S(1)}, bf16[4,128,512]{2,1,0:T(8,128)(2,1)S(1)}, u32[]{:S(2)}, u32[]{:S(2)}) %collective-permute-start.33) | collective-permute-done | bytes 524320 | tf_op jit(solution)/shard_map/ppermute | solution.py:1101
  431.1 1.6 collective-permute-start.56
  432.9 4.3 collective-permute-done.52
  437.2 1.6 collective-permute-start.37
  441.1 4.5 all-to-all-done.5
  445.6 3.5 all-to-all-start.6
  452.6 2.4 collective-permute-start.39
  456.5 14.1 %collective-permute-done.66.refs_2_ = bf16[384,1024]{1,0:T(8,128)(2,1)} collective-permute-done((bf16[384,1024]{1,0:T(8,128)(2,1)}, bf16[384,1024]{1,0:T(8,128)(2,1)}, u32[]{:S(2)}, u32[]{:S(2)}) %collective-permute-start.66) | collective-permute-done | bytes 786464 | tf_op jit(solution)/shard_map/ppermute | solution.py:1105
  470.6 4.9 shard_map.209
  475.5 37.1 %collective-permute-done.39 = bf16[2,128,512]{2,1,0:T(8,128)(2,1)S(1)} collective-permute-done((bf16[2,128,512]{2,1,0:T(8,128)(2,1)S(1)}, bf16[2,128,512]{2,1,0:T(8,128)(2,1)S(1)}, u32[]{:S(2)}, u32[]{:S(2)}) %collective-permute-start.39) | collective-permute-done | bytes 262176 | tf_op jit(solution)/shard_map/ppermute | solution.py:1105
  513.2 1.5 collective-permute-start.61
  514.8 1.5 collective-permute-start.57
  516.4 1.6 collective-permute-done.61
  522.4 1.7 collective-permute-done.62.refs_5_
  524.2 2.4 collective-permute-done.58.refs_1_
  528.8 3.4 shard_map.208
  (286 shorter events, 67.5 us)
Async XLA Ops:
  29.2 9.8 %collective-permute-start.4 = (bf16[4,96,512]{2,1,0:T(8,128)(2,1)S(1)}, bf16[4,96,512]{2,1,0:T(8,128)(2,1)S(1)}, u32[]{:S(2)}, u32[]{:S(2)}) collective-permute-start(bf16[4,96,512]{2,1,0:T(8,128)(2,1)S(1)} %get-tuple-element.145), channel_id=1, source_target_pairs={{0,4},{1,5},{2,6},{3,7},{4,0},{5,1},{6,2},{7,3},{8,12},{9,13},{10,... | collective-permute-start | bytes 1179656 | tf_op jit(solution)/shard_map/ppermute | solution.py:1101
  30.8 10.1 %collective-permute-start = (bf16[4,96,512]{2,1,0:T(8,128)(2,1)S(1)}, bf16[4,96,512]{2,1,0:T(8,128)(2,1)S(1)}, u32[]{:S(2)}, u32[]{:S(2)}) collective-permute-start(bf16[4,96,512]{2,1,0:T(8,128)(2,1)S(1)} %get-tuple-element.144), channel_id=1, source_target_pairs={{0,2},{1,3},{2,0},{3,1},{4,6},{5,7},{6,4},{7,5},{8,10},{9,11},{10,... | collective-permute-start | bytes 1179656 | tf_op jit(solution)/shard_map/ppermute | solution.py:1101
  39.1 18.0 %collective-permute-start.5 = (bf16[2,4,96,512]{3,2,1,0:T(8,128)(2,1)S(1)}, bf16[2,4,96,512]{3,2,1,0:T(8,128)(2,1)S(1)}, u32[]{:S(2)}, u32[]{:S(2)}) collective-permute-start(bf16[2,4,96,512]{3,2,1,0:T(8,128)(2,1)S(1)} %pad_maximum_fusion.6.refs_4_), channel_id=1, source_target_pairs={{0,2},{1,3},{2,0},{3,1},{4,6},{5,7},{6,4},{7,5},{8,10},{9,11},{10,... | collective-permute-start | bytes 2359304 | tf_op jit(solution)/shard_map/ppermute | solution.py:1101
  41.0 16.9 %collective-permute-start.1 = (bf16[2,4,96,512]{3,2,1,0:T(8,128)(2,1)S(1)}, bf16[2,4,96,512]{3,2,1,0:T(8,128)(2,1)S(1)}, u32[]{:S(2)}, u32[]{:S(2)}) collective-permute-start(bf16[2,4,96,512]{3,2,1,0:T(8,128)(2,1)S(1)} %pad_maximum_fusion.5.refs_0_), channel_id=1, source_target_pairs={{0,4},{1,5},{2,6},{3,7},{4,0},{5,1},{6,2},{7,3},{8,12},{9,13},{10,... | collective-permute-start | bytes 2359304 | tf_op jit(solution)/shard_map/ppermute | solution.py:1101
  42.4 15.6 %collective-permute-start.6 = (bf16[2,4,96,512]{3,2,1,0:T(8,128)(2,1)S(1)}, bf16[2,4,96,512]{3,2,1,0:T(8,128)(2,1)S(1)}, u32[]{:S(2)}, u32[]{:S(2)}) collective-permute-start(bf16[2,4,96,512]{3,2,1,0:T(8,128)(2,1)S(1)} %pad_maximum_fusion.6.refs_4_), channel_id=1, source_target_pairs={{0,1},{1,0},{2,3},{3,2},{4,5},{5,4},{6,7},{7,6},{8,9},{9,8},{10,11... | collective-permute-start | bytes 2359304 | tf_op jit(solution)/shard_map/ppermute | solution.py:1101
  42.4 15.6 %collective-permute-start.2 = (bf16[2,4,96,512]{3,2,1,0:T(8,128)(2,1)S(1)}, bf16[2,4,96,512]{3,2,1,0:T(8,128)(2,1)S(1)}, u32[]{:S(2)}, u32[]{:S(2)}) collective-permute-start(bf16[2,4,96,512]{3,2,1,0:T(8,128)(2,1)S(1)} %pad_maximum_fusion.5.refs_0_), channel_id=1, source_target_pairs={{0,1},{1,0},{2,3},{3,2},{4,5},{5,4},{6,7},{7,6},{8,9},{9,8},{10,11... | collective-permute-start | bytes 2359304 | tf_op jit(solution)/shard_map/ppermute | solution.py:1101
  68.4 50.9 %all-to-all-start.1 = ((bf16[4,2,128,512]{3,2,1,0:T(8,128)(2,1)}), bf16[4,2,128,512]{3,2,1,0:T(8,128)(2,1)S(1)}, u32[]{:S(2)}, u32[]{:S(2)}) async-start(bf16[4,2,128,512]{3,2,1,0:T(8,128)(2,1)} %get-tuple-element.56), calls=%async_computation.1 | async-start | bytes 2097152 | tf_op jit(solution)/shard_map/all_to_all | solution.py:1109
  72.3 23.7 %collective-permute-start.16 = (bf16[2,128,512]{2,1,0:T(8,128)(2,1)S(1)}, bf16[2,128,512]{2,1,0:T(8,128)(2,1)S(1)}, u32[]{:S(2)}, u32[]{:S(2)}) collective-permute-start(bf16[2,128,512]{2,1,0:T(8,128)(2,1)S(1)} %pad_maximum_fusion.11), channel_id=1, source_target_pairs={{0,8},{8,0},{16,24},{24,16},{1,9},{9,1},{17,25},{25,17},{2,10},{10... | collective-permute-start | bytes 786440 | tf_op jit(solution)/shard_map/ppermute | solution.py:1105
  74.4 41.8 %collective-permute-start.17 = (bf16[2,128,512]{2,1,0:T(8,128)(2,1)S(1)}, bf16[2,128,512]{2,1,0:T(8,128)(2,1)S(1)}, u32[]{:S(2)}, u32[]{:S(2)}) collective-permute-start(bf16[2,128,512]{2,1,0:T(8,128)(2,1)S(1)} %pad_maximum_fusion.11), channel_id=1, source_target_pairs={{0,16},{8,24},{16,0},{24,8},{1,17},{9,25},{17,1},{25,9},{2,18},{10... | collective-permute-start | bytes 786440 | tf_op jit(solution)/shard_map/ppermute | solution.py:1105
  76.8 39.5 %collective-permute-start.18 = (bf16[2,128,512]{2,1,0:T(8,128)(2,1)S(1)}, bf16[2,128,512]{2,1,0:T(8,128)(2,1)S(1)}, u32[]{:S(2)}, u32[]{:S(2)}) collective-permute-start(bf16[2,128,512]{2,1,0:T(8,128)(2,1)S(1)} %pad_maximum_fusion.11), channel_id=1, source_target_pairs={{0,24},{8,16},{16,8},{24,0},{1,25},{9,17},{17,9},{25,1},{2,26},{10... | collective-permute-start | bytes 786440 | tf_op jit(solution)/shard_map/ppermute | solution.py:1105
  116.5 15.0 %collective-permute-start.23 = (bf16[4,128,512]{2,1,0:T(8,128)(2,1)S(1)}, bf16[4,128,512]{2,1,0:T(8,128)(2,1)}, u32[]{:S(2)}, u32[]{:S(2)}) collective-permute-start(bf16[4,128,512]{2,1,0:T(8,128)(2,1)S(1)} %get-tuple-element.157), channel_id=1, source_target_pairs={{0,4},{1,5},{2,6},{3,7},{4,0},{5,1},{6,2},{7,3},{8,12},{9,13},{10,... | collective-permute-start | bytes 1572872 | tf_op jit(solution)/shard_map/ppermute | solution.py:1101
  118.1 16.8 %collective-permute-start.19 = (bf16[4,128,512]{2,1,0:T(8,128)(2,1)S(1)}, bf16[4,128,512]{2,1,0:T(8,128)(2,1)}, u32[]{:S(2)}, u32[]{:S(2)}) collective-permute-start(bf16[4,128,512]{2,1,0:T(8,128)(2,1)S(1)} %get-tuple-element.159), channel_id=1, source_target_pairs={{0,2},{1,3},{2,0},{3,1},{4,6},{5,7},{6,4},{7,5},{8,10},{9,11},{10,... | collective-permute-start | bytes 1572872 | tf_op jit(solution)/shard_map/ppermute | solution.py:1101
  120.8 25.4 %collective-permute-start.12 = (bf16[4,128,512]{2,1,0:T(8,128)(2,1)}, bf16[4,128,512]{2,1,0:T(8,128)(2,1)S(1)}, u32[]{:S(2)}, u32[]{:S(2)}) collective-permute-start(bf16[4,128,512]{2,1,0:T(8,128)(2,1)} %get-tuple-element.140), channel_id=1, source_target_pairs={{0,4},{1,5},{2,6},{3,7},{4,0},{5,1},{6,2},{7,3},{8,12},{9,13},{10,... | collective-permute-start | bytes 1572872 | tf_op jit(solution)/shard_map/ppermute | solution.py:1101
  121.5 27.1 %collective-permute-start.8 = (bf16[4,128,512]{2,1,0:T(8,128)(2,1)}, bf16[4,128,512]{2,1,0:T(8,128)(2,1)}, u32[]{:S(2)}, u32[]{:S(2)}) collective-permute-start(bf16[4,128,512]{2,1,0:T(8,128)(2,1)} %get-tuple-element.139), channel_id=1, source_target_pairs={{0,2},{1,3},{2,0},{3,1},{4,6},{5,7},{6,4},{7,5},{8,10},{9,11},{10,... | collective-permute-start | bytes 1572872 | tf_op jit(solution)/shard_map/ppermute | solution.py:1101
  133.5 68.7 %collective-permute-start.24 = (bf16[2,4,128,512]{3,2,1,0:T(8,128)(2,1)}, bf16[2,4,128,512]{3,2,1,0:T(8,128)(2,1)}, u32[]{:S(2)}, u32[]{:S(2)}) collective-permute-start(bf16[2,4,128,512]{3,2,1,0:T(8,128)(2,1)} %pad_maximum_fusion.3), channel_id=1, source_target_pairs={{0,2},{1,3},{2,0},{3,1},{4,6},{5,7},{6,4},{7,5},{8,10},{9,11},{10,... | collective-permute-start | bytes 3145736 | tf_op jit(solution)/shard_map/ppermute | solution.py:1101
  137.0 66.5 %collective-permute-start.20 = (bf16[2,4,128,512]{3,2,1,0:T(8,128)(2,1)}, bf16[2,4,128,512]{3,2,1,0:T(8,128)(2,1)}, u32[]{:S(2)}, u32[]{:S(2)}) collective-permute-start(bf16[2,4,128,512]{3,2,1,0:T(8,128)(2,1)} %pad_maximum_fusion.2), channel_id=1, source_target_pairs={{0,4},{1,5},{2,6},{3,7},{4,0},{5,1},{6,2},{7,3},{8,12},{9,13},{10,... | collective-permute-start | bytes 3145736 | tf_op jit(solution)/shard_map/ppermute | solution.py:1101
  140.9 32.6 %collective-permute-start.27 = (bf16[384,1024]{1,0:T(8,128)(2,1)}, bf16[384,1024]{1,0:T(8,128)(2,1)S(1)}, u32[]{:S(2)}, u32[]{:S(2)}) collective-permute-start(bf16[384,1024]{1,0:T(8,128)(2,1)} %get-tuple-element.57), channel_id=1, source_target_pairs={{0,8},{8,0},{16,24},{24,16},{1,9},{9,1},{17,25},{25,17},{2,10},{10... | collective-permute-start | bytes 2359304 | tf_op jit(solution)/shard_map/ppermute | solution.py:1105
  147.0 55.2 %collective-permute-start.28 = (bf16[384,1024]{1,0:T(8,128)(2,1)}, bf16[384,1024]{1,0:T(8,128)(2,1)S(1)}, u32[]{:S(2)}, u32[]{:S(2)}) collective-permute-start(bf16[384,1024]{1,0:T(8,128)(2,1)} %get-tuple-element.58), channel_id=1, source_target_pairs={{0,16},{8,24},{16,0},{24,8},{1,17},{9,25},{17,1},{25,9},{2,18},{10... | collective-permute-start | bytes 2359304 | tf_op jit(solution)/shard_map/ppermute | solution.py:1105
  148.6 54.2 %collective-permute-start.29 = (bf16[384,1024]{1,0:T(8,128)(2,1)}, bf16[384,1024]{1,0:T(8,128)(2,1)S(1)}, u32[]{:S(2)}, u32[]{:S(2)}) collective-permute-start(bf16[384,1024]{1,0:T(8,128)(2,1)} %get-tuple-element.59), channel_id=1, source_target_pairs={{0,24},{8,16},{16,8},{24,0},{1,25},{9,17},{17,9},{25,1},{2,26},{10... | collective-permute-start | bytes 2359304 | tf_op jit(solution)/shard_map/ppermute | solution.py:1105
  173.5 30.6 %collective-permute-start.25 = (bf16[2,4,128,512]{3,2,1,0:T(8,128)(2,1)}, bf16[2,4,128,512]{3,2,1,0:T(8,128)(2,1)}, u32[]{:S(2)}, u32[]{:S(2)}) collective-permute-start(bf16[2,4,128,512]{3,2,1,0:T(8,128)(2,1)} %pad_maximum_fusion.3), channel_id=1, source_target_pairs={{0,1},{1,0},{2,3},{3,2},{4,5},{5,4},{6,7},{7,6},{8,9},{9,8},{10,11... | collective-permute-start | bytes 3145736 | tf_op jit(solution)/shard_map/ppermute | solution.py:1101
  202.7 25.5 %collective-permute-start.13 = (bf16[2,4,128,512]{3,2,1,0:T(8,128)(2,1)}, bf16[2,4,128,512]{3,2,1,0:T(8,128)(2,1)}, u32[]{:S(2)}, u32[]{:S(2)}) collective-permute-start(bf16[2,4,128,512]{3,2,1,0:T(8,128)(2,1)} %pad_maximum_fusion.1), channel_id=1, source_target_pairs={{0,2},{1,3},{2,0},{3,1},{4,6},{5,7},{6,4},{7,5},{8,10},{9,11},{10,... | collective-permute-start | bytes 3145736 | tf_op jit(solution)/shard_map/ppermute | solution.py:1101
  203.5 25.2 %collective-permute-start.9 = (bf16[2,4,128,512]{3,2,1,0:T(8,128)(2,1)}, bf16[2,4,128,512]{3,2,1,0:T(8,128)(2,1)}, u32[]{:S(2)}, u32[]{:S(2)}) collective-permute-start(bf16[2,4,128,512]{3,2,1,0:T(8,128)(2,1)} %pad_maximum_fusion), channel_id=1, source_target_pairs={{0,4},{1,5},{2,6},{3,7},{4,0},{5,1},{6,2},{7,3},{8,12},{9,13},{10,... | collective-permute-start | bytes 3145736 | tf_op jit(solution)/shard_map/ppermute | solution.py:1101
  204.1 44.4 %collective-permute-start.22 = (bf16[2,4,128,512]{3,2,1,0:T(8,128)(2,1)}, bf16[2,4,128,512]{3,2,1,0:T(8,128)(2,1)}, u32[]{:S(2)}, u32[]{:S(2)}) collective-permute-start(bf16[2,4,128,512]{3,2,1,0:T(8,128)(2,1)} %collective-permute-done.20), channel_id=1, source_target_pairs={{0,1},{1,0},{2,3},{3,2},{4,5},{5,4},{6,7},{7,6},{8,9},{9,8},{10,11... | collective-permute-start | bytes 3145736 | tf_op jit(solution)/shard_map/ppermute | solution.py:1101
  205.2 43.3 %collective-permute-start.14 = (bf16[2,4,128,512]{3,2,1,0:T(8,128)(2,1)}, bf16[2,4,128,512]{3,2,1,0:T(8,128)(2,1)}, u32[]{:S(2)}, u32[]{:S(2)}) collective-permute-start(bf16[2,4,128,512]{3,2,1,0:T(8,128)(2,1)} %pad_maximum_fusion.1), channel_id=1, source_target_pairs={{0,1},{1,0},{2,3},{3,2},{4,5},{5,4},{6,7},{7,6},{8,9},{9,8},{10,11... | collective-permute-start | bytes 3145736 | tf_op jit(solution)/shard_map/ppermute | solution.py:1101
  206.7 41.8 %collective-permute-start.10 = (bf16[2,4,128,512]{3,2,1,0:T(8,128)(2,1)}, bf16[2,4,128,512]{3,2,1,0:T(8,128)(2,1)}, u32[]{:S(2)}, u32[]{:S(2)}) collective-permute-start(bf16[2,4,128,512]{3,2,1,0:T(8,128)(2,1)} %pad_maximum_fusion), channel_id=1, source_target_pairs={{0,1},{1,0},{2,3},{3,2},{4,5},{5,4},{6,7},{7,6},{8,9},{9,8},{10,11... | collective-permute-start | bytes 3145736 | tf_op jit(solution)/shard_map/ppermute | solution.py:1101
  228.2 20.3 %collective-permute-start.15 = (bf16[2,4,128,512]{3,2,1,0:T(8,128)(2,1)}, bf16[2,4,128,512]{3,2,1,0:T(8,128)(2,1)}, u32[]{:S(2)}, u32[]{:S(2)}) collective-permute-start(bf16[2,4,128,512]{3,2,1,0:T(8,128)(2,1)} %collective-permute-done.13), channel_id=1, source_target_pairs={{0,1},{1,0},{2,3},{3,2},{4,5},{5,4},{6,7},{7,6},{8,9},{9,8},{10,11... | collective-permute-start | bytes 3145736 | tf_op jit(solution)/shard_map/ppermute | solution.py:1101
  228.7 19.8 %collective-permute-start.11 = (bf16[2,4,128,512]{3,2,1,0:T(8,128)(2,1)}, bf16[2,4,128,512]{3,2,1,0:T(8,128)(2,1)}, u32[]{:S(2)}, u32[]{:S(2)}) collective-permute-start(bf16[2,4,128,512]{3,2,1,0:T(8,128)(2,1)} %collective-permute-done.9), channel_id=1, source_target_pairs={{0,1},{1,0},{2,3},{3,2},{4,5},{5,4},{6,7},{7,6},{8,9},{9,8},{10,11... | collective-permute-start | bytes 3145736 | tf_op jit(solution)/shard_map/ppermute | solution.py:1101
  282.4 5.9 %collective-permute-start.41 = (bf16[2,4,128,512]{3,2,1,0:T(8,128)(2,1)}, bf16[2,4,128,512]{3,2,1,0:T(8,128)(2,1)S(1)}, u32[]{:S(2)}, u32[]{:S(2)}) collective-permute-start(bf16[2,4,128,512]{3,2,1,0:T(8,128)(2,1)} %bitcast.270), channel_id=1, source_target_pairs={{0,1},{1,0},{2,3},{3,2},{4,5},{5,4},{6,7},{7,6},{8,9},{9,8},{10,11... | collective-permute-start | bytes 3145736 | tf_op jit(solution)/shard_map/ppermute | solution.py:1101
  286.3 25.3 %collective-permute-start.43 = (bf16[2,4,128,512]{3,2,1,0:T(8,128)(2,1)S(1)}, bf16[2,4,128,512]{3,2,1,0:T(8,128)(2,1)S(1)}, u32[]{:S(2)}, u32[]{:S(2)}) collective-permute-start(bf16[2,4,128,512]{3,2,1,0:T(8,128)(2,1)S(1)} %fusion.2), channel_id=1, source_target_pairs={{0,4},{1,5},{2,6},{3,7},{4,0},{5,1},{6,2},{7,3},{8,12},{9,13},{10,... | collective-permute-start | bytes 3145736 | tf_op jit(solution)/shard_map/ppermute | solution.py:1101
  287.2 26.5 %collective-permute-start.45 = (bf16[2,4,128,512]{3,2,1,0:T(8,128)(2,1)S(1)}, bf16[2,4,128,512]{3,2,1,0:T(8,128)(2,1)S(1)}, u32[]{:S(2)}, u32[]{:S(2)}) collective-permute-start(bf16[2,4,128,512]{3,2,1,0:T(8,128)(2,1)S(1)} %bitcast.269), channel_id=1, source_target_pairs={{0,1},{1,0},{2,3},{3,2},{4,5},{5,4},{6,7},{7,6},{8,9},{9,8},{10,11... | collective-permute-start | bytes 3145736 | tf_op jit(solution)/shard_map/ppermute | solution.py:1101
  287.5 26.1 %collective-permute-start.47 = (bf16[2,4,128,512]{3,2,1,0:T(8,128)(2,1)S(1)}, bf16[2,4,128,512]{3,2,1,0:T(8,128)(2,1)S(1)}, u32[]{:S(2)}, u32[]{:S(2)}) collective-permute-start(bf16[2,4,128,512]{3,2,1,0:T(8,128)(2,1)S(1)} %fusion), channel_id=1, source_target_pairs={{0,2},{1,3},{2,0},{3,1},{4,6},{5,7},{6,4},{7,5},{8,10},{9,11},{10,... | collective-permute-start | bytes 3145736 | tf_op jit(solution)/shard_map/ppermute | solution.py:1101
  288.1 49.2 %collective-permute-start.31 = (bf16[2,4,128,512]{3,2,1,0:T(8,128)(2,1)}, bf16[2,4,128,512]{3,2,1,0:T(8,128)(2,1)}, u32[]{:S(2)}, u32[]{:S(2)}) collective-permute-start(bf16[2,4,128,512]{3,2,1,0:T(8,128)(2,1)} %bitcast.60), channel_id=1, source_target_pairs={{0,1},{1,0},{2,3},{3,2},{4,5},{5,4},{6,7},{7,6},{8,9},{9,8},{10,11... | collective-permute-start | bytes 3145736 | tf_op jit(solution)/shard_map/ppermute | solution.py:1101
  312.9 13.5 %collective-permute-start.44 = (bf16[4,128,512]{2,1,0:T(8,128)(2,1)}, bf16[4,128,512]{2,1,0:T(8,128)(2,1)}, u32[]{:S(2)}, u32[]{:S(2)}) collective-permute-start(bf16[4,128,512]{2,1,0:T(8,128)(2,1)} %slice_bitcast_fusion.2), channel_id=1, source_target_pairs={{0,2},{1,3},{2,0},{3,1},{4,6},{5,7},{6,4},{7,5},{8,10},{9,11},{10,... | collective-permute-start | bytes 1572872 | tf_op jit(solution)/shard_map/ppermute | solution.py:1101
  316.9 13.4 %collective-permute-start.48 = (bf16[4,128,512]{2,1,0:T(8,128)(2,1)}, bf16[4,128,512]{2,1,0:T(8,128)(2,1)}, u32[]{:S(2)}, u32[]{:S(2)}) collective-permute-start(bf16[4,128,512]{2,1,0:T(8,128)(2,1)} %slice_bitcast_fusion), channel_id=1, source_target_pairs={{0,4},{1,5},{2,6},{3,7},{4,0},{5,1},{6,2},{7,3},{8,12},{9,13},{10,... | collective-permute-start | bytes 1572872 | tf_op jit(solution)/shard_map/ppermute | solution.py:1101
  317.6 23.5 %collective-permute-start.35 = (bf16[2,4,128,512]{3,2,1,0:T(8,128)(2,1)}, bf16[2,4,128,512]{3,2,1,0:T(8,128)(2,1)}, u32[]{:S(2)}, u32[]{:S(2)}) collective-permute-start(bf16[2,4,128,512]{3,2,1,0:T(8,128)(2,1)} %bitcast.66), channel_id=1, source_target_pairs={{0,1},{1,0},{2,3},{3,2},{4,5},{5,4},{6,7},{7,6},{8,9},{9,8},{10,11... | collective-permute-start | bytes 3145736 | tf_op jit(solution)/shard_map/ppermute | solution.py:1101
  317.6 15.1 %all-to-all-start.4 = ((f32[32,1,128]{2,1,0:T(1,128)}), f32[32,1,128]{2,1,0:T(1,128)S(1)}, u32[]{:S(2)}, u32[]{:S(2)}) async-start(f32[32,1,128]{2,1,0:T(1,128)} %get-tuple-element.78), calls=%async_computation.4 | async-start | bytes 32768 | tf_op jit(solution)/shard_map/all_to_all | solution.py:1109
  320.8 25.3 %collective-permute-start.30 = (bf16[2,4,128,512]{3,2,1,0:T(8,128)(2,1)}, bf16[2,4,128,512]{3,2,1,0:T(8,128)(2,1)}, u32[]{:S(2)}, u32[]{:S(2)}) collective-permute-start(bf16[2,4,128,512]{3,2,1,0:T(8,128)(2,1)} %bitcast.268), channel_id=1, source_target_pairs={{0,1},{1,0},{2,3},{3,2},{4,5},{5,4},{6,7},{7,6},{8,9},{9,8},{10,11... | collective-permute-start | bytes 3145736 | tf_op jit(solution)/shard_map/ppermute | solution.py:1101
  332.8 33.8 %all-to-all-start.3 = ((bf16[4,2,128,512]{3,2,1,0:T(8,128)(2,1)}), bf16[4,2,128,512]{3,2,1,0:T(8,128)(2,1)}, u32[]{:S(2)}, u32[]{:S(2)}) async-start(bf16[4,2,128,512]{3,2,1,0:T(8,128)(2,1)} %pad_maximum_fusion.4), calls=%async_computation.3 | async-start | bytes 2097152 | tf_op jit(solution)/shard_map/all_to_all | solution.py:1109
  339.9 23.6 %collective-permute-start.32 = (bf16[2,4,128,512]{3,2,1,0:T(8,128)(2,1)}, bf16[2,4,128,512]{3,2,1,0:T(8,128)(2,1)}, u32[]{:S(2)}, u32[]{:S(2)}) collective-permute-start(bf16[2,4,128,512]{3,2,1,0:T(8,128)(2,1)} %fusion.6), channel_id=1, source_target_pairs={{0,4},{1,5},{2,6},{3,7},{4,0},{5,1},{6,2},{7,3},{8,12},{9,13},{10,... | collective-permute-start | bytes 3145736 | tf_op jit(solution)/shard_map/ppermute | solution.py:1101
  341.1 39.9 %collective-permute-start.34 = (bf16[2,4,128,512]{3,2,1,0:T(8,128)(2,1)}, bf16[2,4,128,512]{3,2,1,0:T(8,128)(2,1)}, u32[]{:S(2)}, u32[]{:S(2)}) collective-permute-start(bf16[2,4,128,512]{3,2,1,0:T(8,128)(2,1)} %bitcast.64), channel_id=1, source_target_pairs={{0,1},{1,0},{2,3},{3,2},{4,5},{5,4},{6,7},{7,6},{8,9},{9,8},{10,11... | collective-permute-start | bytes 3145736 | tf_op jit(solution)/shard_map/ppermute | solution.py:1101
  343.6 37.4 %collective-permute-start.36 = (bf16[2,4,128,512]{3,2,1,0:T(8,128)(2,1)}, bf16[2,4,128,512]{3,2,1,0:T(8,128)(2,1)}, u32[]{:S(2)}, u32[]{:S(2)}) collective-permute-start(bf16[2,4,128,512]{3,2,1,0:T(8,128)(2,1)} %fusion.4), channel_id=1, source_target_pairs={{0,2},{1,3},{2,0},{3,1},{4,6},{5,7},{6,4},{7,5},{8,10},{9,11},{10,... | collective-permute-start | bytes 3145736 | tf_op jit(solution)/shard_map/ppermute | solution.py:1101
  344.3 110.7 %collective-permute-start.65 = (bf16[384,1024]{1,0:T(8,128)(2,1)}, bf16[384,1024]{1,0:T(8,128)(2,1)}, u32[]{:S(2)}, u32[]{:S(2)}) collective-permute-start(bf16[384,1024]{1,0:T(8,128)(2,1)} %get-tuple-element.95), channel_id=1, source_target_pairs={{0,8},{8,0},{16,24},{24,16},{1,9},{9,1},{17,25},{25,17},{2,10},{10... | collective-permute-start | bytes 2359304 | tf_op jit(solution)/shard_map/ppermute | solution.py:1105
  380.4 5.8 %collective-permute-start.50 = (bf16[2,4,96,512]{3,2,1,0:T(8,128)(2,1)}, bf16[2,4,96,512]{3,2,1,0:T(8,128)(2,1)}, u32[]{:S(2)}, u32[]{:S(2)}) collective-permute-start(bf16[2,4,96,512]{3,2,1,0:T(8,128)(2,1)} %get-tuple-element.85), channel_id=1, source_target_pairs={{0,1},{1,0},{2,3},{3,2},{4,5},{5,4},{6,7},{7,6},{8,9},{9,8},{10,11... | collective-permute-start | bytes 2359304 | tf_op jit(solution)/shard_map/ppermute | solution.py:1101
  380.5 9.7 %collective-permute-start.54 = (bf16[2,4,96,512]{3,2,1,0:T(8,128)(2,1)}, bf16[2,4,96,512]{3,2,1,0:T(8,128)(2,1)}, u32[]{:S(2)}, u32[]{:S(2)}) collective-permute-start(bf16[2,4,96,512]{3,2,1,0:T(8,128)(2,1)} %get-tuple-element.89), channel_id=1, source_target_pairs={{0,1},{1,0},{2,3},{3,2},{4,5},{5,4},{6,7},{7,6},{8,9},{9,8},{10,11... | collective-permute-start | bytes 2359304 | tf_op jit(solution)/shard_map/ppermute | solution.py:1101
  385.3 13.7 %collective-permute-start.49 = (bf16[2,4,96,512]{3,2,1,0:T(8,128)(2,1)}, bf16[2,4,96,512]{3,2,1,0:T(8,128)(2,1)}, u32[]{:S(2)}, u32[]{:S(2)}) collective-permute-start(bf16[2,4,96,512]{3,2,1,0:T(8,128)(2,1)} %get-tuple-element.83), channel_id=1, source_target_pairs={{0,1},{1,0},{2,3},{3,2},{4,5},{5,4},{6,7},{7,6},{8,9},{9,8},{10,11... | collective-permute-start | bytes 2359304 | tf_op jit(solution)/shard_map/ppermute | solution.py:1101
  385.3 31.0 %collective-permute-start.53 = (bf16[2,4,96,512]{3,2,1,0:T(8,128)(2,1)}, bf16[2,4,96,512]{3,2,1,0:T(8,128)(2,1)}, u32[]{:S(2)}, u32[]{:S(2)}) collective-permute-start(bf16[2,4,96,512]{3,2,1,0:T(8,128)(2,1)} %get-tuple-element.87), channel_id=1, source_target_pairs={{0,1},{1,0},{2,3},{3,2},{4,5},{5,4},{6,7},{7,6},{8,9},{9,8},{10,11... | collective-permute-start | bytes 2359304 | tf_op jit(solution)/shard_map/ppermute | solution.py:1101
  388.5 22.8 %collective-permute-start.51 = (bf16[2,4,96,512]{3,2,1,0:T(8,128)(2,1)}, bf16[2,4,96,512]{3,2,1,0:T(8,128)(2,1)}, u32[]{:S(2)}, u32[]{:S(2)}) collective-permute-start(bf16[2,4,96,512]{3,2,1,0:T(8,128)(2,1)} %add_convert_fusion.8), channel_id=1, source_target_pairs={{0,4},{1,5},{2,6},{3,7},{4,0},{5,1},{6,2},{7,3},{8,12},{9,13},{10,... | collective-permute-start | bytes 2359304 | tf_op jit(solution)/shard_map/ppermute | solution.py:1101
  392.6 24.9 %collective-permute-start.55 = (bf16[2,4,96,512]{3,2,1,0:T(8,128)(2,1)}, bf16[2,4,96,512]{3,2,1,0:T(8,128)(2,1)}, u32[]{:S(2)}, u32[]{:S(2)}) collective-permute-start(bf16[2,4,96,512]{3,2,1,0:T(8,128)(2,1)} %add_convert_fusion.5), channel_id=1, source_target_pairs={{0,2},{1,3},{2,0},{3,1},{4,6},{5,7},{6,4},{7,5},{8,10},{9,11},{10,... | collective-permute-start | bytes 2359304 | tf_op jit(solution)/shard_map/ppermute | solution.py:1101
  393.8 51.9 %all-to-all-start.5 = ((f32[32,1,3072]{2,1,0:T(1,128)}), f32[32,1,3072]{2,1,0:T(1,128)S(1)}, u32[]{:S(2)}, u32[]{:S(2)}) async-start(f32[32,1,3072]{2,1,0:T(1,128)} %all_to_all.29), calls=%async_computation.5 | async-start | bytes 786432 | tf_op jit(solution)/shard_map/all_to_all | solution.py:1109
  399.0 71.6 %collective-permute-start.66 = (bf16[384,1024]{1,0:T(8,128)(2,1)}, bf16[384,1024]{1,0:T(8,128)(2,1)}, u32[]{:S(2)}, u32[]{:S(2)}) collective-permute-start(bf16[384,1024]{1,0:T(8,128)(2,1)} %get-tuple-element.96), channel_id=1, source_target_pairs={{0,16},{8,24},{16,0},{24,8},{1,17},{9,25},{17,1},{25,9},{2,18},{10... | collective-permute-start | bytes 2359304 | tf_op jit(solution)/shard_map/ppermute | solution.py:1105
  411.3 59.3 %collective-permute-start.67 = (bf16[384,1024]{1,0:T(8,128)(2,1)}, bf16[384,1024]{1,0:T(8,128)(2,1)}, u32[]{:S(2)}, u32[]{:S(2)}) collective-permute-start(bf16[384,1024]{1,0:T(8,128)(2,1)} %get-tuple-element.97), channel_id=1, source_target_pairs={{0,24},{8,16},{16,8},{24,0},{1,25},{9,17},{17,9},{25,1},{2,26},{10... | collective-permute-start | bytes 2359304 | tf_op jit(solution)/shard_map/ppermute | solution.py:1105
  416.3 14.9 %collective-permute-start.33 = (bf16[4,128,512]{2,1,0:T(8,128)(2,1)S(1)}, bf16[4,128,512]{2,1,0:T(8,128)(2,1)S(1)}, u32[]{:S(2)}, u32[]{:S(2)}) collective-permute-start(bf16[4,128,512]{2,1,0:T(8,128)(2,1)S(1)} %copy-done.45), channel_id=1, source_target_pairs={{0,2},{1,3},{2,0},{3,1},{4,6},{5,7},{6,4},{7,5},{8,10},{9,11},{10,... | collective-permute-start | bytes 1572872 | tf_op jit(solution)/shard_map/ppermute | solution.py:1101
  417.4 19.8 %collective-permute-start.52 = (bf16[4,96,512]{2,1,0:T(8,128)(2,1)S(1)}, bf16[4,96,512]{2,1,0:T(8,128)(2,1)S(1)}, u32[]{:S(2)}, u32[]{:S(2)}) collective-permute-start(bf16[4,96,512]{2,1,0:T(8,128)(2,1)S(1)} %slice_bitcast_fusion.14), channel_id=1, source_target_pairs={{0,2},{1,3},{2,0},{3,1},{4,6},{5,7},{6,4},{7,5},{8,10},{9,11},{10,... | collective-permute-start | bytes 1179656 | tf_op jit(solution)/shard_map/ppermute | solution.py:1101
  431.1 8.8 %collective-permute-start.56 = (bf16[4,96,512]{2,1,0:T(8,128)(2,1)S(1)}, bf16[4,96,512]{2,1,0:T(8,128)(2,1)S(1)}, u32[]{:S(2)}, u32[]{:S(2)}) collective-permute-start(bf16[4,96,512]{2,1,0:T(8,128)(2,1)S(1)} %slice_bitcast_fusion.12), channel_id=1, source_target_pairs={{0,4},{1,5},{2,6},{3,7},{4,0},{5,1},{6,2},{7,3},{8,12},{9,13},{10,... | collective-permute-start | bytes 1179656 | tf_op jit(solution)/shard_map/ppermute | solution.py:1101
  437.2 13.3 %collective-permute-start.37 = (bf16[4,128,512]{2,1,0:T(8,128)(2,1)}, bf16[4,128,512]{2,1,0:T(8,128)(2,1)}, u32[]{:S(2)}, u32[]{:S(2)}) collective-permute-start(bf16[4,128,512]{2,1,0:T(8,128)(2,1)} %slice_bitcast_fusion.4), channel_id=1, source_target_pairs={{0,4},{1,5},{2,6},{3,7},{4,0},{5,1},{6,2},{7,3},{8,12},{9,13},{10,... | collective-permute-start | bytes 1572872 | tf_op jit(solution)/shard_map/ppermute | solution.py:1101
  445.6 67.4 %all-to-all-start.6 = ((bf16[4,2,96,512]{3,2,1,0:T(8,128)(2,1)}), bf16[4,2,96,512]{3,2,1,0:T(8,128)(2,1)S(1)}, u32[]{:S(2)}, u32[]{:S(2)}) async-start(bf16[4,2,96,512]{3,2,1,0:T(8,128)(2,1)} %copy.34), calls=%async_computation.6 | async-start | bytes 1572864 | tf_op jit(solution)/shard_map/all_to_all | solution.py:1109
  451.8 23.7 %collective-permute-start.38 = (bf16[2,128,512]{2,1,0:T(8,128)(2,1)S(1)}, bf16[2,128,512]{2,1,0:T(8,128)(2,1)S(1)}, u32[]{:S(2)}, u32[]{:S(2)}) collective-permute-start(bf16[2,128,512]{2,1,0:T(8,128)(2,1)S(1)} %pad_maximum_fusion.12), channel_id=1, source_target_pairs={{0,8},{8,0},{16,24},{24,16},{1,9},{9,1},{17,25},{25,17},{2,10},{10... | collective-permute-start | bytes 786440 | tf_op jit(solution)/shard_map/ppermute | solution.py:1105
  452.6 60.1 %collective-permute-start.39 = (bf16[2,128,512]{2,1,0:T(8,128)(2,1)S(1)}, bf16[2,128,512]{2,1,0:T(8,128)(2,1)S(1)}, u32[]{:S(2)}, u32[]{:S(2)}) collective-permute-start(bf16[2,128,512]{2,1,0:T(8,128)(2,1)S(1)} %pad_maximum_fusion.13), channel_id=1, source_target_pairs={{0,16},{8,24},{16,0},{24,8},{1,17},{9,25},{17,1},{25,9},{2,18},{10... | collective-permute-start | bytes 786440 | tf_op jit(solution)/shard_map/ppermute | solution.py:1105
  455.0 57.6 %collective-permute-start.40 = (bf16[2,128,512]{2,1,0:T(8,128)(2,1)S(1)}, bf16[2,128,512]{2,1,0:T(8,128)(2,1)S(1)}, u32[]{:S(2)}, u32[]{:S(2)}) collective-permute-start(bf16[2,128,512]{2,1,0:T(8,128)(2,1)S(1)} %pad_maximum_fusion.14), channel_id=1, source_target_pairs={{0,24},{8,16},{16,8},{24,0},{1,25},{9,17},{17,9},{25,1},{2,26},{10... | collective-permute-start | bytes 786440 | tf_op jit(solution)/shard_map/ppermute | solution.py:1105
  514.8 5.8 %collective-permute-start.57 = (bf16[97,512]{1,0:T(8,128)(2,1)S(1)}, bf16[97,512]{1,0:T(8,128)(2,1)S(1)}, u32[]{:S(2)}, u32[]{:S(2)}) collective-permute-start(bf16[97,512]{1,0:T(8,128)(2,1)S(1)} %bitcast.259), channel_id=1, source_target_pairs={{0,2},{1,3},{2,0},{3,1},{4,6},{5,7},{6,4},{7,5},{8,10},{9,11},{10,... | collective-permute-start | bytes 297992 | tf_op jit(solution)/shard_map/ppermute | solution.py:1101
  518.0 6.1 %collective-permute-start.62 = (bf16[2,97,512]{2,1,0:T(8,128)(2,1)S(1)}, bf16[2,97,512]{2,1,0:T(8,128)(2,1)S(1)}, u32[]{:S(2)}, u32[]{:S(2)}) collective-permute-start(bf16[2,97,512]{2,1,0:T(8,128)(2,1)S(1)} %pad_maximum_fusion.16.refs_4_), channel_id=1, source_target_pairs={{0,2},{1,3},{2,0},{3,1},{4,6},{5,7},{6,4},{7,5},{8,10},{9,11},{10,... | collective-permute-start | bytes 595976 | tf_op jit(solution)/shard_map/ppermute | solution.py:1101
  520.7 5.9 %collective-permute-start.58 = (bf16[2,97,512]{2,1,0:T(8,128)(2,1)S(1)}, bf16[2,97,512]{2,1,0:T(8,128)(2,1)S(1)}, u32[]{:S(2)}, u32[]{:S(2)}) collective-permute-start(bf16[2,97,512]{2,1,0:T(8,128)(2,1)S(1)} %pad_maximum_fusion.15.refs_0_), channel_id=1, source_target_pairs={{0,4},{1,5},{2,6},{3,7},{4,0},{5,1},{6,2},{7,3},{8,12},{9,13},{10,... | collective-permute-start | bytes 595976 | tf_op jit(solution)/shard_map/ppermute | solution.py:1101
  521.9 5.3 collective-permute-start.63
  521.9 5.3 collective-permute-start.59
  (66 other events, 723.8 us)

commit v2 on v1

--- a/solution.py
+++ b/solution.py
@@ -989,14 +989,13 @@
 def attention_backward(pieces_a, pieces_b, *rest):
     hbm = pl.BlockSpec(memory_space=pltpu.HBM)
     f32, b16 = jnp.float32, jnp.bfloat16
-    piece = jax.ShapeDtypeStruct((2, 4, 96, D // 2), b16)
     far = pltpu.HBM((2, 4, 96, D // 2), b16)
     shapes = [((128, D), b16), ((2, D), f32), ((EXPERTS, D), f32)]
     outs = pl.pallas_call(
         attention_backward_kernel,
         in_specs=[hbm] * (8 + len(rest)),
         out_specs=[hbm] * 11,
-        out_shape=([piece] * 2 + [far] * 2) * 2 + [pltpu.HBM(*pair) for pair in shapes],
+        out_shape=[far] * 8 + [pltpu.HBM(*pair) for pair in shapes],
         scratch_shapes=[pltpu.VMEM(array.shape, array.dtype) for array in rest]
         + [pltpu.VMEM(*pair) for pair in shapes]
         + [
@@ -1192,11 +1191,13 @@
     router = router.reshape(EXPERTS, D)
 
     sent = sliced(w_gate_up, w_down)
-    weights = [w_gate_up, w_down] + [trade(sent[s - 1], s) for s in range(1, 4)]
-    cot_a, cot_b = gather_traded(split(out_cotangent))
 
     def in_hbm(pieces):
         return [pltpu.with_memory_space_constraint(p, pltpu.HBM) for p in pieces]
+
+    weights = [w_gate_up, w_down]
+    weights += in_hbm([trade(sent[s - 1], s) for s in range(1, 4)])
+    cot_a, cot_b = gather_traded(split(out_cotangent))
 
     weights_a, weights_b = in_hbm(weights_a), in_hbm(weights_b)
     rope = jnp.asarray(np.stack(rope_constants(128)))

time: 538 us -> 535 us (level)
  waiting for transfers between devices: 287 us -> 281 us
  transfers between devices with their start and end apart: 73 -> 73, of which waited for: 33 -> 31; matrix products, arithmetic and copies ran while one was open for 9% -> 9% of each run, Pallas kernels for 4% -> 3%
where the time goes in v2:
time: 535 us; the launch traced here: 531 us
  waiting for transfers between devices  281 us (53%)
  starting transfers between devices  82.6 us (15%)
  Pallas kernels  60.6 us (11%)
  blocking collectives  45.1 us (8%)
  other arithmetic  39.3 us (7%)
  local copies, waits for them, and re-layouts  20.9 us (4%)
    ppermute x56, waiting for transfers between devices, swap(): return lax.ppermute(array, EX, [(i, i ^ bit) for i in range(8)])  140 us
    ppermute x12, waiting for transfers between devices, trade(): return lax.ppermute(array, DP, [(i, i ^ step) for i in range(4)])  136 us
    all_to_all x2, blocking collectives, everyone(): return lax.all_to_all(array, axes, split_axis=0, concat_axis=0, tiled=True)  45.1 us
    ppermute x56, starting transfers between devices, swap(): return lax.ppermute(array, EX, [(i, i ^ bit) for i in range(8)])  36.4 us
    pallas_call x1, Pallas kernels, expert_call(): pl.pallas_call(expert_kernel, in_specs=[hbm] * 21 + [vmem] * 2, out_specs...  32.1 us
    ppermute x12, starting transfers between devices, trade(): return lax.ppermute(array, DP, [(i, i ^ step) for i in range(4)])  26.7 us
    convert_element_type x14, other arithmetic, add(): (one.astype(jnp.float32) + two.astype(jnp.float32)).astype(jnp.bfloat16)  23.5 us
    all_to_all x5, starting transfers between devices, everyone(): return lax.all_to_all(array, axes, split_axis=0, concat_axis=0, tiled=True)  19.5 us
  transfers between devices with their start and end apart: 73, of which 31 were waited for; matrix products, arithmetic and copies ran while one was open for 9% of the time, Pallas kernels for 3%

profile of v2, /device:TPU:0, one launch (start us, length us, event | category | flops | bytes accessed | tf_op | source)
XLA Modules:
  0.0 531.2 jit_solution(981055161936947077)
XLA Ops:
  2.7 26.3 %all_to_all.39 = bf16[4,2,96,512]{3,2,1,0:T(8,128)(2,1)S(1)} all-to-all(bf16[4,2,96,512]{3,2,1,0:T(8,128)(2,1)S(1)} %broadcast_in_dim.28), channel_id=1, replica_groups=mesh['dp'=4,'expert'=8] {'dp'}, dimensions={0} | all-to-all | bytes 1572864 | tf_op jit(solution)/shard_map/all_to_all | solution.py:1108
  29.2 1.6 collective-permute-start.4
  32.3 6.8 %collective-permute-done.4 = bf16[4,96,512]{2,1,0:T(8,128)(2,1)S(1)} collective-permute-done((bf16[4,96,512]{2,1,0:T(8,128)(2,1)S(1)}, bf16[4,96,512]{2,1,0:T(8,128)(2,1)S(1)}, u32[]{:S(2)}, u32[]{:S(2)}) %collective-permute-start.4) | collective-permute-done | bytes 393248 | tf_op jit(solution)/shard_map/ppermute | solution.py:1100
  39.1 1.6 collective-permute-start.5
  42.9 14.3 %collective-permute-done.5.refs_5_ = bf16[2,4,96,512]{3,2,1,0:T(8,128)(2,1)S(1)} collective-permute-done((bf16[2,4,96,512]{3,2,1,0:T(8,128)(2,1)S(1)}, bf16[2,4,96,512]{3,2,1,0:T(8,128)(2,1)S(1)}, u32[]{:S(2)}, u32[]{:S(2)}) %collective-permute-start.5) | collective-permute-done | bytes 786464 | tf_op jit(solution)/shard_map/ppermute | solution.py:1100
  61.5 7.0 %shard_map.204 = (bf16[128,4096]{1,0:T(8,128)(2,1)}, f32[128,1024]{1,0:T(8,128)}, f32[256,16]{1,0:T(8,128)}, bf16[4,2,128,512]{3,2,1,0:T(8,128)(2,1)}) custom-call(bf16[2,4,96,512]{3,2,1,0:T(8,128)(2,1)} %copy-done.20, bf16[2,4,96,512]{3,2,1,0:T(8,128)(2,1)} %copy-done.25, bf16[2,4,96,512]{3,2,1,0:T(8,128)(2,1)} %copy-done.27, ...), custom_call_target="tpu_custom_call" | custom-call | tf_op jit(solution)/shard_map/pallas_call | solution.py:799
  68.5 3.8 all-to-all-start.1
  72.3 2.1 collective-permute-start.16
  74.4 2.4 collective-permute-start.17
  76.9 19.2 %collective-permute-done.16 = bf16[2,128,512]{2,1,0:T(8,128)(2,1)S(1)} collective-permute-done((bf16[2,128,512]{2,1,0:T(8,128)(2,1)S(1)}, bf16[2,128,512]{2,1,0:T(8,128)(2,1)S(1)}, u32[]{:S(2)}, u32[]{:S(2)}) %collective-permute-start.16) | collective-permute-done | bytes 262176 | tf_op jit(solution)/shard_map/ppermute | solution.py:1104
  96.1 20.2 %collective-permute-done.17 = bf16[2,128,512]{2,1,0:T(8,128)(2,1)S(1)} collective-permute-done((bf16[2,128,512]{2,1,0:T(8,128)(2,1)S(1)}, bf16[2,128,512]{2,1,0:T(8,128)(2,1)S(1)}, u32[]{:S(2)}, u32[]{:S(2)}) %collective-permute-start.17) | collective-permute-done | bytes 262176 | tf_op jit(solution)/shard_map/ppermute | solution.py:1104
  123.1 8.3 %collective-permute-done.23 = bf16[4,128,512]{2,1,0:T(8,128)(2,1)S(1)} collective-permute-done((bf16[4,128,512]{2,1,0:T(8,128)(2,1)S(1)}, bf16[4,128,512]{2,1,0:T(8,128)(2,1)S(1)}, u32[]{:S(2)}, u32[]{:S(2)}) %collective-permute-start.23) | collective-permute-done | bytes 524320 | tf_op jit(solution)/shard_map/ppermute | solution.py:1100
  137.4 2.6 shard_map.205
  140.0 5.2 collective-permute-start.27
  145.3 2.6 collective-permute-start.28
  147.9 2.4 collective-permute-start.29
  150.2 2.1 pad_maximum_fusion.1
  152.4 2.1 pad_maximum_fusion
  154.5 18.9 %collective-permute-done.27.refs_18_ = bf16[384,1024]{1,0:T(8,128)(2,1)S(1)} collective-permute-done((bf16[384,1024]{1,0:T(8,128)(2,1)}, bf16[384,1024]{1,0:T(8,128)(2,1)S(1)}, u32[]{:S(2)}, u32[]{:S(2)}) %collective-permute-start.27) | collective-permute-done | bytes 786464 | tf_op jit(solution)/shard_map/ppermute | solution.py:1104
  173.4 27.1 %collective-permute-done.28.refs_19_ = bf16[384,1024]{1,0:T(8,128)(2,1)S(1)} collective-permute-done((bf16[384,1024]{1,0:T(8,128)(2,1)}, bf16[384,1024]{1,0:T(8,128)(2,1)S(1)}, u32[]{:S(2)}, u32[]{:S(2)}) %collective-permute-start.28) | collective-permute-done | bytes 786464 | tf_op jit(solution)/shard_map/ppermute | solution.py:1104
  206.4 20.1 %collective-permute-done.13 = bf16[2,4,128,512]{3,2,1,0:T(8,128)(2,1)} collective-permute-done((bf16[2,4,128,512]{3,2,1,0:T(8,128)(2,1)}, bf16[2,4,128,512]{3,2,1,0:T(8,128)(2,1)}, u32[]{:S(2)}, u32[]{:S(2)}) %collective-permute-start.13) | collective-permute-done | bytes 1048608 | tf_op jit(solution)/shard_map/ppermute | solution.py:1100
  227.7 18.9 %all_to_all.40 = bf16[32,2,1024]{2,1,0:T(2,128)(2,1)S(1)} all-to-all(bf16[32,2,1024]{2,1,0:T(2,128)(2,1)S(1)} %broadcast_in_dim.32), channel_id=1, replica_groups=mesh['dp'=4,'expert'=8] {'expert','dp'}, dimensions={0} | all-to-all | bytes 262144 | tf_op jit(solution)/shard_map/all_to_all | solution.py:1108
  248.9 32.1 %shard_map.206 = (bf16[1024,512]{1,0:T(8,128)(2,1)S(1)}, bf16[1024,512]{1,0:T(8,128)(2,1)S(1)}, bf16[1024,512]{1,0:T(8,128)(2,1)}, bf16[1024,512]{1,0:T(8,128)(2...) custom-call(bf16[1024,512]{1,0:T(8,128)(2,1)} %bitcast.14.refs_0_, ...), custom_call_target="tpu_custom_call" | custom-call | tf_op jit(solution)/shard_map/pallas_call | solution.py:621
  281.7 2.3 collective-permute-done.42
  287.5 23.2 %collective-permute-done.43 = bf16[2,4,128,512]{3,2,1,0:T(8,128)(2,1)S(1)} collective-permute-done((bf16[2,4,128,512]{3,2,1,0:T(8,128)(2,1)S(1)}, bf16[2,4,128,512]{3,2,1,0:T(8,128)(2,1)S(1)}, u32[]{:S(2)}, u32[]{:S(2)}) %collective-permute-start.43) | collective-permute-done | bytes 1048608 | tf_op jit(solution)/shard_map/ppermute | solution.py:1100
  314.3 1.9 slice_bitcast_fusion
  316.9 3.1 all-to-all-start.4
  320.4 5.3 %collective-permute-done.44 = bf16[4,128,512]{2,1,0:T(8,128)(2,1)} collective-permute-done((bf16[4,128,512]{2,1,0:T(8,128)(2,1)}, bf16[4,128,512]{2,1,0:T(8,128)(2,1)}, u32[]{:S(2)}, u32[]{:S(2)}) %collective-permute-start.44) | collective-permute-done | bytes 524320 | tf_op jit(solution)/shard_map/ppermute | solution.py:1100
  326.8 2.7 collective-permute-done.48
  332.1 3.7 all-to-all-start.3
  335.8 2.5 fusion.6
  339.6 2.5 fusion.4
  342.8 1.8 collective-permute-start.65
  344.6 17.4 %collective-permute-done.32 = bf16[2,4,128,512]{3,2,1,0:T(8,128)(2,1)} collective-permute-done((bf16[2,4,128,512]{3,2,1,0:T(8,128)(2,1)}, bf16[2,4,128,512]{3,2,1,0:T(8,128)(2,1)}, u32[]{:S(2)}, u32[]{:S(2)}) %collective-permute-start.32) | collective-permute-done | bytes 1048608 | tf_op jit(solution)/shard_map/ppermute | solution.py:1100
  362.0 3.0 add_convert_fusion.3
  366.3 10.7 %shard_map.207 = (bf16[2,4,96,512]{3,2,1,0:T(8,128)(2,1)}, bf16[2,4,96,512]{3,2,1,0:T(8,128)(2,1)}, bf16[2,4,96,512]{3,2,1,0:T(8,128)(2,1)}, bf16[2,4,96,512]{3,...) custom-call(bf16[2,4,96,512]{3,2,1,0:T(8,128)(2,1)} %copy-done.20, ...), custom_call_target="tpu_custom_call" | custom-call | tf_op jit(solution)/shard_map/pallas_call | solution.py:994
  377.6 2.1 add_convert_fusion.2
  382.4 2.5 add_convert_fusion.8
  384.9 1.7 collective-permute-start.51
  386.7 2.2 add_convert_fusion.5
  390.1 5.3 all-to-all-start.5
  395.5 2.4 collective-permute-start.66
  397.9 9.9 %collective-permute-done.51 = bf16[2,4,96,512]{3,2,1,0:T(8,128)(2,1)} collective-permute-done((bf16[2,4,96,512]{3,2,1,0:T(8,128)(2,1)}, bf16[2,4,96,512]{3,2,1,0:T(8,128)(2,1)}, u32[]{:S(2)}, u32[]{:S(2)}) %collective-permute-start.51) | collective-permute-done | bytes 786464 | tf_op jit(solution)/shard_map/ppermute | solution.py:1100
  407.8 3.2 collective-permute-start.67
  411.0 1.9 add_convert_fusion.7
  415.1 1.7 add_convert_fusion.4
  416.8 11.0 %collective-permute-done.33 = bf16[4,128,512]{2,1,0:T(8,128)(2,1)S(1)} collective-permute-done((bf16[4,128,512]{2,1,0:T(8,128)(2,1)S(1)}, bf16[4,128,512]{2,1,0:T(8,128)(2,1)S(1)}, u32[]{:S(2)}, u32[]{:S(2)}) %collective-permute-start.33) | collective-permute-done | bytes 524320 | tf_op jit(solution)/shard_map/ppermute | solution.py:1100
  427.8 1.6 collective-permute-start.56
  429.6 4.4 collective-permute-done.52
  434.0 1.6 collective-permute-start.37
  437.6 4.5 all-to-all-done.5
  442.1 3.5 all-to-all-start.6
  445.6 1.6 collective-permute-done.37
  449.0 2.4 collective-permute-start.39
  451.5 1.7 collective-permute-start.40
  453.2 13.8 %collective-permute-done.66.refs_2_ = bf16[384,1024]{1,0:T(8,128)(2,1)} collective-permute-done((bf16[384,1024]{1,0:T(8,128)(2,1)}, bf16[384,1024]{1,0:T(8,128)(2,1)}, u32[]{:S(2)}, u32[]{:S(2)}) %collective-permute-start.66) | collective-permute-done | bytes 786464 | tf_op jit(solution)/shard_map/ppermute | solution.py:1104
  467.0 4.9 shard_map.209
  471.9 37.1 %collective-permute-done.39 = bf16[2,128,512]{2,1,0:T(8,128)(2,1)S(1)} collective-permute-done((bf16[2,128,512]{2,1,0:T(8,128)(2,1)S(1)}, bf16[2,128,512]{2,1,0:T(8,128)(2,1)S(1)}, u32[]{:S(2)}, u32[]{:S(2)}) %collective-permute-start.39) | collective-permute-done | bytes 262176 | tf_op jit(solution)/shard_map/ppermute | solution.py:1104
  510.6 1.5 collective-permute-start.61
  512.2 1.5 collective-permute-start.57
  513.7 1.6 collective-permute-done.61
  519.8 1.7 collective-permute-done.62.refs_5_
  521.5 2.4 collective-permute-done.58.refs_1_
  526.2 3.4 shard_map.208
  (290 shorter events, 68.5 us)
Async XLA Ops:
  29.2 9.8 %collective-permute-start.4 = (bf16[4,96,512]{2,1,0:T(8,128)(2,1)S(1)}, bf16[4,96,512]{2,1,0:T(8,128)(2,1)S(1)}, u32[]{:S(2)}, u32[]{:S(2)}) collective-permute-start(bf16[4,96,512]{2,1,0:T(8,128)(2,1)S(1)} %get-tuple-element.145), channel_id=1, source_target_pairs={{0,4},{1,5},{2,6},{3,7},{4,0},{5,1},{6,2},{7,3},{8,12},{9,13},{10,... | collective-permute-start | bytes 1179656 | tf_op jit(solution)/shard_map/ppermute | solution.py:1100
  30.8 10.1 %collective-permute-start = (bf16[4,96,512]{2,1,0:T(8,128)(2,1)S(1)}, bf16[4,96,512]{2,1,0:T(8,128)(2,1)S(1)}, u32[]{:S(2)}, u32[]{:S(2)}) collective-permute-start(bf16[4,96,512]{2,1,0:T(8,128)(2,1)S(1)} %get-tuple-element.144), channel_id=1, source_target_pairs={{0,2},{1,3},{2,0},{3,1},{4,6},{5,7},{6,4},{7,5},{8,10},{9,11},{10,... | collective-permute-start | bytes 1179656 | tf_op jit(solution)/shard_map/ppermute | solution.py:1100
  39.1 18.0 %collective-permute-start.5 = (bf16[2,4,96,512]{3,2,1,0:T(8,128)(2,1)S(1)}, bf16[2,4,96,512]{3,2,1,0:T(8,128)(2,1)S(1)}, u32[]{:S(2)}, u32[]{:S(2)}) collective-permute-start(bf16[2,4,96,512]{3,2,1,0:T(8,128)(2,1)S(1)} %pad_maximum_fusion.6.refs_4_), channel_id=1, source_target_pairs={{0,2},{1,3},{2,0},{3,1},{4,6},{5,7},{6,4},{7,5},{8,10},{9,11},{10,... | collective-permute-start | bytes 2359304 | tf_op jit(solution)/shard_map/ppermute | solution.py:1100
  41.0 16.9 %collective-permute-start.1 = (bf16[2,4,96,512]{3,2,1,0:T(8,128)(2,1)S(1)}, bf16[2,4,96,512]{3,2,1,0:T(8,128)(2,1)S(1)}, u32[]{:S(2)}, u32[]{:S(2)}) collective-permute-start(bf16[2,4,96,512]{3,2,1,0:T(8,128)(2,1)S(1)} %pad_maximum_fusion.5.refs_0_), channel_id=1, source_target_pairs={{0,4},{1,5},{2,6},{3,7},{4,0},{5,1},{6,2},{7,3},{8,12},{9,13},{10,... | collective-permute-start | bytes 2359304 | tf_op jit(solution)/shard_map/ppermute | solution.py:1100
  42.4 15.6 %collective-permute-start.6 = (bf16[2,4,96,512]{3,2,1,0:T(8,128)(2,1)S(1)}, bf16[2,4,96,512]{3,2,1,0:T(8,128)(2,1)S(1)}, u32[]{:S(2)}, u32[]{:S(2)}) collective-permute-start(bf16[2,4,96,512]{3,2,1,0:T(8,128)(2,1)S(1)} %pad_maximum_fusion.6.refs_4_), channel_id=1, source_target_pairs={{0,1},{1,0},{2,3},{3,2},{4,5},{5,4},{6,7},{7,6},{8,9},{9,8},{10,11... | collective-permute-start | bytes 2359304 | tf_op jit(solution)/shard_map/ppermute | solution.py:1100
  42.4 15.6 %collective-permute-start.2 = (bf16[2,4,96,512]{3,2,1,0:T(8,128)(2,1)S(1)}, bf16[2,4,96,512]{3,2,1,0:T(8,128)(2,1)S(1)}, u32[]{:S(2)}, u32[]{:S(2)}) collective-permute-start(bf16[2,4,96,512]{3,2,1,0:T(8,128)(2,1)S(1)} %pad_maximum_fusion.5.refs_0_), channel_id=1, source_target_pairs={{0,1},{1,0},{2,3},{3,2},{4,5},{5,4},{6,7},{7,6},{8,9},{9,8},{10,11... | collective-permute-start | bytes 2359304 | tf_op jit(solution)/shard_map/ppermute | solution.py:1100
  68.5 51.8 %all-to-all-start.1 = ((bf16[4,2,128,512]{3,2,1,0:T(8,128)(2,1)}), bf16[4,2,128,512]{3,2,1,0:T(8,128)(2,1)S(1)}, u32[]{:S(2)}, u32[]{:S(2)}) async-start(bf16[4,2,128,512]{3,2,1,0:T(8,128)(2,1)} %get-tuple-element.56), calls=%async_computation.1 | async-start | bytes 2097152 | tf_op jit(solution)/shard_map/all_to_all | solution.py:1108
  72.3 23.7 %collective-permute-start.16 = (bf16[2,128,512]{2,1,0:T(8,128)(2,1)S(1)}, bf16[2,128,512]{2,1,0:T(8,128)(2,1)S(1)}, u32[]{:S(2)}, u32[]{:S(2)}) collective-permute-start(bf16[2,128,512]{2,1,0:T(8,128)(2,1)S(1)} %pad_maximum_fusion.11), channel_id=1, source_target_pairs={{0,8},{8,0},{16,24},{24,16},{1,9},{9,1},{17,25},{25,17},{2,10},{10... | collective-permute-start | bytes 786440 | tf_op jit(solution)/shard_map/ppermute | solution.py:1104
  74.4 41.8 %collective-permute-start.17 = (bf16[2,128,512]{2,1,0:T(8,128)(2,1)S(1)}, bf16[2,128,512]{2,1,0:T(8,128)(2,1)S(1)}, u32[]{:S(2)}, u32[]{:S(2)}) collective-permute-start(bf16[2,128,512]{2,1,0:T(8,128)(2,1)S(1)} %pad_maximum_fusion.11), channel_id=1, source_target_pairs={{0,16},{8,24},{16,0},{24,8},{1,17},{9,25},{17,1},{25,9},{2,18},{10... | collective-permute-start | bytes 786440 | tf_op jit(solution)/shard_map/ppermute | solution.py:1104
  76.8 39.5 %collective-permute-start.18 = (bf16[2,128,512]{2,1,0:T(8,128)(2,1)S(1)}, bf16[2,128,512]{2,1,0:T(8,128)(2,1)S(1)}, u32[]{:S(2)}, u32[]{:S(2)}) collective-permute-start(bf16[2,128,512]{2,1,0:T(8,128)(2,1)S(1)} %pad_maximum_fusion.11), channel_id=1, source_target_pairs={{0,24},{8,16},{16,8},{24,0},{1,25},{9,17},{17,9},{25,1},{2,26},{10... | collective-permute-start | bytes 786440 | tf_op jit(solution)/shard_map/ppermute | solution.py:1104
  116.5 14.9 %collective-permute-start.23 = (bf16[4,128,512]{2,1,0:T(8,128)(2,1)S(1)}, bf16[4,128,512]{2,1,0:T(8,128)(2,1)S(1)}, u32[]{:S(2)}, u32[]{:S(2)}) collective-permute-start(bf16[4,128,512]{2,1,0:T(8,128)(2,1)S(1)} %get-tuple-element.157), channel_id=1, source_target_pairs={{0,4},{1,5},{2,6},{3,7},{4,0},{5,1},{6,2},{7,3},{8,12},{9,13},{10,... | collective-permute-start | bytes 1572872 | tf_op jit(solution)/shard_map/ppermute | solution.py:1100
  119.0 15.7 %collective-permute-start.19 = (bf16[4,128,512]{2,1,0:T(8,128)(2,1)}, bf16[4,128,512]{2,1,0:T(8,128)(2,1)}, u32[]{:S(2)}, u32[]{:S(2)}) collective-permute-start(bf16[4,128,512]{2,1,0:T(8,128)(2,1)} %get-tuple-element.159), channel_id=1, source_target_pairs={{0,2},{1,3},{2,0},{3,1},{4,6},{5,7},{6,4},{7,5},{8,10},{9,11},{10,... | collective-permute-start | bytes 1572872 | tf_op jit(solution)/shard_map/ppermute | solution.py:1100
  121.7 23.6 %collective-permute-start.12 = (bf16[4,128,512]{2,1,0:T(8,128)(2,1)}, bf16[4,128,512]{2,1,0:T(8,128)(2,1)}, u32[]{:S(2)}, u32[]{:S(2)}) collective-permute-start(bf16[4,128,512]{2,1,0:T(8,128)(2,1)} %get-tuple-element.140), channel_id=1, source_target_pairs={{0,4},{1,5},{2,6},{3,7},{4,0},{5,1},{6,2},{7,3},{8,12},{9,13},{10,... | collective-permute-start | bytes 1572872 | tf_op jit(solution)/shard_map/ppermute | solution.py:1100
  122.4 25.5 %collective-permute-start.8 = (bf16[4,128,512]{2,1,0:T(8,128)(2,1)}, bf16[4,128,512]{2,1,0:T(8,128)(2,1)}, u32[]{:S(2)}, u32[]{:S(2)}) collective-permute-start(bf16[4,128,512]{2,1,0:T(8,128)(2,1)} %get-tuple-element.139), channel_id=1, source_target_pairs={{0,2},{1,3},{2,0},{3,1},{4,6},{5,7},{6,4},{7,5},{8,10},{9,11},{10,... | collective-permute-start | bytes 1572872 | tf_op jit(solution)/shard_map/ppermute | solution.py:1100
  133.3 67.2 %collective-permute-start.24 = (bf16[2,4,128,512]{3,2,1,0:T(8,128)(2,1)S(1)}, bf16[2,4,128,512]{3,2,1,0:T(8,128)(2,1)}, u32[]{:S(2)}, u32[]{:S(2)}) collective-permute-start(bf16[2,4,128,512]{3,2,1,0:T(8,128)(2,1)S(1)} %pad_maximum_fusion.3), channel_id=1, source_target_pairs={{0,2},{1,3},{2,0},{3,1},{4,6},{5,7},{6,4},{7,5},{8,10},{9,11},{10,... | collective-permute-start | bytes 3145736 | tf_op jit(solution)/shard_map/ppermute | solution.py:1100
  136.0 66.2 %collective-permute-start.20 = (bf16[2,4,128,512]{3,2,1,0:T(8,128)(2,1)S(1)}, bf16[2,4,128,512]{3,2,1,0:T(8,128)(2,1)}, u32[]{:S(2)}, u32[]{:S(2)}) collective-permute-start(bf16[2,4,128,512]{3,2,1,0:T(8,128)(2,1)S(1)} %pad_maximum_fusion.2), channel_id=1, source_target_pairs={{0,4},{1,5},{2,6},{3,7},{4,0},{5,1},{6,2},{7,3},{8,12},{9,13},{10,... | collective-permute-start | bytes 3145736 | tf_op jit(solution)/shard_map/ppermute | solution.py:1100
  140.0 33.4 %collective-permute-start.27 = (bf16[384,1024]{1,0:T(8,128)(2,1)}, bf16[384,1024]{1,0:T(8,128)(2,1)S(1)}, u32[]{:S(2)}, u32[]{:S(2)}) collective-permute-start(bf16[384,1024]{1,0:T(8,128)(2,1)} %get-tuple-element.57), channel_id=1, source_target_pairs={{0,8},{8,0},{16,24},{24,16},{1,9},{9,1},{17,25},{25,17},{2,10},{10... | collective-permute-start | bytes 2359304 | tf_op jit(solution)/shard_map/ppermute | solution.py:1104
  145.3 55.2 %collective-permute-start.28 = (bf16[384,1024]{1,0:T(8,128)(2,1)}, bf16[384,1024]{1,0:T(8,128)(2,1)S(1)}, u32[]{:S(2)}, u32[]{:S(2)}) collective-permute-start(bf16[384,1024]{1,0:T(8,128)(2,1)} %get-tuple-element.58), channel_id=1, source_target_pairs={{0,16},{8,24},{16,0},{24,8},{1,17},{9,25},{17,1},{25,9},{2,18},{10... | collective-permute-start | bytes 2359304 | tf_op jit(solution)/shard_map/ppermute | solution.py:1104
  147.9 53.2 %collective-permute-start.29 = (bf16[384,1024]{1,0:T(8,128)(2,1)}, bf16[384,1024]{1,0:T(8,128)(2,1)S(1)}, u32[]{:S(2)}, u32[]{:S(2)}) collective-permute-start(bf16[384,1024]{1,0:T(8,128)(2,1)} %get-tuple-element.59), channel_id=1, source_target_pairs={{0,24},{8,16},{16,8},{24,0},{1,25},{9,17},{17,9},{25,1},{2,26},{10... | collective-permute-start | bytes 2359304 | tf_op jit(solution)/shard_map/ppermute | solution.py:1104
  173.4 30.0 %collective-permute-start.25 = (bf16[2,4,128,512]{3,2,1,0:T(8,128)(2,1)S(1)}, bf16[2,4,128,512]{3,2,1,0:T(8,128)(2,1)S(1)}, u32[]{:S(2)}, u32[]{:S(2)}) collective-permute-start(bf16[2,4,128,512]{3,2,1,0:T(8,128)(2,1)S(1)} %pad_maximum_fusion.3), channel_id=1, source_target_pairs={{0,1},{1,0},{2,3},{3,2},{4,5},{5,4},{6,7},{7,6},{8,9},{9,8},{10,11... | collective-permute-start | bytes 3145736 | tf_op jit(solution)/shard_map/ppermute | solution.py:1100
  201.0 25.5 %collective-permute-start.13 = (bf16[2,4,128,512]{3,2,1,0:T(8,128)(2,1)}, bf16[2,4,128,512]{3,2,1,0:T(8,128)(2,1)}, u32[]{:S(2)}, u32[]{:S(2)}) collective-permute-start(bf16[2,4,128,512]{3,2,1,0:T(8,128)(2,1)} %pad_maximum_fusion.1), channel_id=1, source_target_pairs={{0,2},{1,3},{2,0},{3,1},{4,6},{5,7},{6,4},{7,5},{8,10},{9,11},{10,... | collective-permute-start | bytes 3145736 | tf_op jit(solution)/shard_map/ppermute | solution.py:1100
  202.2 25.2 %collective-permute-start.9 = (bf16[2,4,128,512]{3,2,1,0:T(8,128)(2,1)}, bf16[2,4,128,512]{3,2,1,0:T(8,128)(2,1)}, u32[]{:S(2)}, u32[]{:S(2)}) collective-permute-start(bf16[2,4,128,512]{3,2,1,0:T(8,128)(2,1)} %pad_maximum_fusion), channel_id=1, source_target_pairs={{0,4},{1,5},{2,6},{3,7},{4,0},{5,1},{6,2},{7,3},{8,12},{9,13},{10,... | collective-permute-start | bytes 3145736 | tf_op jit(solution)/shard_map/ppermute | solution.py:1100
  203.4 44.2 %collective-permute-start.22 = (bf16[2,4,128,512]{3,2,1,0:T(8,128)(2,1)}, bf16[2,4,128,512]{3,2,1,0:T(8,128)(2,1)S(1)}, u32[]{:S(2)}, u32[]{:S(2)}) collective-permute-start(bf16[2,4,128,512]{3,2,1,0:T(8,128)(2,1)} %collective-permute-done.20), channel_id=1, source_target_pairs={{0,1},{1,0},{2,3},{3,2},{4,5},{5,4},{6,7},{7,6},{8,9},{9,8},{10,11... | collective-permute-start | bytes 3145736 | tf_op jit(solution)/shard_map/ppermute | solution.py:1100
  204.4 43.2 %collective-permute-start.14 = (bf16[2,4,128,512]{3,2,1,0:T(8,128)(2,1)}, bf16[2,4,128,512]{3,2,1,0:T(8,128)(2,1)S(1)}, u32[]{:S(2)}, u32[]{:S(2)}) collective-permute-start(bf16[2,4,128,512]{3,2,1,0:T(8,128)(2,1)} %pad_maximum_fusion.1), channel_id=1, source_target_pairs={{0,1},{1,0},{2,3},{3,2},{4,5},{5,4},{6,7},{7,6},{8,9},{9,8},{10,11... | collective-permute-start | bytes 3145736 | tf_op jit(solution)/shard_map/ppermute | solution.py:1100
  206.4 41.2 %collective-permute-start.10 = (bf16[2,4,128,512]{3,2,1,0:T(8,128)(2,1)}, bf16[2,4,128,512]{3,2,1,0:T(8,128)(2,1)}, u32[]{:S(2)}, u32[]{:S(2)}) collective-permute-start(bf16[2,4,128,512]{3,2,1,0:T(8,128)(2,1)} %pad_maximum_fusion), channel_id=1, source_target_pairs={{0,1},{1,0},{2,3},{3,2},{4,5},{5,4},{6,7},{7,6},{8,9},{9,8},{10,11... | collective-permute-start | bytes 3145736 | tf_op jit(solution)/shard_map/ppermute | solution.py:1100
  226.5 21.1 %collective-permute-start.15 = (bf16[2,4,128,512]{3,2,1,0:T(8,128)(2,1)}, bf16[2,4,128,512]{3,2,1,0:T(8,128)(2,1)}, u32[]{:S(2)}, u32[]{:S(2)}) collective-permute-start(bf16[2,4,128,512]{3,2,1,0:T(8,128)(2,1)} %collective-permute-done.13), channel_id=1, source_target_pairs={{0,1},{1,0},{2,3},{3,2},{4,5},{5,4},{6,7},{7,6},{8,9},{9,8},{10,11... | collective-permute-start | bytes 3145736 | tf_op jit(solution)/shard_map/ppermute | solution.py:1100
  227.4 20.3 %collective-permute-start.11 = (bf16[2,4,128,512]{3,2,1,0:T(8,128)(2,1)}, bf16[2,4,128,512]{3,2,1,0:T(8,128)(2,1)}, u32[]{:S(2)}, u32[]{:S(2)}) collective-permute-start(bf16[2,4,128,512]{3,2,1,0:T(8,128)(2,1)} %collective-permute-done.9), channel_id=1, source_target_pairs={{0,1},{1,0},{2,3},{3,2},{4,5},{5,4},{6,7},{7,6},{8,9},{9,8},{10,11... | collective-permute-start | bytes 3145736 | tf_op jit(solution)/shard_map/ppermute | solution.py:1100
  281.6 5.9 %collective-permute-start.41 = (bf16[2,4,128,512]{3,2,1,0:T(8,128)(2,1)}, bf16[2,4,128,512]{3,2,1,0:T(8,128)(2,1)S(1)}, u32[]{:S(2)}, u32[]{:S(2)}) collective-permute-start(bf16[2,4,128,512]{3,2,1,0:T(8,128)(2,1)} %bitcast.277), channel_id=1, source_target_pairs={{0,1},{1,0},{2,3},{3,2},{4,5},{5,4},{6,7},{7,6},{8,9},{9,8},{10,11... | collective-permute-start | bytes 3145736 | tf_op jit(solution)/shard_map/ppermute | solution.py:1100
  285.5 25.3 %collective-permute-start.43 = (bf16[2,4,128,512]{3,2,1,0:T(8,128)(2,1)S(1)}, bf16[2,4,128,512]{3,2,1,0:T(8,128)(2,1)S(1)}, u32[]{:S(2)}, u32[]{:S(2)}) collective-permute-start(bf16[2,4,128,512]{3,2,1,0:T(8,128)(2,1)S(1)} %fusion.2), channel_id=1, source_target_pairs={{0,4},{1,5},{2,6},{3,7},{4,0},{5,1},{6,2},{7,3},{8,12},{9,13},{10,... | collective-permute-start | bytes 3145736 | tf_op jit(solution)/shard_map/ppermute | solution.py:1100
  286.4 26.5 %collective-permute-start.45 = (bf16[2,4,128,512]{3,2,1,0:T(8,128)(2,1)S(1)}, bf16[2,4,128,512]{3,2,1,0:T(8,128)(2,1)S(1)}, u32[]{:S(2)}, u32[]{:S(2)}) collective-permute-start(bf16[2,4,128,512]{3,2,1,0:T(8,128)(2,1)S(1)} %bitcast.276), channel_id=1, source_target_pairs={{0,1},{1,0},{2,3},{3,2},{4,5},{5,4},{6,7},{7,6},{8,9},{9,8},{10,11... | collective-permute-start | bytes 3145736 | tf_op jit(solution)/shard_map/ppermute | solution.py:1100
  286.7 26.2 %collective-permute-start.47 = (bf16[2,4,128,512]{3,2,1,0:T(8,128)(2,1)S(1)}, bf16[2,4,128,512]{3,2,1,0:T(8,128)(2,1)S(1)}, u32[]{:S(2)}, u32[]{:S(2)}) collective-permute-start(bf16[2,4,128,512]{3,2,1,0:T(8,128)(2,1)S(1)} %fusion), channel_id=1, source_target_pairs={{0,2},{1,3},{2,0},{3,1},{4,6},{5,7},{6,4},{7,5},{8,10},{9,11},{10,... | collective-permute-start | bytes 3145736 | tf_op jit(solution)/shard_map/ppermute | solution.py:1100
  287.3 48.5 %collective-permute-start.31 = (bf16[2,4,128,512]{3,2,1,0:T(8,128)(2,1)}, bf16[2,4,128,512]{3,2,1,0:T(8,128)(2,1)}, u32[]{:S(2)}, u32[]{:S(2)}) collective-permute-start(bf16[2,4,128,512]{3,2,1,0:T(8,128)(2,1)} %bitcast.60), channel_id=1, source_target_pairs={{0,1},{1,0},{2,3},{3,2},{4,5},{5,4},{6,7},{7,6},{8,9},{9,8},{10,11... | collective-permute-start | bytes 3145736 | tf_op jit(solution)/shard_map/ppermute | solution.py:1100
  312.1 13.5 %collective-permute-start.44 = (bf16[4,128,512]{2,1,0:T(8,128)(2,1)}, bf16[4,128,512]{2,1,0:T(8,128)(2,1)}, u32[]{:S(2)}, u32[]{:S(2)}) collective-permute-start(bf16[4,128,512]{2,1,0:T(8,128)(2,1)} %slice_bitcast_fusion.2), channel_id=1, source_target_pairs={{0,2},{1,3},{2,0},{3,1},{4,6},{5,7},{6,4},{7,5},{8,10},{9,11},{10,... | collective-permute-start | bytes 1572872 | tf_op jit(solution)/shard_map/ppermute | solution.py:1100
  316.2 13.4 %collective-permute-start.48 = (bf16[4,128,512]{2,1,0:T(8,128)(2,1)}, bf16[4,128,512]{2,1,0:T(8,128)(2,1)}, u32[]{:S(2)}, u32[]{:S(2)}) collective-permute-start(bf16[4,128,512]{2,1,0:T(8,128)(2,1)} %slice_bitcast_fusion), channel_id=1, source_target_pairs={{0,4},{1,5},{2,6},{3,7},{4,0},{5,1},{6,2},{7,3},{8,12},{9,13},{10,... | collective-permute-start | bytes 1572872 | tf_op jit(solution)/shard_map/ppermute | solution.py:1100
  316.9 22.7 %collective-permute-start.35 = (bf16[2,4,128,512]{3,2,1,0:T(8,128)(2,1)}, bf16[2,4,128,512]{3,2,1,0:T(8,128)(2,1)}, u32[]{:S(2)}, u32[]{:S(2)}) collective-permute-start(bf16[2,4,128,512]{3,2,1,0:T(8,128)(2,1)} %bitcast.66), channel_id=1, source_target_pairs={{0,1},{1,0},{2,3},{3,2},{4,5},{5,4},{6,7},{7,6},{8,9},{9,8},{10,11... | collective-permute-start | bytes 3145736 | tf_op jit(solution)/shard_map/ppermute | solution.py:1100
  316.9 15.2 %all-to-all-start.4 = ((f32[32,1,128]{2,1,0:T(1,128)}), f32[32,1,128]{2,1,0:T(1,128)S(1)}, u32[]{:S(2)}, u32[]{:S(2)}) async-start(f32[32,1,128]{2,1,0:T(1,128)} %get-tuple-element.78), calls=%async_computation.4 | async-start | bytes 32768 | tf_op jit(solution)/shard_map/all_to_all | solution.py:1108
  320.0 24.5 %collective-permute-start.30 = (bf16[2,4,128,512]{3,2,1,0:T(8,128)(2,1)}, bf16[2,4,128,512]{3,2,1,0:T(8,128)(2,1)}, u32[]{:S(2)}, u32[]{:S(2)}) collective-permute-start(bf16[2,4,128,512]{3,2,1,0:T(8,128)(2,1)} %bitcast.275), channel_id=1, source_target_pairs={{0,1},{1,0},{2,3},{3,2},{4,5},{5,4},{6,7},{7,6},{8,9},{9,8},{10,11... | collective-permute-start | bytes 3145736 | tf_op jit(solution)/shard_map/ppermute | solution.py:1100
  332.1 32.9 %all-to-all-start.3 = ((bf16[4,2,128,512]{3,2,1,0:T(8,128)(2,1)}), bf16[4,2,128,512]{3,2,1,0:T(8,128)(2,1)S(1)}, u32[]{:S(2)}, u32[]{:S(2)}) async-start(bf16[4,2,128,512]{3,2,1,0:T(8,128)(2,1)} %pad_maximum_fusion.4), calls=%async_computation.3 | async-start | bytes 2097152 | tf_op jit(solution)/shard_map/all_to_all | solution.py:1108
  338.3 23.6 %collective-permute-start.32 = (bf16[2,4,128,512]{3,2,1,0:T(8,128)(2,1)}, bf16[2,4,128,512]{3,2,1,0:T(8,128)(2,1)}, u32[]{:S(2)}, u32[]{:S(2)}) collective-permute-start(bf16[2,4,128,512]{3,2,1,0:T(8,128)(2,1)} %fusion.6), channel_id=1, source_target_pairs={{0,4},{1,5},{2,6},{3,7},{4,0},{5,1},{6,2},{7,3},{8,12},{9,13},{10,... | collective-permute-start | bytes 3145736 | tf_op jit(solution)/shard_map/ppermute | solution.py:1100
  339.5 38.0 %collective-permute-start.34 = (bf16[2,4,128,512]{3,2,1,0:T(8,128)(2,1)}, bf16[2,4,128,512]{3,2,1,0:T(8,128)(2,1)}, u32[]{:S(2)}, u32[]{:S(2)}) collective-permute-start(bf16[2,4,128,512]{3,2,1,0:T(8,128)(2,1)} %bitcast.64), channel_id=1, source_target_pairs={{0,1},{1,0},{2,3},{3,2},{4,5},{5,4},{6,7},{7,6},{8,9},{9,8},{10,11... | collective-permute-start | bytes 3145736 | tf_op jit(solution)/shard_map/ppermute | solution.py:1100
  342.0 35.5 %collective-permute-start.36 = (bf16[2,4,128,512]{3,2,1,0:T(8,128)(2,1)}, bf16[2,4,128,512]{3,2,1,0:T(8,128)(2,1)}, u32[]{:S(2)}, u32[]{:S(2)}) collective-permute-start(bf16[2,4,128,512]{3,2,1,0:T(8,128)(2,1)} %fusion.4), channel_id=1, source_target_pairs={{0,2},{1,3},{2,0},{3,1},{4,6},{5,7},{6,4},{7,5},{8,10},{9,11},{10,... | collective-permute-start | bytes 3145736 | tf_op jit(solution)/shard_map/ppermute | solution.py:1100
  342.8 108.7 %collective-permute-start.65 = (bf16[384,1024]{1,0:T(8,128)(2,1)}, bf16[384,1024]{1,0:T(8,128)(2,1)}, u32[]{:S(2)}, u32[]{:S(2)}) collective-permute-start(bf16[384,1024]{1,0:T(8,128)(2,1)} %get-tuple-element.95), channel_id=1, source_target_pairs={{0,8},{8,0},{16,24},{24,16},{1,9},{9,1},{17,25},{25,17},{2,10},{10... | collective-permute-start | bytes 2359304 | tf_op jit(solution)/shard_map/ppermute | solution.py:1104
  377.0 5.4 %collective-permute-start.50 = (bf16[2,4,96,512]{3,2,1,0:T(8,128)(2,1)}, bf16[2,4,96,512]{3,2,1,0:T(8,128)(2,1)}, u32[]{:S(2)}, u32[]{:S(2)}) collective-permute-start(bf16[2,4,96,512]{3,2,1,0:T(8,128)(2,1)} %get-tuple-element.85), channel_id=1, source_target_pairs={{0,1},{1,0},{2,3},{3,2},{4,5},{5,4},{6,7},{7,6},{8,9},{9,8},{10,11... | collective-permute-start | bytes 2359304 | tf_op jit(solution)/shard_map/ppermute | solution.py:1100
  377.1 9.6 %collective-permute-start.54 = (bf16[2,4,96,512]{3,2,1,0:T(8,128)(2,1)}, bf16[2,4,96,512]{3,2,1,0:T(8,128)(2,1)}, u32[]{:S(2)}, u32[]{:S(2)}) collective-permute-start(bf16[2,4,96,512]{3,2,1,0:T(8,128)(2,1)} %get-tuple-element.89), channel_id=1, source_target_pairs={{0,1},{1,0},{2,3},{3,2},{4,5},{5,4},{6,7},{7,6},{8,9},{9,8},{10,11... | collective-permute-start | bytes 2359304 | tf_op jit(solution)/shard_map/ppermute | solution.py:1100
  381.4 14.1 %collective-permute-start.49 = (bf16[2,4,96,512]{3,2,1,0:T(8,128)(2,1)}, bf16[2,4,96,512]{3,2,1,0:T(8,128)(2,1)}, u32[]{:S(2)}, u32[]{:S(2)}) collective-permute-start(bf16[2,4,96,512]{3,2,1,0:T(8,128)(2,1)} %get-tuple-element.83), channel_id=1, source_target_pairs={{0,1},{1,0},{2,3},{3,2},{4,5},{5,4},{6,7},{7,6},{8,9},{9,8},{10,11... | collective-permute-start | bytes 2359304 | tf_op jit(solution)/shard_map/ppermute | solution.py:1100
  381.4 31.5 %collective-permute-start.53 = (bf16[2,4,96,512]{3,2,1,0:T(8,128)(2,1)}, bf16[2,4,96,512]{3,2,1,0:T(8,128)(2,1)}, u32[]{:S(2)}, u32[]{:S(2)}) collective-permute-start(bf16[2,4,96,512]{3,2,1,0:T(8,128)(2,1)} %get-tuple-element.87), channel_id=1, source_target_pairs={{0,1},{1,0},{2,3},{3,2},{4,5},{5,4},{6,7},{7,6},{8,9},{9,8},{10,11... | collective-permute-start | bytes 2359304 | tf_op jit(solution)/shard_map/ppermute | solution.py:1100
  384.9 22.9 %collective-permute-start.51 = (bf16[2,4,96,512]{3,2,1,0:T(8,128)(2,1)}, bf16[2,4,96,512]{3,2,1,0:T(8,128)(2,1)}, u32[]{:S(2)}, u32[]{:S(2)}) collective-permute-start(bf16[2,4,96,512]{3,2,1,0:T(8,128)(2,1)} %add_convert_fusion.8), channel_id=1, source_target_pairs={{0,4},{1,5},{2,6},{3,7},{4,0},{5,1},{6,2},{7,3},{8,12},{9,13},{10,... | collective-permute-start | bytes 2359304 | tf_op jit(solution)/shard_map/ppermute | solution.py:1100
  388.9 25.3 %collective-permute-start.55 = (bf16[2,4,96,512]{3,2,1,0:T(8,128)(2,1)}, bf16[2,4,96,512]{3,2,1,0:T(8,128)(2,1)}, u32[]{:S(2)}, u32[]{:S(2)}) collective-permute-start(bf16[2,4,96,512]{3,2,1,0:T(8,128)(2,1)} %add_convert_fusion.5), channel_id=1, source_target_pairs={{0,2},{1,3},{2,0},{3,1},{4,6},{5,7},{6,4},{7,5},{8,10},{9,11},{10,... | collective-permute-start | bytes 2359304 | tf_op jit(solution)/shard_map/ppermute | solution.py:1100
  390.1 52.0 %all-to-all-start.5 = ((f32[32,1,3072]{2,1,0:T(1,128)}), f32[32,1,3072]{2,1,0:T(1,128)}, u32[]{:S(2)}, u32[]{:S(2)}) async-start(f32[32,1,3072]{2,1,0:T(1,128)} %all_to_all.29), calls=%async_computation.5 | async-start | bytes 786432 | tf_op jit(solution)/shard_map/all_to_all | solution.py:1108
  395.5 71.5 %collective-permute-start.66 = (bf16[384,1024]{1,0:T(8,128)(2,1)}, bf16[384,1024]{1,0:T(8,128)(2,1)}, u32[]{:S(2)}, u32[]{:S(2)}) collective-permute-start(bf16[384,1024]{1,0:T(8,128)(2,1)} %get-tuple-element.96), channel_id=1, source_target_pairs={{0,16},{8,24},{16,0},{24,8},{1,17},{9,25},{17,1},{25,9},{2,18},{10... | collective-permute-start | bytes 2359304 | tf_op jit(solution)/shard_map/ppermute | solution.py:1104
  407.8 59.2 %collective-permute-start.67 = (bf16[384,1024]{1,0:T(8,128)(2,1)}, bf16[384,1024]{1,0:T(8,128)(2,1)}, u32[]{:S(2)}, u32[]{:S(2)}) collective-permute-start(bf16[384,1024]{1,0:T(8,128)(2,1)} %get-tuple-element.97), channel_id=1, source_target_pairs={{0,24},{8,16},{16,8},{24,0},{1,25},{9,17},{17,9},{25,1},{2,26},{10... | collective-permute-start | bytes 2359304 | tf_op jit(solution)/shard_map/ppermute | solution.py:1104
  413.0 14.9 %collective-permute-start.33 = (bf16[4,128,512]{2,1,0:T(8,128)(2,1)S(1)}, bf16[4,128,512]{2,1,0:T(8,128)(2,1)S(1)}, u32[]{:S(2)}, u32[]{:S(2)}) collective-permute-start(bf16[4,128,512]{2,1,0:T(8,128)(2,1)S(1)} %copy-done.47), channel_id=1, source_target_pairs={{0,2},{1,3},{2,0},{3,1},{4,6},{5,7},{6,4},{7,5},{8,10},{9,11},{10,... | collective-permute-start | bytes 1572872 | tf_op jit(solution)/shard_map/ppermute | solution.py:1100
  414.1 19.8 %collective-permute-start.52 = (bf16[4,96,512]{2,1,0:T(8,128)(2,1)S(1)}, bf16[4,96,512]{2,1,0:T(8,128)(2,1)S(1)}, u32[]{:S(2)}, u32[]{:S(2)}) collective-permute-start(bf16[4,96,512]{2,1,0:T(8,128)(2,1)S(1)} %slice_bitcast_fusion.14), channel_id=1, source_target_pairs={{0,2},{1,3},{2,0},{3,1},{4,6},{5,7},{6,4},{7,5},{8,10},{9,11},{10,... | collective-permute-start | bytes 1179656 | tf_op jit(solution)/shard_map/ppermute | solution.py:1100
  427.8 8.7 %collective-permute-start.56 = (bf16[4,96,512]{2,1,0:T(8,128)(2,1)S(1)}, bf16[4,96,512]{2,1,0:T(8,128)(2,1)S(1)}, u32[]{:S(2)}, u32[]{:S(2)}) collective-permute-start(bf16[4,96,512]{2,1,0:T(8,128)(2,1)S(1)} %slice_bitcast_fusion.12), channel_id=1, source_target_pairs={{0,4},{1,5},{2,6},{3,7},{4,0},{5,1},{6,2},{7,3},{8,12},{9,13},{10,... | collective-permute-start | bytes 1179656 | tf_op jit(solution)/shard_map/ppermute | solution.py:1100
  434.0 13.2 %collective-permute-start.37 = (bf16[4,128,512]{2,1,0:T(8,128)(2,1)}, bf16[4,128,512]{2,1,0:T(8,128)(2,1)}, u32[]{:S(2)}, u32[]{:S(2)}) collective-permute-start(bf16[4,128,512]{2,1,0:T(8,128)(2,1)} %slice_bitcast_fusion.4), channel_id=1, source_target_pairs={{0,4},{1,5},{2,6},{3,7},{4,0},{5,1},{6,2},{7,3},{8,12},{9,13},{10,... | collective-permute-start | bytes 1572872 | tf_op jit(solution)/shard_map/ppermute | solution.py:1100
  442.1 68.3 %all-to-all-start.6 = ((bf16[4,2,96,512]{3,2,1,0:T(8,128)(2,1)}), bf16[4,2,96,512]{3,2,1,0:T(8,128)(2,1)S(1)}, u32[]{:S(2)}, u32[]{:S(2)}) async-start(bf16[4,2,96,512]{3,2,1,0:T(8,128)(2,1)} %copy.34), calls=%async_computation.6 | async-start | bytes 1572864 | tf_op jit(solution)/shard_map/all_to_all | solution.py:1108
  448.5 23.4 %collective-permute-start.38 = (bf16[2,128,512]{2,1,0:T(8,128)(2,1)S(1)}, bf16[2,128,512]{2,1,0:T(8,128)(2,1)S(1)}, u32[]{:S(2)}, u32[]{:S(2)}) collective-permute-start(bf16[2,128,512]{2,1,0:T(8,128)(2,1)S(1)} %pad_maximum_fusion.12), channel_id=1, source_target_pairs={{0,8},{8,0},{16,24},{24,16},{1,9},{9,1},{17,25},{25,17},{2,10},{10... | collective-permute-start | bytes 786440 | tf_op jit(solution)/shard_map/ppermute | solution.py:1104
  449.0 60.0 %collective-permute-start.39 = (bf16[2,128,512]{2,1,0:T(8,128)(2,1)S(1)}, bf16[2,128,512]{2,1,0:T(8,128)(2,1)S(1)}, u32[]{:S(2)}, u32[]{:S(2)}) collective-permute-start(bf16[2,128,512]{2,1,0:T(8,128)(2,1)S(1)} %pad_maximum_fusion.13), channel_id=1, source_target_pairs={{0,16},{8,24},{16,0},{24,8},{1,17},{9,25},{17,1},{25,9},{2,18},{10... | collective-permute-start | bytes 786440 | tf_op jit(solution)/shard_map/ppermute | solution.py:1104
  451.5 57.5 %collective-permute-start.40 = (bf16[2,128,512]{2,1,0:T(8,128)(2,1)S(1)}, bf16[2,128,512]{2,1,0:T(8,128)(2,1)S(1)}, u32[]{:S(2)}, u32[]{:S(2)}) collective-permute-start(bf16[2,128,512]{2,1,0:T(8,128)(2,1)S(1)} %pad_maximum_fusion.14), channel_id=1, source_target_pairs={{0,24},{8,16},{16,8},{24,0},{1,25},{9,17},{17,9},{25,1},{2,26},{10... | collective-permute-start | bytes 786440 | tf_op jit(solution)/shard_map/ppermute | solution.py:1104
  512.2 5.8 %collective-permute-start.57 = (bf16[97,512]{1,0:T(8,128)(2,1)S(1)}, bf16[97,512]{1,0:T(8,128)(2,1)S(1)}, u32[]{:S(2)}, u32[]{:S(2)}) collective-permute-start(bf16[97,512]{1,0:T(8,128)(2,1)S(1)} %bitcast.266), channel_id=1, source_target_pairs={{0,2},{1,3},{2,0},{3,1},{4,6},{5,7},{6,4},{7,5},{8,10},{9,11},{10,... | collective-permute-start | bytes 297992 | tf_op jit(solution)/shard_map/ppermute | solution.py:1100
  515.4 6.1 %collective-permute-start.62 = (bf16[2,97,512]{2,1,0:T(8,128)(2,1)S(1)}, bf16[2,97,512]{2,1,0:T(8,128)(2,1)S(1)}, u32[]{:S(2)}, u32[]{:S(2)}) collective-permute-start(bf16[2,97,512]{2,1,0:T(8,128)(2,1)S(1)} %pad_maximum_fusion.16.refs_4_), channel_id=1, source_target_pairs={{0,2},{1,3},{2,0},{3,1},{4,6},{5,7},{6,4},{7,5},{8,10},{9,11},{10,... | collective-permute-start | bytes 595976 | tf_op jit(solution)/shard_map/ppermute | solution.py:1100
  518.0 5.9 %collective-permute-start.58 = (bf16[2,97,512]{2,1,0:T(8,128)(2,1)S(1)}, bf16[2,97,512]{2,1,0:T(8,128)(2,1)S(1)}, u32[]{:S(2)}, u32[]{:S(2)}) collective-permute-start(bf16[2,97,512]{2,1,0:T(8,128)(2,1)S(1)} %pad_maximum_fusion.15.refs_0_), channel_id=1, source_target_pairs={{0,4},{1,5},{2,6},{3,7},{4,0},{5,1},{6,2},{7,3},{8,12},{9,13},{10,... | collective-permute-start | bytes 595976 | tf_op jit(solution)/shard_map/ppermute | solution.py:1100
  519.3 5.3 collective-permute-start.63
  519.3 5.3 collective-permute-start.59
  (68 other events, 825.5 us)
